TPU v7x, 128 devices: a whole 4x4x4 slice. The times are simulated.
128 devices in a mesh: wide: 16 (over z, y), narrow: 8 (over x, core).
Axes of the slice: x: 4, y: 4, z: 4, core: 2. Of those that a mesh axis runs over, the one named last changes fastest.
Arguments:
- velocity: float32 [3, 512, 16384], P(None, None, ('wide', 'narrow')), may hold values from -6 to 6
- element_slot: int32 [128, 128], P(('wide', 'narrow')), may hold values from 0 to 127, as said below
- corner_vertex: int32 [8, 16384], P(None, ('wide', 'narrow')), may hold values from 0 to 17407, as said below
- axial_size: float32 [16], P('wide'), may hold values from 0.5 to 2
- arc_size: float32 [16], replicated, may hold values from 0.5 to 2
- radial_size: float32 [16], replicated, may hold values from 0.3 to 1.5
- fdm_vectors: float32 [10, 10], replicated, may hold values from -2 to 2
- fdm_values: float32 [10], replicated, may hold values from 0.5 to 60
Outputs:
- velocity_out: float32 [3, 512, 16384], P(None, None, ('wide', 'narrow'))
- coarse_residual: float32 [3, 17408], P(None, ('wide', 'narrow'))
Inputs may be any that keep to these rules, and one draw needn't show every extreme that they name: `element_slot`: each device's row is a permutation of the block positions of its 128 elements. `corner_vertex`: the ids of a permutation of the 17408 vertices of the coarse grid (vertex at axial index, around index and radial offset 0 to 16, periodic along and around the pipe); corner a * 4 + b * 2 + c lies at axial offset a, around offset b, radial offset c of its element; elements that share a corner share its id.
All inputs are finite; a program needn't handle non-finite values.
Results may differ from a plain program's by a relative error of at most 0.0001.
Values sent between devices are 32-bit elements; how exact they have to be, the bound alone decides.
No kernel may reach another device: no remote copies, remote signals or barrier semaphores. Data moves between devices by JAX's collectives and lax.ppermute only.
A program may use at most 128 MiB of HBM per device.

v0:
```python
from functools import partial

import jax
import jax.numpy as jnp
import numpy as np
from jax import lax
from jax.sharding import PartitionSpec as P

AXIAL_DEV = 1
AROUND_DEV = 8
RADIAL = 16
STEPS = 2


SIGMA = 4.0
VISCOSITY = 0.05
HIGH_ACCURACY = lax.Precision.HIGHEST


def padded(cells, sides, width):
    for axis, dim in sides:
        count = lax.axis_size(axis)
        head = lax.slice_in_dim(cells, 0, width, axis=dim)
        tail = lax.slice_in_dim(cells, cells.shape[dim] - width, cells.shape[dim], axis=dim)
        cells = jnp.concatenate(
            [
                lax.ppermute(tail, axis, [(i, (i + 1) % count) for i in range(count)]),
                cells,
                lax.ppermute(head, axis, [((i + 1) % count, i) for i in range(count)]),
            ],
            axis=dim,
        )
    return cells


def node_tables():
    gll_nodes = np.array(
        [
            -1.0,
            -0.8717401485096066,
            -0.5917001814331423,
            -0.2092992179024789,
            0.2092992179024789,
            0.5917001814331423,
            0.8717401485096066,
            1.0,
        ]
    )
    gll_weights = np.array(
        [
            1.0 / 28.0,
            0.2107042271435061,
            0.3411226924835044,
            0.4124587946587038,
            0.4124587946587038,
            0.3411226924835044,
            0.2107042271435061,
            1.0 / 28.0,
        ]
    )
    bary_scale = np.array(
        [
            np.prod(
                [
                    gll_nodes[target] - gll_nodes[partner]
                    for partner in range(8)
                    if partner != target
                ]
            )
            for target in range(8)
        ]
    )
    derivative = np.zeros((8, 8))
    for target in range(8):
        for source in range(8):
            if target != source:
                derivative[target, source] = bary_scale[target] / (
                    bary_scale[source] * (gll_nodes[target] - gll_nodes[source])
                )
        derivative[target, target] = -np.sum(derivative[target])
    fine_nodes = np.array(
        [
            -0.9815606342467192,
            -0.9041172563704749,
            -0.7699026741943047,
            -0.5873179542866175,
            -0.3678314989981802,
            -0.1252334085114689,
            0.1252334085114689,
            0.3678314989981802,
            0.5873179542866175,
            0.7699026741943047,
            0.9041172563704749,
            0.9815606342467192,
        ]
    )
    fine_weights = np.array(
        [
            0.0471753363865118,
            0.1069393259953184,
            0.1600783285433462,
            0.2031674267230659,
            0.2334925365383548,
            0.2491470458134028,
            0.2491470458134028,
            0.2334925365383548,
            0.2031674267230659,
            0.1600783285433462,
            0.1069393259953184,
            0.0471753363865118,
        ]
    )
    interp = np.ones((12, 8))
    for source in range(8):
        for partner in range(8):
            if partner != source:
                interp[:, source] = (
                    interp[:, source]
                    * (fine_nodes - gll_nodes[partner])
                    / (gll_nodes[source] - gll_nodes[partner])
                )
    linear = np.stack([(1.0 - gll_nodes) / 2.0, (1.0 + gll_nodes) / 2.0])
    corner_map = (
        linear[:, None, None, :, None, None]
        * linear[None, :, None, None, :, None]
        * linear[None, None, :, None, None, :]
    ).reshape(8, 512)
    mass_gll = gll_weights[:, None, None] * gll_weights[None, :, None] * gll_weights[None, None, :]
    mass_fine = (
        fine_weights[:, None, None] * fine_weights[None, :, None] * fine_weights[None, None, :]
    )
    dealias_interp_matrix = np.kron(interp, np.kron(interp, interp))
    return tuple(
        (
            jnp.asarray(matrix, jnp.float32)
            for matrix in (
                derivative,
                interp,
                corner_map,
                mass_gll,
                mass_fine,
                dealias_interp_matrix,
            )
        )
    )


def apply_first(matrix, tensor):
    return jnp.einsum("ai,cijkb->cajkb", matrix, tensor, precision=HIGH_ACCURACY)


def apply_second(matrix, tensor):
    return jnp.einsum("aj,cijkb->ciakb", matrix, tensor, precision=HIGH_ACCURACY)


def apply_third(matrix, tensor):
    return jnp.einsum("ak,cijkb->cijab", matrix, tensor, precision=HIGH_ACCURACY)


def to_fine(tensor, dealias_interp_matrix):
    channels = tensor.shape[0]
    flattened_values = tensor.reshape(channels, 512, tensor.shape[-1])
    return jnp.einsum(
        "mh,jhr->jmr", dealias_interp_matrix, flattened_values, precision=HIGH_ACCURACY
    )


def element_residual(velocity, lengths, tables):
    derivative = tables[0]
    mass_gll = tables[3]
    mass_fine = tables[4]
    dealias_interp_matrix = tables[5]
    block_width = velocity.shape[-1]
    tensor = velocity.reshape(3, 8, 8, 8, block_width)
    inverse = 2.0 / lengths
    volume = lengths[0] * lengths[1] * lengths[2] / 8.0
    grad_z = apply_first(derivative, tensor) * inverse[0]
    grad_t = apply_second(derivative, tensor) * inverse[1]
    grad_r = apply_third(derivative, tensor) * inverse[2]
    fine_vel = to_fine(tensor, dealias_interp_matrix)
    convective_term = (
        fine_vel[0:1] * to_fine(grad_z, dealias_interp_matrix)
        + fine_vel[1:2] * to_fine(grad_t, dealias_interp_matrix)
        + fine_vel[2:3] * to_fine(grad_r, dealias_interp_matrix)
    )
    convective_term = convective_term * (mass_fine.reshape(1728)[:, None] * volume[None])
    advect_velocity = jnp.einsum(
        "ue,kua->kea", dealias_interp_matrix, convective_term, precision=HIGH_ACCURACY
    )
    weight = mass_gll[:, :, :, None] * volume
    stiff = apply_first(derivative.T, grad_z * weight) * inverse[0]
    stiff = stiff + apply_second(derivative.T, grad_t * weight) * inverse[1]
    stiff = stiff + apply_third(derivative.T, grad_r * weight) * inverse[2]
    return -(advect_velocity + VISCOSITY * stiff.reshape(3, 512, block_width))


def quadratic_form(direction, lengths, tables):
    derivative = tables[0]
    mass_gll = tables[3]
    block_width = direction.shape[-1]
    tensor = direction.reshape(3, 8, 8, 8, block_width)
    inverse = 2.0 / lengths
    volume = lengths[0] * lengths[1] * lengths[2] / 8.0
    weight = mass_gll[:, :, :, None] * volume
    grad_z = apply_first(derivative, tensor) * inverse[0]
    grad_t = apply_second(derivative, tensor) * inverse[1]
    grad_r = apply_third(derivative, tensor) * inverse[2]
    return jnp.sum(
        weight
        * (
            SIGMA * tensor * tensor
            + VISCOSITY * (grad_z * grad_z + grad_t * grad_t + grad_r * grad_r)
        )
    )


def fdm_solve(extended, lengths, vectors, values):
    block_width = extended.shape[-1]
    tensor = extended.reshape(3, 10, 10, 10, block_width)
    spectral = apply_third(vectors.T, apply_second(vectors.T, apply_first(vectors.T, tensor)))
    squared = (2.0 / lengths) ** 2
    volume = lengths[0] * lengths[1] * lengths[2] / 8.0
    scaling = volume * (
        SIGMA
        + VISCOSITY
        * (
            values[:, None, None, None] * squared[0]
            + values[None, :, None, None] * squared[1]
            + values[None, None, :, None] * squared[2]
        )
    )
    spectral = spectral / scaling
    restored = apply_third(vectors, apply_second(vectors, apply_first(vectors, spectral)))
    return restored[:, 1:9, 1:9, 1:9].reshape(3, 512, block_width)


def blockwise(function, arrays, block_width):
    blocks_total = arrays[0].shape[-1] // block_width

    def single(block_index):
        pieces = [
            lax.dynamic_slice_in_dim(
                member, block_index * block_width, block_width, member.ndim - 1
            )
            for member in arrays
        ]
        return function(*pieces)

    stacked = lax.map(single, jnp.arange(blocks_total, dtype=jnp.int32))
    if stacked.ndim == 1:
        return jnp.sum(stacked)
    reordered = jnp.moveaxis(stacked, 0, -2)
    return reordered.reshape(reordered.shape[:-2] + (blocks_total * block_width,))


def node_masks(elem_count):
    node_index = jnp.arange(512)
    node_i = node_index // 64
    node_j = node_index // 8 % 8
    node_k = node_index % 8
    radial_pos = jnp.arange(elem_count) % RADIAL
    on_wall = (node_k == 0)[:, None] & (radial_pos == 0)[None] | (node_k == 7)[:, None] & (
        radial_pos == RADIAL - 1
    )[None]
    wall_keep = jnp.where(on_wall, 0.0, 1.0).astype(jnp.float32)
    face_z = jnp.where((node_i == 0) | (node_i == 7), 2.0, 1.0)[:, None]
    face_t = jnp.where((node_j == 0) | (node_j == 7), 2.0, 1.0)[:, None]
    inner_r = (node_k == 0)[:, None] & (radial_pos > 0)[None] | (node_k == 7)[:, None] & (
        radial_pos < RADIAL - 1
    )[None]
    sharing = (face_z * face_t * jnp.where(inner_r, 2.0, 1.0)).astype(jnp.float32)
    return (wall_keep, sharing)


def take_part(tensor, axis_pos, start, stop):
    return lax.slice_in_dim(tensor, start, stop, axis=axis_pos)


def elem_stride(direction):
    if direction == 0:
        return (AROUND_DEV * RADIAL, AXIAL_DEV)
    if direction == 1:
        return (RADIAL, AROUND_DEV)
    return (1, RADIAL)


def edge_elements(plane, direction, which):
    elem_count = plane.shape[-1]
    lead = plane.shape[:-1]
    if direction == 0:
        cycle_size = AROUND_DEV * RADIAL
        if which == 0:
            return plane[..., :cycle_size]
        return plane[..., elem_count - cycle_size :]
    grouped = plane.reshape(lead + (AXIAL_DEV, AROUND_DEV, RADIAL))
    position = 0 if which == 0 else AROUND_DEV - 1
    picked = take_part(grouped, len(lead) + 1, position, position + 1)
    return picked.reshape(lead + (AXIAL_DEV * RADIAL,))


def spread_edge(received, direction):
    lead = received.shape[:-1]
    if direction == 0:
        return jnp.tile(received, (1,) * len(lead) + (AXIAL_DEV,))
    grouped = received.reshape(lead + (AXIAL_DEV, 1, RADIAL))
    spread = jnp.broadcast_to(grouped, lead + (AXIAL_DEV, AROUND_DEV, RADIAL))
    return spread.reshape(lead + (AXIAL_DEV * AROUND_DEV * RADIAL,))


def from_next(plane, direction, edge):
    stride, extent = elem_stride(direction)
    elem_count = plane.shape[-1]
    position = jnp.arange(elem_count) // stride % extent
    moved = jnp.roll(plane, -stride, axis=plane.ndim - 1)
    fill = jnp.zeros_like(plane) if edge is None else spread_edge(edge, direction)
    return jnp.where(position == extent - 1, fill, moved)


def from_prev(plane, direction, edge):
    stride, extent = elem_stride(direction)
    elem_count = plane.shape[-1]
    position = jnp.arange(elem_count) // stride % extent
    moved = jnp.roll(plane, stride, axis=plane.ndim - 1)
    fill = jnp.zeros_like(plane) if edge is None else spread_edge(edge, direction)
    return jnp.where(position == 0, fill, moved)


def face_pair(tensor, node_axis, direction, low_nodes, high_nodes):
    first_planes = edge_elements(
        take_part(tensor, node_axis, low_nodes[0], low_nodes[1]), direction, 0
    )
    last_planes = edge_elements(
        take_part(tensor, node_axis, high_nodes[0], high_nodes[1]), direction, 1
    )
    return jnp.stack([first_planes, last_planes])


def add_faces(tensor, node_axis, direction, below_high, above_low):
    low_plane = take_part(tensor, node_axis, 0, 1)
    high_plane = take_part(tensor, node_axis, 7, 8)
    middle = take_part(tensor, node_axis, 1, 7)
    lower = low_plane + from_prev(high_plane, direction, below_high)
    upper = high_plane + from_next(low_plane, direction, above_low)
    return jnp.concatenate([lower, middle, upper], axis=node_axis)


def extend_field(tensor, node_axis, direction, below_six, above_one):
    lower = from_prev(take_part(tensor, node_axis, 6, 7), direction, below_six)
    upper = from_next(take_part(tensor, node_axis, 1, 2), direction, above_one)
    return jnp.concatenate([lower, tensor, upper], axis=node_axis)


def assemble(tensor):
    channels = tensor.shape[0]
    grid_view = tensor.reshape(channels, 8, 8, 8, tensor.shape[-1])
    received = padded(face_pair(grid_view, 1, 0, (0, 1), (7, 8)), (("wide", 0),), 1)
    grid_view = add_faces(grid_view, 1, 0, received[0], received[-1])
    received = padded(face_pair(grid_view, 2, 1, (0, 1), (7, 8)), (("narrow", 0),), 1)
    grid_view = add_faces(grid_view, 2, 1, received[0], received[-1])
    grid_view = add_faces(grid_view, 3, 2, None, None)
    return grid_view.reshape(tensor.shape)


def widen(tensor):
    grid_view = tensor.reshape(3, 8, 8, 8, tensor.shape[-1])
    received = padded(face_pair(grid_view, 1, 0, (1, 2), (6, 7)), (("wide", 0),), 1)
    grid_view = extend_field(grid_view, 1, 0, received[0], received[-1])
    received = padded(face_pair(grid_view, 2, 1, (1, 2), (6, 7)), (("narrow", 0),), 1)
    grid_view = extend_field(grid_view, 2, 1, received[0], received[-1])
    grid_view = extend_field(grid_view, 3, 2, None, None)
    return grid_view.reshape(3, 1000, -1)


def shards(
    velocity,
    element_slot,
    corner_vertex,
    axial_size,
    arc_size,
    radial_size,
    fdm_vectors,
    fdm_values,
):
    tables = node_tables()
    local_count = velocity.shape[-1]
    block_width = min(128, local_count)
    slot_of = element_slot[0]
    inverse_slot = (
        jnp.zeros((local_count,), jnp.int32)
        .at[slot_of]
        .set(jnp.arange(local_count, dtype=jnp.int32))
    )
    shape_grid = (AXIAL_DEV, AROUND_DEV, RADIAL)
    axial_len = jnp.broadcast_to(axial_size[:, None, None], shape_grid)
    around_len = jnp.broadcast_to(arc_size[None, None, :], shape_grid)
    radial_len = jnp.broadcast_to(radial_size[None, None, :], shape_grid)
    lengths = jnp.stack([axial_len, around_len, radial_len]).reshape(3, local_count)
    volume = lengths[0] * lengths[1] * lengths[2] / 8.0
    node_mass = tables[3].reshape(512)[:, None] * volume[None]
    wall_keep, sharing = node_masks(local_count)
    stored_first = velocity[:, :, inverse_slot]
    summed = assemble(jnp.concatenate([stored_first * node_mass[None], node_mass[None]], 0))
    velocity_now = summed[:3] / summed[3:4] * wall_keep
    residual_fn = partial(element_residual, tables=tables)
    solve_fn = partial(fdm_solve, vectors=fdm_vectors, values=fdm_values)
    quad_fn = partial(quadratic_form, tables=tables)
    for step_index in range(STEPS):
        local_res = blockwise(residual_fn, (velocity_now, lengths), block_width) * wall_keep
        assembled = assemble(local_res)
        extended = widen(assembled)
        correction = blockwise(solve_fn, (extended, lengths), block_width)
        direction = assemble(correction / sharing) * wall_keep
        numerator = jnp.sum(assembled * direction / sharing)
        denominator = blockwise(quad_fn, (direction, lengths), block_width)
        numerator, denominator = lax.psum((numerator, denominator), ("wide", "narrow"))
        velocity_now = velocity_now + numerator / denominator * direction
    final_res = blockwise(residual_fn, (velocity_now, lengths), block_width) * wall_keep
    corner_sums = jnp.einsum("qp,cpe->cqe", tables[2], final_res, precision=HIGH_ACCURACY)
    vertex_ids = corner_vertex[:, inverse_slot].reshape(-1)
    wide_count = lax.axis_size("wide")
    narrow_count = lax.axis_size("narrow")
    vertex_count = AXIAL_DEV * wide_count * AROUND_DEV * narrow_count * (RADIAL + 1)
    coarse_full = jax.ops.segment_sum(
        corner_sums.reshape(3, -1).T, vertex_ids, num_segments=vertex_count
    ).T
    coarse = lax.psum_scatter(coarse_full, ("wide", "narrow"), scatter_dimension=1, tiled=True)
    return (velocity_now[:, :, slot_of], coarse)


def solution(mesh):
    return jax.shard_map(
        shards,
        mesh=mesh,
        in_specs=(
            P(None, None, ("wide", "narrow")),
            P(("wide", "narrow"), None),
            P(None, ("wide", "narrow")),
            P("wide"),
            P(),
            P(),
            P(),
            P(),
        ),
        out_specs=(P(None, None, ("wide", "narrow")), P(None, ("wide", "narrow"))),
        check_vma=False,
    )
```

profile of v0, /device:TPU:1, one launch (start us, length us, event | category | flops | bytes accessed | tf_op | source)
XLA Modules:
  0.0 1332.8 jit_solution(15016492736996709649)
XLA Ops:
  23.3 4.8 collective-permute-done
  35.0 3.0 collective-permute-start.2
  68.9 7.1 convolution_bitcast_fusion.11
  77.2 6.2 fusion.19
  83.4 6.0 fusion.18
  89.4 6.4 fusion.16
  95.8 5.7 fusion.132
  105.2 6.8 collective-permute-done.4
  120.7 4.0 collective-permute-start.6
  150.6 5.0 collective-permute-start.9
  175.3 3.7 collective-permute-start.11
  189.0 2.8 fusion.95
  191.7 3.4 fusion.68
  195.2 3.0 bitcast_divide_fusion.1
  198.1 3.6 fusion.71
  201.8 3.4 fusion.74
  205.2 2.8 fusion.77
  208.3 8.3 collective-permute-done.12
  236.0 4.5 collective-permute-start.15
  259.5 66.9 %all-reduce.2 = (f32[]{:T(128)}, f32[]{:T(128)}) all-reduce(f32[]{:T(128)} %get-tuple-element.138, f32[]{:T(128)} %fusion.190), channel_id=1, replica_groups=mesh['wide'=16,'narrow'=8] {'wide','narrow'}, use_global_device_ids=true, to_apply=%region_2.3 | all-reduce | flops 2 | bytes 16 | tf_op jit(solution)/shard_map/psum | solution.py:415
  340.3 3.3 broadcast_multiply_fusion.3
  353.0 7.6 convolution_bitcast_fusion.7
  361.7 6.0 fusion.13
  367.7 6.5 fusion.12
  374.2 6.0 fusion.10
  380.3 5.9 fusion.134
  389.8 6.8 collective-permute-done.16
  396.8 3.4 collective-permute-done.17
  417.0 4.5 collective-permute-start.19
  433.0 3.1 collective-permute-start.21
  438.1 5.2 collective-permute-done.20
  459.9 4.7 collective-permute-start.23
  474.8 3.4 fusion.80
  478.2 3.0 bitcast_divide_fusion
  481.2 3.8 fusion.83
  485.0 3.4 fusion.86
  488.4 2.9 fusion.89
  491.5 6.8 collective-permute-done.24
  498.6 3.4 collective-permute-done.25
  544.8 67.7 %all-reduce.1 = (f32[]{:T(128)}, f32[]{:T(128)}) all-reduce(f32[]{:T(128)} %get-tuple-element.126, f32[]{:T(128)} %fusion.189), channel_id=1, replica_groups=mesh['wide'=16,'narrow'=8] {'wide','narrow'}, use_global_device_ids=true, to_apply=%region_6.7 | all-reduce | flops 2 | bytes 16 | tf_op jit(solution)/shard_map/psum | solution.py:415
  623.2 3.1 multiply_add_fusion.1
  638.7 7.3 convolution_bitcast_fusion.3
  647.1 6.0 fusion.7
  653.1 6.2 fusion.6
  659.3 6.0 fusion.4
  665.4 5.0 fusion.137
  671.5 10.2 scatter_custom_fusion.1
  685.9 638.3 %reduce-scatter.5.cloned.1.call-done = f32[3,136]{0,1:T(8,128)} async-done(((f32[3,17408]{0,1:T(8,128)}), f32[3,136]{0,1:T(8,128)}) %reduce-scatter.5.cloned.1.call-update) | async-done | bytes 1648
  (512 shorter events, 316.5 us)
Async XLA Ops:
  7.2 181.8 %copy-start = (f32[10,10]{1,0:T(8,128)S(1)}, f32[10,10]{1,0:T(8,128)}, u32[]{:S(2)}) copy-start(f32[10,10]{1,0:T(8,128)} %param.19) | copy-start | bytes 1204
  7.2 1317.0 %reduce-scatter.5.cloned.1.call-start = ((), (), s32[]{:S(2)}) async-start(), calls=%async_computation.1 | async-start | bytes 8982528
  10.3 6.4 copy-start.96
  11.8 50.3 %copy-start.9 = (f32[8,8,8,128]{3,0,2,1:T(8,128)}, f32[8,8,8,128]{3,0,2,1:T(8,128)S(1)}, u32[]{:S(2)}) copy-start(f32[8,8,8,128]{3,0,2,1:T(8,128)S(1)} %broadcast_multiply_fusion.8) | copy-start | bytes 786436
  16.7 6.5 copy-start.100
  16.7 6.5 copy-start.101
  17.8 10.3 collective-permute-start
  20.0 26.1 %copy-start.80 = (pred[128]{0:T(512)(128)(4,1)}, pred[128]{0:T(512)(128)(4,1)S(1)}, u32[]{:S(2)}) copy-start(pred[128]{0:T(512)(128)(4,1)S(1)} %get-tuple-element.242) | copy-start | bytes 388
  23.2 9.8 copy-start.33
  28.1 4.9 collective-permute-start.1
  32.3 15.8 %copy-start.38 = (f32[8,8,8,128]{3,2,1,0:T(8,128)}, f32[8,8,8,128]{3,2,1,0:T(8,128)S(1)}, u32[]{:S(2)}) copy-start(f32[8,8,8,128]{3,2,1,0:T(8,128)S(1)} %copy.201) | copy-start | bytes 786436
  35.0 5.3 collective-permute-start.2
  39.1 4.6 collective-permute-start.3
  77.2 6.2 copy-start.40
  89.4 6.5 copy-start.42
  105.1 6.9 collective-permute-start.4
  112.0 3.5 collective-permute-start.5
  120.7 7.9 collective-permute-start.6
  137.6 4.1 collective-permute-start.7
  150.5 7.3 copy-start.27
  150.5 6.9 collective-permute-start.8
  150.6 6.8 collective-permute-start.9
  162.2 3.7 collective-permute-start.10
  175.3 7.3 collective-permute-start.11
  208.2 8.4 collective-permute-start.12
  216.6 3.9 collective-permute-start.13
  225.2 2.6 collective-permute-start.14
  236.0 6.6 collective-permute-start.15
  367.7 6.5 copy-start.19
  374.2 6.1 copy-start.43
  389.8 6.9 collective-permute-start.16
  396.6 3.5 collective-permute-start.17
  404.7 4.2 collective-permute-start.18
  417.0 6.5 collective-permute-start.19
  432.8 10.5 copy-start.2
  433.0 5.2 collective-permute-start.21
  436.1 7.3 collective-permute-start.20
  448.2 2.1 collective-permute-start.22
  459.9 5.7 collective-permute-start.23
  491.4 6.9 collective-permute-start.24
  498.3 3.7 collective-permute-start.25
  507.3 7.4 collective-permute-start.26
  523.8 4.1 collective-permute-start.27
  530.9 6.0 copy-start.23
  530.9 6.0 copy-start.74
  653.1 6.2 copy-start.20
  659.3 6.1 copy-start.32
  659.3 6.1 copy-start.51
  (87 other events, 288.4 us)
Sparse Core Ops, SparseCore 0:
  681.8 642.2 reduce-scatter.4
where the time goes:
time: 1350 us; the launch traced here: 1330 us
  waiting for transfers between devices  701 us (52%)
  matrix products  168 us (12%)
  local copies, waits for them, and re-layouts  164 us (12%)
  blocking collectives  135 us (10%)
  other arithmetic  95.1 us (7%)
  starting transfers between devices  50.4 us (4%)
  between operations  19.7 us (1%)
    unnamed x2, waiting for transfers between devices  638 us
    psum x2, blocking collectives, shards(): lax.psum((numerator, denominator), ('wide', 'narrow'))  135 us
    dot_general x12, matrix products, to_fine(): jnp.einsum('mh,jhr->jmr', dealias_interp_matrix, flattened_values, precis...  77.2 us
    ppermute x14, waiting for transfers between devices, padded(): lax.ppermute(tail, axis, [(i, (i + 1) % count) for i in range(count)])  46.2 us
    broadcast_in_dim x28, local copies, waits for them, and re-layouts, spread_edge(): spread = jnp.broadcast_to(grouped, lead + (AXIAL_DEV, AROUND_DEV, RADIAL))  42 us
    ppermute x14, starting transfers between devices, padded(): lax.ppermute(head, axis, [((i + 1) % count, i) for i in range(count)])  33.9 us
    dot_general x12, matrix products, apply_first(): jnp.einsum('ai,cijkb->cajkb', matrix, tensor, precision=HIGH_ACCURACY)  27.9 us
  transfers between devices with their start and end apart: 29, of which 21 were waited for; matrix products, arithmetic and copies ran while one was open for 3% of the time, Pallas kernels for 0%

commit v1 on v0

v1 whole, which is shorter than its diff:
```python
from functools import partial

import jax
import jax.numpy as jnp
import ml_dtypes
import numpy as np
from jax import lax
from jax.experimental import pallas as pl
from jax.experimental.pallas import tpu as pltpu
from jax.sharding import PartitionSpec as P

RADIAL = 16
SIGMA = 4.0
VISCOSITY = 0.05
F32 = jnp.float32
BF16 = jnp.bfloat16
EXACT = lax.Precision.HIGHEST
BOTH = ("wide", "narrow")


def node_tables():
    x = np.array(
        [-1.0, -0.8717401485096066, -0.5917001814331423, -0.2092992179024789]
    )
    x = np.concatenate([x, -x[::-1]])
    w = np.array([1.0 / 28.0, 0.2107042271435061, 0.3411226924835044, 0.4124587946587038])
    w = np.concatenate([w, w[::-1]])
    scale = np.array([np.prod([x[t] - x[p] for p in range(8) if p != t]) for t in range(8)])
    deriv = np.zeros((8, 8))
    for t in range(8):
        for s in range(8):
            if t != s:
                deriv[t, s] = scale[t] / (scale[s] * (x[t] - x[s]))
        deriv[t, t] = -np.sum(deriv[t])
    y = np.array(
        [
            -0.9815606342467192,
            -0.9041172563704749,
            -0.7699026741943047,
            -0.5873179542866175,
            -0.3678314989981802,
            -0.1252334085114689,
        ]
    )
    y = np.concatenate([y, -y[::-1]])
    v = np.array(
        [
            0.0471753363865118,
            0.1069393259953184,
            0.1600783285433462,
            0.2031674267230659,
            0.2334925365383548,
            0.2491470458134028,
        ]
    )
    v = np.concatenate([v, v[::-1]])
    interp = np.ones((12, 8))
    for s in range(8):
        for p in range(8):
            if p != s:
                interp[:, s] = interp[:, s] * (y - x[p]) / (x[s] - x[p])
    linear = np.stack([(1.0 - x) / 2.0, (1.0 + x) / 2.0])
    return w, deriv, v, interp, linear


W, D, VF, J, LIN = node_tables()
B = J @ D
JV = J.T * VF[None, :]
STIFF = D.T @ (W[:, None] * D)
WJK = np.kron(W, W)


def two_parts(matrix):
    hi = matrix.astype(np.float32).astype(ml_dtypes.bfloat16)
    lo = (matrix - hi.astype(np.float64)).astype(ml_dtypes.bfloat16)
    return hi, lo


def four_terms(matrix):
    hi, lo = two_parts(matrix)
    return np.concatenate([hi, lo, hi, lo], axis=1)


def three_terms(matrix):
    hi, lo = two_parts(matrix)
    return np.concatenate([hi, lo, hi], axis=1)


FINE = four_terms(np.concatenate([np.kron(J, J), np.kron(B, J), np.kron(J, B)]))
BACK = three_terms(np.kron(JV, JV))
STIFF_JK = four_terms(
    np.concatenate([np.kron(STIFF, np.diag(W)), np.kron(np.diag(W), STIFF)])
)
GRAD_JK = four_terms(np.concatenate([np.kron(D, np.eye(8)), np.kron(np.eye(8), D)]))


def call(kernel, outs, args, scratch=(), spaces=None):
    spaces = spaces or {}
    return pl.pallas_call(
        kernel,
        out_shape=[jax.ShapeDtypeStruct(s, d) for s, d in outs],
        in_specs=[
            pl.BlockSpec(memory_space=spaces.get(i, pltpu.VMEM)) for i in range(len(args))
        ],
        out_specs=[pl.BlockSpec(memory_space=pltpu.VMEM) for _ in outs],
        scratch_shapes=list(scratch),
        compiler_params=pltpu.CompilerParams(vmem_limit_bytes=56 << 20),
        name=kernel.func.__name__ if isinstance(kernel, partial) else kernel.__name__,
    )(*args)


def iota(shape, dim):
    return lax.broadcasted_iota(jnp.int32, shape, dim)


def lanes_by(x, shift):
    return pltpu.roll(x, shift % x.shape[-1], x.ndim - 1)


def rows_by(x, shift):
    return pltpu.roll(x, shift % 8, x.ndim - 2)


def split(x):
    hi = x.astype(BF16)
    return hi, (x - hi.astype(F32)).astype(BF16)


def dot(a, b):
    return jnp.dot(a, b, preferred_element_type=F32)


def even_odd(matrix, xs, sign):
    n_out, n_in = matrix.shape
    half = n_in // 2
    even = [xs[i] + xs[n_in - 1 - i] for i in range(half)]
    odd = [xs[i] - xs[n_in - 1 - i] for i in range(half)]
    outs = [None] * n_out
    for a in range(n_out // 2):
        e = sum(
            float((matrix[a, i] + matrix[a, n_in - 1 - i]) / 2) * even[i] for i in range(half)
        )
        o = sum(
            float((matrix[a, i] - matrix[a, n_in - 1 - i]) / 2) * odd[i] for i in range(half)
        )
        outs[a] = e + o
        outs[n_out - 1 - a] = e - o if sign > 0 else o - e
    return outs


def keep_rows(rows):
    k = iota((rows, 128), 0) & 7
    r = iota((rows, 128), 1) & (RADIAL - 1)
    wall = ((k == 0) & (r == 0)) | ((k == 7) & (r == RADIAL - 1))
    return jnp.where(wall, 0.0, 1.0).astype(F32)


def radial_parts(x):
    r = iota((8, 128), 1) & (RADIAL - 1)
    below = jnp.where(r > 0, lanes_by(x, 1), 0.0)
    above = jnp.where(r < RADIAL - 1, lanes_by(x, -1), 0.0)
    return below, above


def radial_sum(x, below, above):
    k = iota((8, 128), 0)
    return x + jnp.where(k == 0, rows_by(below, 1), jnp.where(k == 7, rows_by(above, -1), 0.0))


def pack_low(plane_of):
    et = iota((8, 128), 1) >> 4
    out = jnp.zeros((8, 128), F32)
    for i in range(8):
        out = jnp.where(et == i, lanes_by(plane_of(i), 16 * i), out)
    return out


def pack_high(plane_of):
    et = iota((8, 128), 1) >> 4
    out = jnp.zeros((8, 128), F32)
    for i in range(8):
        out = jnp.where(et == i, lanes_by(plane_of(i), 16 * i + 16), out)
    return out


def from_low(plane, packed, i):
    lane = iota((8, 128), 1)
    return jnp.where(lane < 16, lanes_by(packed, -16 * i), lanes_by(plane, 16))


def from_high(plane, packed, i):
    lane = iota((8, 128), 1)
    return jnp.where(lane >= 112, lanes_by(packed, 112 - 16 * i), lanes_by(plane, -16))


def start_kernel(vel, slot, corner, arc, rad, axial, mv, low, high, lanes, place):
    ht = jnp.broadcast_to(arc[...], (8, 16))
    hr = jnp.broadcast_to(rad[...], (8, 16))
    spread = ((iota((16, 256), 1) & 15) == iota((16, 256), 0)).astype(F32)
    ht = jnp.dot(ht, spread, precision=EXACT, preferred_element_type=F32)[0:1]
    hr = jnp.dot(hr, spread, precision=EXACT, preferred_element_type=F32)[0:1]
    hz = jnp.zeros((1, 256), F32) + axial[0]
    g = ht * hr / 8.0
    vol = hz * g
    r = iota((1, 256), 1) & (RADIAL - 1)
    g_low = g + jnp.where(r > 0, lanes_by(g, 1), 0.0)
    g_high = g + jnp.where(r < RADIAL - 1, lanes_by(g, -1), 0.0)
    rows = [
        vol,
        vol * (2.0 / hz),
        vol * (2.0 / ht),
        vol * (2.0 / hr),
        VISCOSITY * vol * (2.0 / hz) * (2.0 / hz),
        VISCOSITY * vol * (2.0 / ht) * (2.0 / ht),
        VISCOSITY * vol * (2.0 / hr) * (2.0 / hr),
        hz,
        1.0 / g,
        1.0 / g_low,
        1.0 / g_high,
    ]
    for n, row in enumerate(rows):
        lanes[n : n + 1] = row
    for n in range(len(rows), 16):
        lanes[n : n + 1] = jnp.zeros((1, 256), F32)
    hot = (slot[...] == iota((128, 128), 0)).astype(F32)
    nt = (((1,), (1,)), ((), ()))

    def body(c, carry):
        x = vel[c].reshape(512, 128)
        y = lax.dot_general(x, hot, nt, precision=EXACT, preferred_element_type=F32)
        mv[c] = (y * vol[:, :128]).reshape(8, 64, 128)
        low[c] = pack_low(lambda i: mv[c, i, 0:8])
        high[c] = pack_high(lambda i: mv[c, i, 56:64])
        return carry

    lax.fori_loop(0, 3, body, 0)
    ids = lax.dot_general(
        corner[...].astype(F32), hot, nt, precision=EXACT, preferred_element_type=F32
    )
    place[...] = (ids + 0.5).astype(jnp.int32)


def solve_tables_kernel(vectors, values, lanes, forward, inverse, scale):
    s = vectors[...]
    ident = (iota((10, 10), 0) == iota((10, 10), 1)).astype(F32)
    st = lax.dot_general(
        ident, s, (((1,), (1,)), ((), ())), precision=EXACT, preferred_element_type=F32
    )

    def mul(a, b):
        return jnp.dot(a, b, precision=EXACT, preferred_element_type=F32)

    row, col = iota((112, 10), 0), iota((112, 10), 1)
    live = row < 100
    by_b = ((row // 10 == col) & live).astype(F32)
    by_c = ((row % 10 == col) & live).astype(F32)
    node, pos = iota((10, 160), 0), iota((10, 160), 1)
    slot = pos & 15
    k_of = jnp.where(slot < 8, slot + 1, jnp.where(slot == 8, 0, jnp.where(slot == 9, 9, -1)))
    by_j = (node == (pos >> 4)).astype(F32)
    by_k = (node == k_of).astype(F32)
    full = mul(mul(by_b, st), by_j) * mul(mul(by_c, st), by_k)
    hi, lo = split(full)
    forward[:, 0:160] = hi
    forward[:, 160:320] = lo
    forward[:, 320:480] = hi

    row8, col8 = iota((64, 10), 0), iota((64, 10), 1)
    by_j8 = ((row8 >> 3) + 1 == col8).astype(F32)
    by_k8 = ((row8 & 7) + 1 == col8).astype(F32)
    node2, pos2 = iota((10, 112), 0), iota((10, 112), 1)
    b_of = jnp.where(pos2 < 100, pos2 // 10, -1)
    c_of = jnp.where(pos2 < 100, pos2 % 10, -1)
    to_b = (node2 == b_of).astype(F32)
    to_c = (node2 == c_of).astype(F32)
    full = mul(mul(by_j8, s), to_b) * mul(mul(by_k8, s), to_c)
    hi, lo = split(full)
    inverse[:, 0:112] = hi
    inverse[:, 112:224] = lo
    inverse[:, 224:336] = hi

    lam = jnp.broadcast_to(values[...], (8, 10))
    nt = (((1,), (1,)), ((), ()))
    lam_b = lax.dot_general(by_b, lam, nt, precision=EXACT, preferred_element_type=F32)[:, 0:1]
    lam_c = lax.dot_general(by_c, lam, nt, precision=EXACT, preferred_element_type=F32)[:, 0:1]
    vol = lanes[0:1, :128]
    flat = (
        SIGMA * vol
        + lam_b * jnp.broadcast_to(lanes[5:6, :128], (112, 128))
        + lam_c * jnp.broadcast_to(lanes[6:7, :128], (112, 128))
    )
    for a in range(10):
        scale[a] = 1.0 / (flat + values[0:1, a : a + 1] * lanes[4:5, :128])


def around_sum_kernel(field, tlo, thi, lanes, out, down, up):
    def body(c, carry):
        lo, hi = tlo[c], thi[c]
        for i in range(8):
            x = field[c, i]
            first, last = x[0:8], x[56:64]
            head = first + from_low(last, lo, i)
            tail = last + from_high(first, hi, i)
            out[c, i] = x
            out[c, i, 0:8] = head
            out[c, i, 56:64] = tail
        base = pl.multiple_of(c * 64, 64)
        down[pl.ds(base, 64)] = out[c, 0]
        up[pl.ds(base, 64)] = out[c, 7]
        return carry

    lax.fori_loop(0, 3, body, 0)
    hz = jnp.broadcast_to(lanes[7:8, :128], (8, 128))
    down[192:200] = hz
    up[192:200] = hz


def finish_sum(field, zlo, zhi, out, factor):
    def body(c, carry):
        base = pl.multiple_of(c * 64, 64)
        for i in range(8):
            x = field[c, i]
            if i == 0:
                x = x + zlo[pl.ds(base, 64)]
            if i == 7:
                x = x + zhi[pl.ds(base, 64)]
            for j in range(8):
                v = x[8 * j : 8 * j + 8]
                below, above = radial_parts(v)
                out[c, i, 8 * j : 8 * j + 8] = radial_sum(v, below, above) * factor(i, j)
        return carry

    lax.fori_loop(0, 3, body, 0)


def residual(u, lanes, fine, back, stiff, wjk, res, xu, xw, xs, pf, qf, xc, yf, sz, ks):
    def put(ref, at, rb, half, x):
        hi, lo = split(x)
        for term, part in enumerate((hi, hi, lo, lo)):
            ref[at, pl.ds(pl.multiple_of(term * 64 + rb * 16, 16), 16),
                half * 128 : half * 128 + 128] = part

    def first(t, carry):
        c, rb = t // 4, t % 4
        rows = pl.ds(pl.multiple_of(rb * 16, 16), 16)
        x = [u[c, i, rows] for i in range(8)]
        for a, val in enumerate(even_odd(J, x, 1)):
            put(xu, c * 6 + a // 2, rb, a % 2, val)
        for a, val in enumerate(even_odd(B, x, -1)):
            put(xw, c * 6 + a // 2, rb, a % 2, val)
        for i in range(8):
            put(xs, c * 4 + i // 2, rb, i % 2, x[i])
        for i, val in enumerate(even_odd(STIFF, x, 1)):
            sz[c, i, rows] = val
        return carry

    lax.fori_loop(0, 12, first, 0)

    def second(p, carry):
        for c in range(3):
            pf[c] = dot(fine[...], xu[c * 6 + p])
            qf[c] = dot(fine[0:144], xw[c * 6 + p])
        lz, lt, lr = lanes[1:2], lanes[2:3], lanes[3:4]
        for r in range(9):
            rows = slice(16 * r, 16 * r + 16)
            vz = pf[0, rows] * lz
            vt = pf[1, rows] * lt
            vr = pf[2, rows] * lr
            for c in range(3):
                conv = (
                    vz * qf[c, rows]
                    + vt * pf[c, 144 + 16 * r : 160 + 16 * r]
                    + vr * pf[c, 288 + 16 * r : 304 + 16 * r]
                )
                hi, lo = split(conv)
                xc[c, rows] = hi
                xc[c, 144 + 16 * r : 160 + 16 * r] = hi
                xc[c, 288 + 16 * r : 304 + 16 * r] = lo
        for c in range(3):
            y = dot(back[...], xc[c])
            yf[c, 2 * p] = y[:, :128]
            yf[c, 2 * p + 1] = y[:, 128:]
        return carry

    lax.fori_loop(0, 6, second, 0)

    def third(t, carry):
        y = dot(stiff[...], xs[t])
        c, p = t // 4, t % 4
        ks[c, 2 * p] = y[:, :128]
        ks[c, 2 * p + 1] = y[:, 128:]
        return carry

    lax.fori_loop(0, 12, third, 0)
    kz, kt, kr = lanes[4:5, :128], lanes[5:6, :128], lanes[6:7, :128]
    keep = keep_rows(16)

    def fourth(t, carry):
        c, rb = t // 4, t % 4
        rows = pl.ds(pl.multiple_of(rb * 16, 16), 16)
        more = pl.ds(pl.multiple_of(64 + rb * 16, 16), 16)
        adv = even_odd(JV, [yf[c, a, rows] for a in range(12)], 1)
        wz = wjk[rows] * kz
        for i in range(8):
            plane = float(W[i]) * (kt * ks[c, i, rows] + kr * ks[c, i, more])
            res[c, i, rows] = -(adv[i] + wz * sz[c, i, rows] + plane) * keep
        return carry

    lax.fori_loop(0, 12, fourth, 0)


def pack_two(res, low, high):
    def body(c, carry):
        for n in range(2):
            low[c, 8 * n : 8 * n + 8] = pack_low(lambda i: res[c, i, 8 * n : 8 * n + 8])
            high[c, 8 * n : 8 * n + 8] = pack_high(
                lambda i: res[c, i, 48 + 8 * n : 56 + 8 * n]
            )
        return carry

    lax.fori_loop(0, 3, body, 0)


def project_kernel(
    field, zlo, zhi, lanes, fine, back, stiff, wjk, u, res, low, high, *scratch
):
    hz = lanes[7:8, :128]
    inner = 1.0 / hz
    first = 1.0 / (hz + zlo[192:193])
    last = 1.0 / (hz + zhi[192:193])
    k = iota((8, 128), 0)
    rk = jnp.where(
        k == 0, lanes[9:10, :128], jnp.where(k == 7, lanes[10:11, :128], lanes[8:9, :128])
    )
    rk = rk * keep_rows(8)
    by_plane = {0: rk * first, 7: rk * last}
    middle = rk * inner

    def factor(i, j):
        f = by_plane.get(i, middle)
        return 0.5 * f if j in (0, 7) else f

    finish_sum(field, zlo, zhi, u, factor)
    residual(u, lanes, fine, back, stiff, wjk, res, *scratch)
    pack_two(res, low, high)


def step_length(sums):
    total = jnp.sum(sums[...], axis=0, keepdims=True)
    return total[:, 0:1] / total[:, 1:2]


def advance(u_old, d, sums, u):
    alpha = step_length(sums)

    def body(t, carry):
        c, i = t // 8, t % 8
        u[c, i] = u_old[c, i] + alpha * d[c, i]
        return carry

    lax.fori_loop(0, 24, body, 0)


def advance_kernel(
    u_old, d, sums, lanes, fine, back, stiff, wjk, u, res, low, high, *scratch
):
    advance(u_old, d, sums, u)
    residual(u, lanes, fine, back, stiff, wjk, res, *scratch)
    pack_two(res, low, high)


def around_widen_kernel(res, tlo, thi, out, down, up):
    lane = iota((8, 128), 1)

    def body(c, carry):
        lo6, lo7, hi0, hi1 = tlo[c, 0:8], tlo[c, 8:16], thi[c, 0:8], thi[c, 8:16]
        for i in range(8):
            x = res[c, i]
            first, last = x[0:8], x[56:64]
            out[c, i, 0:64] = x
            out[c, i, 0:8] = first + from_low(last, lo7, i)
            out[c, i, 56:64] = last + from_high(first, hi0, i)
            out[c, i, 64:72] = jnp.where(
                lane < 64, lanes_by(lo6, -16 * i), lanes_by(hi1, 112 - 16 * i)
            )
        for n in range(2):
            down[c, n] = out[c, n]
            up[c, n] = out[c, 6 + n]
        return carry

    lax.fori_loop(0, 3, body, 0)


def solve_kernel(
    field, zlo, zhi, vectors, forward, inverse, scale, corr, low, high, xf, yf, xb
):
    lane = iota((8, 128), 1)
    k = iota((8, 128), 0)
    r = lane & (RADIAL - 1)

    def widen(c, p):
        for half in range(2):
            n = 2 * p + half
            if n == 0:
                e = zlo[c, 0]
            elif n == 1:
                e = field[c, 0] + zlo[c, 1]
            elif n == 8:
                e = field[c, 7] + zhi[c, 0]
            elif n == 9:
                e = zhi[c, 1]
            else:
                e = field[c, n - 1]
            extra = e[64:72]
            planes = [e[8 * j : 8 * j + 8] for j in range(8)]
            under = jnp.where(lane < 16, extra, lanes_by(planes[6], 16))
            over = jnp.where(lane >= 112, extra, lanes_by(planes[1], -16))
            for j, v in enumerate([under] + planes + [over]):
                below, above = radial_parts(v)
                own = radial_sum(v, below, above)
                side = jnp.where(k == 0, rows_by(below, 2), jnp.where(k == 1, above, 0.0))
                hi, lo = split(jnp.concatenate([own, side], axis=0))
                cols = slice(half * 128, half * 128 + 128)
                xf[16 * j : 16 * j + 16, cols] = hi
                xf[160 + 16 * j : 176 + 16 * j, cols] = hi
                xf[320 + 16 * j : 336 + 16 * j, cols] = lo

    def body(c, carry):
        for p in range(5):
            widen(c, p)
            y = dot(forward[...], xf[...])
            yf[c, 2 * p] = y[:, :128]
            yf[c, 2 * p + 1] = y[:, 128:]
        return carry

    lax.fori_loop(0, 3, body, 0)

    def mid(t, carry):
        c, rb = t // 7, t % 7
        rows = pl.ds(pl.multiple_of(rb * 16, 16), 16)
        y = [yf[c, i, rows] for i in range(10)]
        spec = []
        for a in range(10):
            acc = vectors[0, a] * y[0]
            for i in range(1, 10):
                acc = acc + vectors[i, a] * y[i]
            spec.append(acc * scale[a, rows])
        for i in range(8):
            acc = vectors[i + 1, 0] * spec[0]
            for a in range(1, 10):
                acc = acc + vectors[i + 1, a] * spec[a]
            hi, lo = split(acc)
            cols = slice((i % 2) * 128, (i % 2) * 128 + 128)
            for term, part in enumerate((hi, hi, lo)):
                xb[c * 4 + i // 2, pl.ds(pl.multiple_of(term * 112 + rb * 16, 16), 16),
                   cols] = part
        return carry

    lax.fori_loop(0, 21, mid, 0)

    inner = ((k == 0) & (r > 0)) | ((k == 7) & (r < RADIAL - 1))
    share = jnp.where(inner, 0.5, 1.0).astype(F32)

    def last(c, carry):
        for p in range(4):
            y = dot(inverse[...], xb[c * 4 + p])
            for half in range(2):
                i = 2 * p + half
                for j in range(8):
                    f = (0.5 if i in (0, 7) else 1.0) * (0.5 if j in (0, 7) else 1.0)
                    corr[c, i, 8 * j : 8 * j + 8] = (
                        y[8 * j : 8 * j + 8, half * 128 : half * 128 + 128] * (share * f)
                    )
        low[c] = pack_low(lambda i: corr[c, i, 0:8])
        high[c] = pack_high(lambda i: corr[c, i, 56:64])
        return carry

    lax.fori_loop(0, 3, last, 0)


def direction_kernel(field, zlo, zhi, res, lanes, grad, wjk, d, sums, xs, acc):
    keep = keep_rows(8)
    finish_sum(field, zlo, zhi, d, lambda i, j: keep)
    acc[...] = jnp.zeros_like(acc)
    vol = lanes[0:1, :128]
    kz, kt, kr = lanes[4:5, :128], lanes[5:6, :128], lanes[6:7, :128]

    def first(t, carry):
        c, rb = t // 4, t % 4
        rows = pl.ds(pl.multiple_of(rb * 16, 16), 16)
        x = [d[c, i, rows] for i in range(8)]
        num = sum(x[i] * res[c, i, rows] for i in range(8))
        sq = sum(float(W[i]) * (x[i] * x[i]) for i in range(8))
        gz = sum(float(W[i]) * (g * g) for i, g in enumerate(even_odd(D, x, -1)))
        acc[0] += num
        acc[1] += wjk[rows] * (SIGMA * vol * sq + kz * gz)
        for i in range(8):
            hi, lo = split(x[i])
            for term, part in enumerate((hi, hi, lo, lo)):
                xs[c * 4 + i // 2, pl.ds(pl.multiple_of(term * 64 + rb * 16, 16), 16),
                   (i % 2) * 128 : (i % 2) * 128 + 128] = part
        return carry

    lax.fori_loop(0, 12, first, 0)

    def second(c, carry):
        total = jnp.zeros((16, 128), F32)
        for p in range(4):
            y = dot(grad[...], xs[c * 4 + p])
            for half in range(2):
                v = y[:, half * 128 : half * 128 + 128]
                v = v * v
                plane = jnp.zeros((16, 128), F32)
                for q in range(4):
                    rows = slice(16 * q, 16 * q + 16)
                    plane = plane + wjk[rows] * (
                        kt * v[rows] + kr * v[64 + 16 * q : 80 + 16 * q]
                    )
                total = total + float(W[2 * p + half]) * plane
        acc[1] += total
        return carry

    lax.fori_loop(0, 3, second, 0)
    num = jnp.sum(jnp.sum(acc[0], axis=0, keepdims=True), axis=1, keepdims=True)
    den = jnp.sum(jnp.sum(acc[1], axis=0, keepdims=True), axis=1, keepdims=True)
    at = iota((128, 128), 1)
    sums[...] = jnp.where(at == 0, num, jnp.where(at == 1, den, 0.0))


def last_kernel(
    u_old, d, sums, lanes, fine, back, stiff, wjk, slot, place, vel, dense, u, res, *scratch
):
    advance(u_old, d, sums, u)
    residual(u, lanes, fine, back, stiff, wjk, res, *scratch)
    hot = (slot[...] == iota((128, 128), 0)).astype(F32)
    nt = (((1,), (1,)), ((), ()))
    row, col = iota((8, 64), 0), iota((8, 64), 1)

    def weight(node, upper):
        out = jnp.zeros((8, 64), F32)
        for n in range(8):
            out = jnp.where(
                node == n, jnp.where(upper, float(LIN[1, n]), float(LIN[0, n])), out
            )
        return out

    corner_jk = weight(col >> 3, (row & 2) != 0) * weight(col & 7, (row & 1) != 0)
    owner = place[...] // 136
    place_in = place[...] - owner * 136
    dev = iota((128, 128), 0)
    dense[...] = jnp.zeros_like(dense)

    def body(c, carry):
        flat = u[c].reshape(512, 128)
        vel[c] = jnp.dot(flat, hot, precision=EXACT, preferred_element_type=F32).reshape(
            8, 64, 128
        )
        planes = [res[c, i] for i in range(8)]
        z1 = sum(float(LIN[1, i]) * planes[i] for i in range(1, 8))
        z0 = sum(float(LIN[0, i]) * planes[i] for i in range(7))
        s0 = jnp.dot(corner_jk, z0, precision=EXACT, preferred_element_type=F32)
        s1 = jnp.dot(corner_jk, z1, precision=EXACT, preferred_element_type=F32)
        left, right = [], []
        pos = iota((408, 128), 0)
        for q in range(8):
            val = (s1 if q >= 4 else s0)[q % 4 : q % 4 + 1]
            left.append(jnp.where(owner[q : q + 1] == dev, val, 0.0))
            right.append((place_in[q : q + 1] + c * 136 == pos).astype(F32))
        dense[...] += lax.dot_general(
            jnp.concatenate(left, axis=1),
            jnp.concatenate(right, axis=1),
            nt,
            precision=EXACT,
            preferred_element_type=F32,
        )
        return carry

    lax.fori_loop(0, 3, body, 0)


FIELD = (3, 8, 64, 128)


def both_ways(axis, to_next, to_prev):
    n = lax.axis_size(axis)
    up = [(i, (i + 1) % n) for i in range(n)]
    down = [((i + 1) % n, i) for i in range(n)]
    return lax.ppermute(to_next, axis, up), lax.ppermute(to_prev, axis, down)


def residual_scratch():
    return [
        pltpu.VMEM((18, 256, 256), BF16),
        pltpu.VMEM((18, 256, 256), BF16),
        pltpu.VMEM((12, 256, 256), BF16),
        pltpu.VMEM((3, 432, 256), F32),
        pltpu.VMEM((3, 144, 256), F32),
        pltpu.VMEM((3, 432, 256), BF16),
        pltpu.VMEM((3, 12, 64, 128), F32),
        pltpu.VMEM(FIELD, F32),
        pltpu.VMEM((3, 8, 128, 128), F32),
    ]


def shards(vel, slot, corner, axial, arc, rad, vectors, values):
    fine, back, stiff, grad = (jnp.asarray(m) for m in (FINE, BACK, STIFF_JK, GRAD_JK))
    wjk = jnp.asarray(np.broadcast_to(WJK[:, None], (64, 128)).astype(np.float32))
    smem = pltpu.SMEM
    mv, low, high, lanes, place = call(
        start_kernel,
        [(FIELD, F32), ((3, 8, 128), F32), ((3, 8, 128), F32), ((16, 256), F32),
         ((8, 128), jnp.int32)],
        (vel.reshape(FIELD), slot, corner, arc[None], rad[None], axial),
        spaces={5: smem},
    )
    forward, inverse, scale = call(
        solve_tables_kernel,
        [((112, 480), BF16), ((64, 336), BF16), ((10, 112, 128), F32)],
        (vectors, values[None], lanes),
    )

    def sum_rounds(field, low, high):
        tlo, thi = both_ways("narrow", high, low)
        out, down, up = call(
            around_sum_kernel,
            [(FIELD, F32), ((200, 128), F32), ((200, 128), F32)],
            (field, tlo, thi, lanes),
        )
        zlo, zhi = both_ways("wide", up, down)
        return out, zlo, zhi

    local = (lanes, fine, back, stiff, wjk)
    packs = [(FIELD, F32), (FIELD, F32), ((3, 16, 128), F32), ((3, 16, 128), F32)]
    u, res, low, high = call(
        project_kernel, packs, (*sum_rounds(mv, low, high), *local), residual_scratch()
    )
    sums = None
    for step in range(2):
        if step > 0:
            u, res, low, high = call(
                advance_kernel, packs, (u, d, sums, *local), residual_scratch()
            )
        tlo, thi = both_ways("narrow", high, low)
        wide_field, down, up = call(
            around_widen_kernel,
            [((3, 8, 72, 128), F32), ((3, 2, 72, 128), F32), ((3, 2, 72, 128), F32)],
            (res, tlo, thi),
        )
        zlo, zhi = both_ways("wide", up, down)
        corr, low, high = call(
            solve_kernel,
            [(FIELD, F32), ((3, 8, 128), F32), ((3, 8, 128), F32)],
            (wide_field, zlo, zhi, vectors, forward, inverse, scale),
            [
                pltpu.VMEM((480, 256), BF16),
                pltpu.VMEM((3, 10, 112, 128), F32),
                pltpu.VMEM((12, 336, 256), BF16),
            ],
            spaces={3: smem},
        )
        d, part = call(
            direction_kernel,
            [(FIELD, F32), ((128, 128), F32)],
            (*sum_rounds(corr, low, high), res, lanes, grad, wjk),
            [pltpu.VMEM((12, 256, 256), BF16), pltpu.VMEM((2, 16, 128), F32)],
        )
        sums = lax.all_to_all(part, BOTH, 0, 0, tiled=True)
    out, dense = call(
        last_kernel,
        [(FIELD, F32), ((128, 408), F32)],
        (u, d, sums, *local, slot, place),
        [pltpu.VMEM(FIELD, F32), pltpu.VMEM(FIELD, F32)] + residual_scratch(),
    )
    coarse = jnp.sum(lax.all_to_all(dense, BOTH, 0, 0, tiled=True), axis=0)
    return out.reshape(3, 512, 128), coarse.reshape(3, 136)


def solution(mesh):
    return jax.shard_map(
        shards,
        mesh=mesh,
        in_specs=(P(None, None, BOTH), P(BOTH, None), P(None, BOTH), P("wide"), P(), P(), P(), P()),
        out_specs=(P(None, None, BOTH), P(None, BOTH)),
        check_vma=False,
    )
```

time: 1350 us -> 216 us (0.16); the launches traced: 1330 us -> 216 us
  waiting for transfers between devices: 701 us -> 29.7 us
  matrix products: 168 us -> 0 us
  local copies, waits for them, and re-layouts: 164 us -> 8.47 us
  other arithmetic: 95.1 us -> 0.24 us
  Pallas kernels: 0 us -> 85.7 us
  blocking collectives: 135 us -> 55.5 us
  between operations: 19.7 us -> 1.33 us
  starting transfers between devices: 50.4 us -> 34.7 us
    unnamed x2 -> x0, waiting for transfers between devices: 638 us -> none
    dot_general x52 -> x0, matrix products: 168 us -> none  [the longest x12 77.2 us: to_fine(): jnp.einsum('mh,jhr->jmr', dealias_interp_matrix, flattened_values, precis...]
    psum x2 -> x0, blocking collectives: 135 us -> none  [shards(): lax.psum((numerator, denominator), ('wide', 'narrow'))]
    pallas_call x0 -> x14, Pallas kernels: none -> 85.7 us  [call(): pl.pallas_call(kernel, out_shape=[jax.ShapeDtypeStruct(s, d) for s, d in...]
    all_to_all x0 -> x3, blocking collectives: none -> 55.5 us  [the longest x2 40 us: shards(): sums = lax.all_to_all(part, BOTH, 0, 0, tiled=True)]
    broadcast_in_dim x28 -> x0, local copies, waits for them, and re-layouts: 42 us -> none  [spread_edge(): spread = jnp.broadcast_to(grouped, lead + (AXIAL_DEV, AROUND_DEV, RADIAL))]
    add x33 -> x0, other arithmetic: 40.7 us -> none  [the longest x15 18.3 us: add_faces(): lower = low_plane + from_prev(high_plane, direction, below_high)]
    ppermute x28 -> x20, waiting for transfers between devices: 62.4 us -> 29.7 us  [both_ways(): return (lax.ppermute(to_next, axis, up), lax.ppermute(to_prev, axis, down))]
  transfers between devices with their start and end apart: 29 -> 20, of which waited for: 21 -> 15; matrix products, arithmetic and copies ran while one was open for 3% -> 0% of each run, Pallas kernels for 0% -> 1%
where the time goes in v1:
time: 216 us
  Pallas kernels  85.7 us (40%)
  blocking collectives  55.5 us (26%)
  starting transfers between devices  34.7 us (16%)
  waiting for transfers between devices  29.7 us (14%)
  local copies, waits for them, and re-layouts  8.47 us (4%)
    pallas_call x14, Pallas kernels, call(): pl.pallas_call(kernel, out_shape=[jax.ShapeDtypeStruct(s, d) for s, d in...  85.7 us
    all_to_all x2, blocking collectives, shards(): sums = lax.all_to_all(part, BOTH, 0, 0, tiled=True)  40 us
    ppermute x20, starting transfers between devices, both_ways(): return (lax.ppermute(to_next, axis, up), lax.ppermute(to_prev, axis, down))  34.7 us
    ppermute x20, waiting for transfers between devices, both_ways(): return (lax.ppermute(to_next, axis, up), lax.ppermute(to_prev, axis, down))  29.7 us
    all_to_all x1, blocking collectives, shards(): coarse = jnp.sum(lax.all_to_all(dense, BOTH, 0, 0, tiled=True), axis=0)  15.5 us
    unnamed x40, local copies, waits for them, and re-layouts  6.57 us
  transfers between devices with their start and end apart: 20, of which 15 were waited for; matrix products, arithmetic and copies ran while one was open for 0% of the time, Pallas kernels for 1%

profile of v1, /device:TPU:1, one launch (start us, length us, event | category | flops | bytes accessed | tf_op | source)
XLA Modules:
  0.0 215.6 jit_solution(9747348558693077625)
XLA Ops:
  1.3 3.6 %start_kernel.1 = (f32[3,8,64,128]{3,2,1,0:T(8,128)}, f32[3,8,128]{2,1,0:T(8,128)}, f32[3,8,128]{2,1,0:T(8,128)}, f32[16,256]{1,0:T(8,128)}, s32[8,128]{1,0:T(8,128)}) custom-call(f32[3,8,64,128]{3,2,1,0:T(8,128)} %bitcast.14, s32[1,128]{1,0:T(1,128)} %slot.3, s32[8,128]{1,0:T(8,128)} %corner.1, f32[1,16]{1,0:T(1,128)} %bitcast.20, f32[1,16]{1,0:T(1,128)} %bitcast.21, ...), custom_call_target="tpu_custom_call" | custom-call | tf_op jit(solution)/shard_map/start_kernel/pallas_call | solution.py:99
  4.8 2.6 %collective-permute-start = (f32[3,8,128]{2,1,0:T(8,128)}, f32[3,8,128]{2,1,0:T(8,128)S(1)}, u32[]{:S(2)}, u32[]{:S(2)}) collective-permute-start(f32[3,8,128]{2,1,0:T(8,128)} %get-tuple-element.46), channel_id=1, source_target_pairs={{0,1},{1,2},{2,3},{3,4},{4,5},{5,6},{6,7},{7,0},{8,9},{9,10},{10,1... | collective-permute-start | bytes 36872 | tf_op jit(solution)/shard_map/ppermute | solution.py:688
  7.4 1.0 collective-permute-done.tlo
  8.5 2.3 %collective-permute-done.1.thi = f32[3,8,128]{2,1,0:T(8,128)S(1)} collective-permute-done((f32[3,8,128]{2,1,0:T(8,128)}, f32[3,8,128]{2,1,0:T(8,128)S(1)}, u32[]{:S(2)}, u32[]{:S(2)}) %collective-permute-start.1) | collective-permute-done | bytes 12320 | tf_op jit(solution)/shard_map/ppermute | solution.py:688
  11.4 2.5 %around_sum_kernel.3 = (f32[3,8,64,128]{3,2,1,0:T(8,128)}, f32[200,128]{1,0:T(8,128)}, f32[200,128]{1,0:T(8,128)}) custom-call(f32[3,8,64,128]{3,2,1,0:T(8,128)} %get-tuple-element.45.field, f32[3,8,128]{2,1,0:T(8,128)} %copy-done.16, f32[3,8,128]{2,1,0:T(8,128)} %copy-done.19, f32[16,256]{1,0:T(8,128)} %get-tuple-element.48.lanes), custom_call_target="tpu_custom_call" | custom-call | tf_op jit(solution)/shard_map/around_sum_kernel/pallas_call | solution.py:99
  13.8 1.3 collective-permute-start.2
  15.1 4.9 %collective-permute-start.3 = (f32[200,128]{1,0:T(8,128)}, f32[200,128]{1,0:T(8,128)S(1)}, u32[]{:S(2)}, u32[]{:S(2)}) collective-permute-start(f32[200,128]{1,0:T(8,128)} %get-tuple-element.51), channel_id=1, source_target_pairs={{8,0},{16,8},{24,16},{32,24},{40,32},{48,40},{56,48},{64,56},{72,6... | collective-permute-start | bytes 307208 | tf_op jit(solution)/shard_map/ppermute | solution.py:688
  20.0 3.3 %collective-permute-done.2.zlo = f32[200,128]{1,0:T(8,128)S(1)} collective-permute-done((f32[200,128]{1,0:T(8,128)}, f32[200,128]{1,0:T(8,128)S(1)}, u32[]{:S(2)}, u32[]{:S(2)}) %collective-permute-start.2) | collective-permute-done | bytes 102432 | tf_op jit(solution)/shard_map/ppermute | solution.py:688
  24.0 11.7 %project_kernel.1 = (f32[3,8,64,128]{3,2,1,0:T(8,128)}, f32[3,8,64,128]{3,2,1,0:T(8,128)}, f32[3,16,128]{2,1,0:T(8,128)}, f32[3,16,128]{2,1,0:T(8,128)}) custom-call(f32[3,8,64,128]{3,2,1,0:T(8,128)} %get-tuple-element.49.field, f32[200,128]{1,0:T(8,128)} %copy-done.4, f32[200,128]{1,0:T(8,128)} %copy-done.5, f32[16,256]{1,0:T(8,128)} %get-tuple-element.48.lanes, ...), custom_call_target="tpu_custom_call" | custom-call | tf_op jit(solution)/shard_map/project_kernel/pallas_call | solution.py:99
  35.8 0.7 collective-permute-start.5
  36.4 0.9 collective-permute-done.4.tlo
  37.3 1.9 collective-permute-done.5.thi
  39.9 2.5 %around_widen_kernel.2 = (f32[3,8,72,128]{3,2,1,0:T(8,128)}, f32[3,2,72,128]{3,2,1,0:T(8,128)}, f32[3,2,72,128]{3,2,1,0:T(8,128)}) custom-call(f32[3,8,64,128]{3,2,1,0:T(8,128)} %get-tuple-element.53.res, f32[3,16,128]{2,1,0:T(8,128)} %copy-done.10, f32[3,16,128]{2,1,0:T(8,128)} %copy-done.12), custom_call_target="tpu_custom_call" | custom-call | tf_op jit(solution)/shard_map/around_widen_kernel/pallas_call | solution.py:99
  42.4 5.6 %collective-permute-start.7 = (f32[3,2,72,128]{3,2,1,0:T(8,128)}, f32[3,2,72,128]{3,2,1,0:T(8,128)S(1)}, u32[]{:S(2)}, u32[]{:S(2)}) collective-permute-start(f32[3,2,72,128]{3,2,1,0:T(8,128)} %get-tuple-element.58), channel_id=1, source_target_pairs={{8,0},{16,8},{24,16},{32,24},{40,32},{48,40},{56,48},{64,56},{72,6... | collective-permute-start | bytes 663560 | tf_op jit(solution)/shard_map/ppermute | solution.py:688
  48.0 2.8 %solve_tables_kernel.1 = (bf16[112,480]{1,0:T(8,128)(2,1)}, bf16[64,336]{1,0:T(8,128)(2,1)}, f32[10,112,128]{2,1,0:T(8,128)}) custom-call(f32[10,10]{1,0:T(8,128)} %vectors.5, f32[1,10]{1,0:T(1,128)} %bitcast.22, f32[16,256]{1,0:T(8,128)} %get-tuple-element.48.lanes), custom_call_target="tpu_custom_call" | custom-call | tf_op jit(solution)/shard_map/solve_tables_kernel/pallas_call | solution.py:99
  50.9 1.8 collective-permute-done.6.zlo
  52.7 0.7 copy-done
  53.5 8.5 %solve_kernel.2 = (f32[3,8,64,128]{3,2,1,0:T(8,128)}, f32[3,8,128]{2,1,0:T(8,128)}, f32[3,8,128]{2,1,0:T(8,128)}) custom-call(f32[3,8,72,128]{3,2,1,0:T(8,128)} %get-tuple-element.56.field, f32[3,2,72,128]{3,2,1,0:T(8,128)} %copy-done, f32[3,2,72,128]{3,2,1,0:T(8,128)} %copy-done.2, f32[10,10]{1,0:T(8,128)} %vectors.5, ...), custom_call_target="tpu_custom_call" | custom-call | tf_op jit(solution)/shard_map/solve_kernel/pallas_call | solution.py:99
  62.0 0.7 collective-permute-start.8
  62.7 1.2 collective-permute-start.9
  63.9 0.9 collective-permute-done.8.tlo
  64.8 1.2 collective-permute-done.9.thi
  66.6 2.4 %around_sum_kernel.4 = (f32[3,8,64,128]{3,2,1,0:T(8,128)}, f32[200,128]{1,0:T(8,128)}, f32[200,128]{1,0:T(8,128)}) custom-call(f32[3,8,64,128]{3,2,1,0:T(8,128)} %get-tuple-element.62.field, f32[3,8,128]{2,1,0:T(8,128)} %copy-done.14, f32[3,8,128]{2,1,0:T(8,128)} %copy-done.17, f32[16,256]{1,0:T(8,128)} %get-tuple-element.48.lanes), custom_call_target="tpu_custom_call" | custom-call | tf_op jit(solution)/shard_map/around_sum_kernel/pallas_call | solution.py:99
  69.1 5.3 %collective-permute-start.11 = (f32[200,128]{1,0:T(8,128)}, f32[200,128]{1,0:T(8,128)S(1)}, u32[]{:S(2)}, u32[]{:S(2)}) collective-permute-start(f32[200,128]{1,0:T(8,128)} %get-tuple-element.67), channel_id=1, source_target_pairs={{8,0},{16,8},{24,16},{32,24},{40,32},{48,40},{56,48},{64,56},{72,6... | collective-permute-start | bytes 307208 | tf_op jit(solution)/shard_map/ppermute | solution.py:688
  74.3 2.3 %collective-permute-done.10.zlo = f32[200,128]{1,0:T(8,128)S(1)} collective-permute-done((f32[200,128]{1,0:T(8,128)}, f32[200,128]{1,0:T(8,128)S(1)}, u32[]{:S(2)}, u32[]{:S(2)}) %collective-permute-start.10) | collective-permute-done | bytes 102432 | tf_op jit(solution)/shard_map/ppermute | solution.py:688
  77.3 4.3 %direction_kernel.2 = (f32[3,8,64,128]{3,2,1,0:T(8,128)}, f32[128,128]{1,0:T(8,128)}) custom-call(f32[3,8,64,128]{3,2,1,0:T(8,128)} %get-tuple-element.65.field, f32[200,128]{1,0:T(8,128)} %copy-done.7, f32[200,128]{1,0:T(8,128)} %copy-done.9, f32[3,8,64,128]{3,2,1,0:T(8,128)} %get-tuple-element.53.res, f32[16,256]{1,0:T(8,128)} %get-tuple-element.48.lanes, ...), custom_call_target="tpu_custom_call" | custom-call | tf_op jit(solution)/shard_map/direction_kernel/pallas_call | solution.py:99
  81.6 20.1 %all_to_all.31 = f32[128,1,128]{2,1,0:T(1,128)} all-to-all(f32[128,1,128]{2,1,0:T(1,128)} %bitcast.19), channel_id=1, replica_groups=mesh['wide'=16,'narrow'=8] {'wide','narrow'}, dimensions={0} | all-to-all | bytes 131072 | tf_op jit(solution)/shard_map/all_to_all | solution.py:767
  101.7 12.3 %advance_kernel.1 = (f32[3,8,64,128]{3,2,1,0:T(8,128)}, f32[3,8,64,128]{3,2,1,0:T(8,128)}, f32[3,16,128]{2,1,0:T(8,128)}, f32[3,16,128]{2,1,0:T(8,128)}) custom-call(f32[3,8,64,128]{3,2,1,0:T(8,128)} %get-tuple-element.52.u_old, f32[3,8,64,128]{3,2,1,0:T(8,128)} %get-tuple-element.68.d, f32[128,128]{1,0:T(8,128)} %bitcast.16, ...), custom_call_target="tpu_custom_call" | custom-call | tf_op jit(solution)/shard_map/advance_kernel/pallas_call | solution.py:99
  114.0 1.2 collective-permute-start.12
  115.2 1.2 collective-permute-done.12.tlo
  116.4 2.6 %collective-permute-done.13.thi = f32[3,16,128]{2,1,0:T(8,128)S(1)} collective-permute-done((f32[3,16,128]{2,1,0:T(8,128)}, f32[3,16,128]{2,1,0:T(8,128)S(1)}, u32[]{:S(2)}, u32[]{:S(2)}) %collective-permute-start.13) | collective-permute-done | bytes 24608 | tf_op jit(solution)/shard_map/ppermute | solution.py:688
  119.6 2.5 %around_widen_kernel.3 = (f32[3,8,72,128]{3,2,1,0:T(8,128)}, f32[3,2,72,128]{3,2,1,0:T(8,128)}, f32[3,2,72,128]{3,2,1,0:T(8,128)}) custom-call(f32[3,8,64,128]{3,2,1,0:T(8,128)} %get-tuple-element.71.res, f32[3,16,128]{2,1,0:T(8,128)} %copy-done.11, f32[3,16,128]{2,1,0:T(8,128)} %copy-done.13), custom_call_target="tpu_custom_call" | custom-call | tf_op jit(solution)/shard_map/around_widen_kernel/pallas_call | solution.py:99
  122.1 4.7 %collective-permute-start.15 = (f32[3,2,72,128]{3,2,1,0:T(8,128)}, f32[3,2,72,128]{3,2,1,0:T(8,128)S(1)}, u32[]{:S(2)}, u32[]{:S(2)}) collective-permute-start(f32[3,2,72,128]{3,2,1,0:T(8,128)} %get-tuple-element.76), channel_id=1, source_target_pairs={{8,0},{16,8},{24,16},{32,24},{40,32},{48,40},{56,48},{64,56},{72,6... | collective-permute-start | bytes 663560 | tf_op jit(solution)/shard_map/ppermute | solution.py:688
  126.9 5.1 %collective-permute-done.14.zlo = f32[3,2,72,128]{3,2,1,0:T(8,128)S(1)} collective-permute-done((f32[3,2,72,128]{3,2,1,0:T(8,128)}, f32[3,2,72,128]{3,2,1,0:T(8,128)S(1)}, u32[]{:S(2)}, u32[]{:S(2)}) %collective-permute-start.14) | collective-permute-done | bytes 221216 | tf_op jit(solution)/shard_map/ppermute | solution.py:688
  132.0 0.7 copy-done.1
  132.8 8.5 %solve_kernel.3 = (f32[3,8,64,128]{3,2,1,0:T(8,128)}, f32[3,8,128]{2,1,0:T(8,128)}, f32[3,8,128]{2,1,0:T(8,128)}) custom-call(f32[3,8,72,128]{3,2,1,0:T(8,128)} %get-tuple-element.74.field, f32[3,2,72,128]{3,2,1,0:T(8,128)} %copy-done.1, f32[3,2,72,128]{3,2,1,0:T(8,128)} %copy-done.3, f32[10,10]{1,0:T(8,128)} %vectors.5, ...), custom_call_target="tpu_custom_call" | custom-call | tf_op jit(solution)/shard_map/solve_kernel/pallas_call | solution.py:99
  141.3 1.1 collective-permute-start.16
  142.8 0.9 collective-permute-done.16.tlo
  143.6 2.1 collective-permute-done.17.thi
  146.3 2.4 %around_sum_kernel.5 = (f32[3,8,64,128]{3,2,1,0:T(8,128)}, f32[200,128]{1,0:T(8,128)}, f32[200,128]{1,0:T(8,128)}) custom-call(f32[3,8,64,128]{3,2,1,0:T(8,128)} %get-tuple-element.77.field, f32[3,8,128]{2,1,0:T(8,128)} %copy-done.15, f32[3,8,128]{2,1,0:T(8,128)} %copy-done.18, f32[16,256]{1,0:T(8,128)} %get-tuple-element.48.lanes), custom_call_target="tpu_custom_call" | custom-call | tf_op jit(solution)/shard_map/around_sum_kernel/pallas_call | solution.py:99
  148.8 4.8 %collective-permute-start.19 = (f32[200,128]{1,0:T(8,128)}, f32[200,128]{1,0:T(8,128)S(1)}, u32[]{:S(2)}, u32[]{:S(2)}) collective-permute-start(f32[200,128]{1,0:T(8,128)} %get-tuple-element.82), channel_id=1, source_target_pairs={{8,0},{16,8},{24,16},{32,24},{40,32},{48,40},{56,48},{64,56},{72,6... | collective-permute-start | bytes 307208 | tf_op jit(solution)/shard_map/ppermute | solution.py:688
  153.6 2.3 %collective-permute-done.18.zlo = f32[200,128]{1,0:T(8,128)S(1)} collective-permute-done((f32[200,128]{1,0:T(8,128)}, f32[200,128]{1,0:T(8,128)S(1)}, u32[]{:S(2)}, u32[]{:S(2)}) %collective-permute-start.18) | collective-permute-done | bytes 102432 | tf_op jit(solution)/shard_map/ppermute | solution.py:688
  156.5 4.3 %direction_kernel.3 = (f32[3,8,64,128]{3,2,1,0:T(8,128)}, f32[128,128]{1,0:T(8,128)}) custom-call(f32[3,8,64,128]{3,2,1,0:T(8,128)} %get-tuple-element.80.field, f32[200,128]{1,0:T(8,128)} %copy-done.6, f32[200,128]{1,0:T(8,128)} %copy-done.8, f32[3,8,64,128]{3,2,1,0:T(8,128)} %get-tuple-element.71.res, f32[16,256]{1,0:T(8,128)} %get-tuple-element.48.lanes, ...), custom_call_target="tpu_custom_call" | custom-call | tf_op jit(solution)/shard_map/direction_kernel/pallas_call | solution.py:99
  160.8 19.9 %all_to_all.32 = f32[128,1,128]{2,1,0:T(1,128)} all-to-all(f32[128,1,128]{2,1,0:T(1,128)} %bitcast.18), channel_id=1, replica_groups=mesh['wide'=16,'narrow'=8] {'wide','narrow'}, dimensions={0} | all-to-all | bytes 131072 | tf_op jit(solution)/shard_map/all_to_all | solution.py:767
  180.7 17.3 %last_kernel.1 = (f32[3,8,64,128]{3,2,1,0:T(8,128)}, f32[128,408]{1,0:T(8,128)}) custom-call(f32[3,8,64,128]{3,2,1,0:T(8,128)} %get-tuple-element.70.u_old, f32[3,8,64,128]{3,2,1,0:T(8,128)} %get-tuple-element.83.d, f32[128,128]{1,0:T(8,128)} %bitcast.15, f32[16,256]{1,0:T(8,128)} %get-tuple-element.48.lanes, bf16[432,256]{1,0:T(8,128)(2,1)} %constant.12.clone.fine, ...), custom_call_target="tpu_custom_call" | custom-call | tf_op jit(solution)/shard_map/last_kernel/pallas_call | solution.py:99
  198.0 1.2 copy.17
  199.2 15.5 %all_to_all.33 = f32[128,1,408]{2,1,0:T(1,128)S(1)} all-to-all(f32[128,1,408]{2,1,0:T(1,128)S(1)} %copy.17), channel_id=1, replica_groups=mesh['wide'=16,'narrow'=8] {'wide','narrow'}, dimensions={0} | all-to-all | bytes 417792 | tf_op jit(solution)/shard_map/all_to_all | solution.py:774
  214.9 0.7 reshape.21
  (52 shorter events, 6.0 us)
Async XLA Ops:
  4.8 3.6 %collective-permute-start = (f32[3,8,128]{2,1,0:T(8,128)}, f32[3,8,128]{2,1,0:T(8,128)S(1)}, u32[]{:S(2)}, u32[]{:S(2)}) collective-permute-start(f32[3,8,128]{2,1,0:T(8,128)} %get-tuple-element.46), channel_id=1, source_target_pairs={{0,1},{1,2},{2,3},{3,4},{4,5},{5,6},{6,7},{7,0},{8,9},{9,10},{10,1... | collective-permute-start | bytes 36872 | tf_op jit(solution)/shard_map/ppermute | solution.py:688
  7.4 3.3 %collective-permute-start.1 = (f32[3,8,128]{2,1,0:T(8,128)}, f32[3,8,128]{2,1,0:T(8,128)S(1)}, u32[]{:S(2)}, u32[]{:S(2)}) collective-permute-start(f32[3,8,128]{2,1,0:T(8,128)} %get-tuple-element.47), channel_id=1, source_target_pairs={{1,0},{2,1},{3,2},{4,3},{5,4},{6,5},{7,6},{0,7},{9,8},{10,9},{11,1... | collective-permute-start | bytes 36872 | tf_op jit(solution)/shard_map/ppermute | solution.py:688
  8.5 2.3 %copy-start.16 = (f32[3,8,128]{2,1,0:T(8,128)}, f32[3,8,128]{2,1,0:T(8,128)S(1)}, u32[]{:S(2)}) copy-start(f32[3,8,128]{2,1,0:T(8,128)S(1)} %collective-permute-done.tlo) | copy-start | bytes 36868
  10.8 0.6 copy-start.19
  13.8 9.5 %collective-permute-start.2 = (f32[200,128]{1,0:T(8,128)}, f32[200,128]{1,0:T(8,128)S(1)}, u32[]{:S(2)}, u32[]{:S(2)}) collective-permute-start(f32[200,128]{1,0:T(8,128)} %get-tuple-element.50), channel_id=1, source_target_pairs={{0,8},{8,16},{16,24},{24,32},{32,40},{40,48},{48,56},{56,64},{64,7... | collective-permute-start | bytes 307208 | tf_op jit(solution)/shard_map/ppermute | solution.py:688
  15.1 8.2 %collective-permute-start.3 = (f32[200,128]{1,0:T(8,128)}, f32[200,128]{1,0:T(8,128)S(1)}, u32[]{:S(2)}, u32[]{:S(2)}) collective-permute-start(f32[200,128]{1,0:T(8,128)} %get-tuple-element.51), channel_id=1, source_target_pairs={{8,0},{16,8},{24,16},{32,24},{40,32},{48,40},{56,48},{64,56},{72,6... | collective-permute-start | bytes 307208 | tf_op jit(solution)/shard_map/ppermute | solution.py:688
  23.4 0.6 copy-start.4
  23.4 0.7 copy-start.5
  35.7 1.6 collective-permute-start.4
  35.8 3.5 %collective-permute-start.5 = (f32[3,16,128]{2,1,0:T(8,128)}, f32[3,16,128]{2,1,0:T(8,128)S(1)}, u32[]{:S(2)}, u32[]{:S(2)}) collective-permute-start(f32[3,16,128]{2,1,0:T(8,128)} %get-tuple-element.55), channel_id=1, source_target_pairs={{1,0},{2,1},{3,2},{4,3},{5,4},{6,5},{7,6},{0,7},{9,8},{10,9},{11,1... | collective-permute-start | bytes 73736 | tf_op jit(solution)/shard_map/ppermute | solution.py:688
  37.3 1.9 copy-start.10
  39.2 0.6 copy-start.12
  42.4 10.3 %collective-permute-start.6 = (f32[3,2,72,128]{3,2,1,0:T(8,128)}, f32[3,2,72,128]{3,2,1,0:T(8,128)S(1)}, u32[]{:S(2)}, u32[]{:S(2)}) collective-permute-start(f32[3,2,72,128]{3,2,1,0:T(8,128)} %get-tuple-element.57), channel_id=1, source_target_pairs={{0,8},{8,16},{16,24},{24,32},{32,40},{40,48},{48,56},{56,64},{64,7... | collective-permute-start | bytes 663560 | tf_op jit(solution)/shard_map/ppermute | solution.py:688
  42.4 10.3 %collective-permute-start.7 = (f32[3,2,72,128]{3,2,1,0:T(8,128)}, f32[3,2,72,128]{3,2,1,0:T(8,128)S(1)}, u32[]{:S(2)}, u32[]{:S(2)}) collective-permute-start(f32[3,2,72,128]{3,2,1,0:T(8,128)} %get-tuple-element.58), channel_id=1, source_target_pairs={{8,0},{16,8},{24,16},{32,24},{40,32},{48,40},{56,48},{64,56},{72,6... | collective-permute-start | bytes 663560 | tf_op jit(solution)/shard_map/ppermute | solution.py:688
  52.7 0.7 copy-start
  52.7 0.8 copy-start.2
  62.0 2.8 %collective-permute-start.8 = (f32[3,8,128]{2,1,0:T(8,128)}, f32[3,8,128]{2,1,0:T(8,128)S(1)}, u32[]{:S(2)}, u32[]{:S(2)}) collective-permute-start(f32[3,8,128]{2,1,0:T(8,128)} %get-tuple-element.63), channel_id=1, source_target_pairs={{0,1},{1,2},{2,3},{3,4},{4,5},{5,6},{6,7},{7,0},{8,9},{9,10},{10,1... | collective-permute-start | bytes 36872 | tf_op jit(solution)/shard_map/ppermute | solution.py:688
  62.7 3.3 %collective-permute-start.9 = (f32[3,8,128]{2,1,0:T(8,128)}, f32[3,8,128]{2,1,0:T(8,128)S(1)}, u32[]{:S(2)}, u32[]{:S(2)}) collective-permute-start(f32[3,8,128]{2,1,0:T(8,128)} %get-tuple-element.64), channel_id=1, source_target_pairs={{1,0},{2,1},{3,2},{4,3},{5,4},{6,5},{7,6},{0,7},{9,8},{10,9},{11,1... | collective-permute-start | bytes 36872 | tf_op jit(solution)/shard_map/ppermute | solution.py:688
  64.8 1.2 copy-start.14
  66.0 0.6 copy-start.17
  69.0 7.5 %collective-permute-start.10 = (f32[200,128]{1,0:T(8,128)}, f32[200,128]{1,0:T(8,128)S(1)}, u32[]{:S(2)}, u32[]{:S(2)}) collective-permute-start(f32[200,128]{1,0:T(8,128)} %get-tuple-element.66), channel_id=1, source_target_pairs={{0,8},{8,16},{16,24},{24,32},{32,40},{40,48},{48,56},{56,64},{64,7... | collective-permute-start | bytes 307208 | tf_op jit(solution)/shard_map/ppermute | solution.py:688
  69.1 7.6 %collective-permute-start.11 = (f32[200,128]{1,0:T(8,128)}, f32[200,128]{1,0:T(8,128)S(1)}, u32[]{:S(2)}, u32[]{:S(2)}) collective-permute-start(f32[200,128]{1,0:T(8,128)} %get-tuple-element.67), channel_id=1, source_target_pairs={{8,0},{16,8},{24,16},{32,24},{40,32},{48,40},{56,48},{64,56},{72,6... | collective-permute-start | bytes 307208 | tf_op jit(solution)/shard_map/ppermute | solution.py:688
  76.6 0.6 copy-start.7
  76.6 0.7 copy-start.9
  114.0 2.4 %collective-permute-start.12 = (f32[3,16,128]{2,1,0:T(8,128)}, f32[3,16,128]{2,1,0:T(8,128)S(1)}, u32[]{:S(2)}, u32[]{:S(2)}) collective-permute-start(f32[3,16,128]{2,1,0:T(8,128)} %get-tuple-element.72), channel_id=1, source_target_pairs={{0,1},{1,2},{2,3},{3,4},{4,5},{5,6},{6,7},{7,0},{8,9},{9,10},{10,1... | collective-permute-start | bytes 73736 | tf_op jit(solution)/shard_map/ppermute | solution.py:688
  115.2 3.8 %collective-permute-start.13 = (f32[3,16,128]{2,1,0:T(8,128)}, f32[3,16,128]{2,1,0:T(8,128)S(1)}, u32[]{:S(2)}, u32[]{:S(2)}) collective-permute-start(f32[3,16,128]{2,1,0:T(8,128)} %get-tuple-element.73), channel_id=1, source_target_pairs={{1,0},{2,1},{3,2},{4,3},{5,4},{6,5},{7,6},{0,7},{9,8},{10,9},{11,1... | collective-permute-start | bytes 73736 | tf_op jit(solution)/shard_map/ppermute | solution.py:688
  116.4 2.6 %copy-start.11 = (f32[3,16,128]{2,1,0:T(8,128)}, f32[3,16,128]{2,1,0:T(8,128)S(1)}, u32[]{:S(2)}) copy-start(f32[3,16,128]{2,1,0:T(8,128)S(1)} %collective-permute-done.12.tlo) | copy-start | bytes 73732
  119.0 0.6 copy-start.13
  122.1 9.9 %collective-permute-start.14 = (f32[3,2,72,128]{3,2,1,0:T(8,128)}, f32[3,2,72,128]{3,2,1,0:T(8,128)S(1)}, u32[]{:S(2)}, u32[]{:S(2)}) collective-permute-start(f32[3,2,72,128]{3,2,1,0:T(8,128)} %get-tuple-element.75), channel_id=1, source_target_pairs={{0,8},{8,16},{16,24},{24,32},{32,40},{40,48},{48,56},{56,64},{64,7... | collective-permute-start | bytes 663560 | tf_op jit(solution)/shard_map/ppermute | solution.py:688
  122.1 9.8 %collective-permute-start.15 = (f32[3,2,72,128]{3,2,1,0:T(8,128)}, f32[3,2,72,128]{3,2,1,0:T(8,128)S(1)}, u32[]{:S(2)}, u32[]{:S(2)}) collective-permute-start(f32[3,2,72,128]{3,2,1,0:T(8,128)} %get-tuple-element.76), channel_id=1, source_target_pairs={{8,0},{16,8},{24,16},{32,24},{40,32},{48,40},{56,48},{64,56},{72,6... | collective-permute-start | bytes 663560 | tf_op jit(solution)/shard_map/ppermute | solution.py:688
  132.0 0.7 copy-start.1
  132.0 0.8 copy-start.3
  141.3 2.4 %collective-permute-start.16 = (f32[3,8,128]{2,1,0:T(8,128)}, f32[3,8,128]{2,1,0:T(8,128)S(1)}, u32[]{:S(2)}, u32[]{:S(2)}) collective-permute-start(f32[3,8,128]{2,1,0:T(8,128)} %get-tuple-element.78), channel_id=1, source_target_pairs={{0,1},{1,2},{2,3},{3,4},{4,5},{5,6},{6,7},{7,0},{8,9},{9,10},{10,1... | collective-permute-start | bytes 36872 | tf_op jit(solution)/shard_map/ppermute | solution.py:688
  142.4 3.3 %collective-permute-start.17 = (f32[3,8,128]{2,1,0:T(8,128)}, f32[3,8,128]{2,1,0:T(8,128)S(1)}, u32[]{:S(2)}, u32[]{:S(2)}) collective-permute-start(f32[3,8,128]{2,1,0:T(8,128)} %get-tuple-element.79), channel_id=1, source_target_pairs={{1,0},{2,1},{3,2},{4,3},{5,4},{6,5},{7,6},{0,7},{9,8},{10,9},{11,1... | collective-permute-start | bytes 36872 | tf_op jit(solution)/shard_map/ppermute | solution.py:688
  143.6 2.1 copy-start.15
  145.7 0.6 copy-start.18
  148.8 7.0 %collective-permute-start.18 = (f32[200,128]{1,0:T(8,128)}, f32[200,128]{1,0:T(8,128)S(1)}, u32[]{:S(2)}, u32[]{:S(2)}) collective-permute-start(f32[200,128]{1,0:T(8,128)} %get-tuple-element.81), channel_id=1, source_target_pairs={{0,8},{8,16},{16,24},{24,32},{32,40},{40,48},{48,56},{56,64},{64,7... | collective-permute-start | bytes 307208 | tf_op jit(solution)/shard_map/ppermute | solution.py:688
  148.8 7.0 %collective-permute-start.19 = (f32[200,128]{1,0:T(8,128)}, f32[200,128]{1,0:T(8,128)S(1)}, u32[]{:S(2)}, u32[]{:S(2)}) collective-permute-start(f32[200,128]{1,0:T(8,128)} %get-tuple-element.82), channel_id=1, source_target_pairs={{8,0},{16,8},{24,16},{32,24},{40,32},{48,40},{56,48},{64,56},{72,6... | collective-permute-start | bytes 307208 | tf_op jit(solution)/shard_map/ppermute | solution.py:688
  155.8 0.6 copy-start.6
  155.8 0.7 copy-start.8

commit v2 on v1

--- a/solution.py
+++ b/solution.py
@@ -94,17 +94,24 @@
 GRAD_JK = four_terms(np.concatenate([np.kron(D, np.eye(8)), np.kron(np.eye(8), D)]))
 
 
-def call(kernel, outs, args, scratch=(), spaces=None):
+def call(kernel, outs, args, scratch=(), spaces=None, hbm_out=()):
     spaces = spaces or {}
+    args = [
+        pltpu.with_memory_space_constraint(a, spaces.get(i, pltpu.VMEM))
+        for i, a in enumerate(args)
+    ]
     return pl.pallas_call(
         kernel,
-        out_shape=[jax.ShapeDtypeStruct(s, d) for s, d in outs],
+        out_shape=[
+            jax.ShapeDtypeStruct(s, d) if i in hbm_out else pltpu.VMEM(s, d)
+            for i, (s, d) in enumerate(outs)
+        ],
         in_specs=[
             pl.BlockSpec(memory_space=spaces.get(i, pltpu.VMEM)) for i in range(len(args))
         ],
         out_specs=[pl.BlockSpec(memory_space=pltpu.VMEM) for _ in outs],
         scratch_shapes=list(scratch),
-        compiler_params=pltpu.CompilerParams(vmem_limit_bytes=56 << 20),
+        compiler_params=pltpu.CompilerParams(vmem_limit_bytes=32 << 20),
         name=kernel.func.__name__ if isinstance(kernel, partial) else kernel.__name__,
     )(*args)
 
@@ -193,7 +200,7 @@
     return jnp.where(lane >= 112, lanes_by(packed, 112 - 16 * i), lanes_by(plane, -16))
 
 
-def start_kernel(vel, slot, corner, arc, rad, axial, mv, low, high, lanes, place):
+def start_kernel(vel, slot, arc, rad, axial, mv, low, high, lanes):
     ht = jnp.broadcast_to(arc[...], (8, 16))
     hr = jnp.broadcast_to(rad[...], (8, 16))
     spread = ((iota((16, 256), 1) & 15) == iota((16, 256), 0)).astype(F32)
@@ -234,10 +241,6 @@
         return carry
 
     lax.fori_loop(0, 3, body, 0)
-    ids = lax.dot_general(
-        corner[...].astype(F32), hot, nt, precision=EXACT, preferred_element_type=F32
-    )
-    place[...] = (ids + 0.5).astype(jnp.int32)
 
 
 def solve_tables_kernel(vectors, values, lanes, forward, inverse, scale):
@@ -333,14 +336,15 @@
     lax.fori_loop(0, 3, body, 0)
 
 
-def residual(u, lanes, fine, back, stiff, wjk, res, xu, xw, xs, pf, qf, xc, yf, sz, ks):
-    def put(ref, at, rb, half, x):
-        hi, lo = split(x)
-        for term, part in enumerate((hi, hi, lo, lo)):
-            ref[at, pl.ds(pl.multiple_of(term * 64 + rb * 16, 16), 16),
-                half * 128 : half * 128 + 128] = part
-
-    def first(t, carry):
+def put(ref, at, rb, half, x):
+    hi, lo = split(x)
+    for term, part in enumerate((hi, hi, lo, lo)):
+        rows = pl.ds(pl.multiple_of(term * 64 + rb * 16, 16), 16)
+        ref[at, rows, half * 128 : half * 128 + 128] = part
+
+
+def along_pipe(u, xu, xw, xs=None, sz=None):
+    def body(t, carry):
         c, rb = t // 4, t % 4
         rows = pl.ds(pl.multiple_of(rb * 16, 16), 16)
         x = [u[c, i, rows] for i in range(8)]
@@ -348,65 +352,136 @@
             put(xu, c * 6 + a // 2, rb, a % 2, val)
         for a, val in enumerate(even_odd(B, x, -1)):
             put(xw, c * 6 + a // 2, rb, a % 2, val)
+        if xs is None:
+            return carry
         for i in range(8):
             put(xs, c * 4 + i // 2, rb, i % 2, x[i])
         for i, val in enumerate(even_odd(STIFF, x, 1)):
             sz[c, i, rows] = val
         return carry
 
-    lax.fori_loop(0, 12, first, 0)
-
-    def second(p, carry):
-        for c in range(3):
-            pf[c] = dot(fine[...], xu[c * 6 + p])
-            qf[c] = dot(fine[0:144], xw[c * 6 + p])
-        lz, lt, lr = lanes[1:2], lanes[2:3], lanes[3:4]
+    lax.fori_loop(0, 12, body, 0)
+
+
+def fine_dots(p, at, fine, xu, xw, pf, qf):
+    for c in range(3):
+        pf[at, c] = dot(fine[...], xu[c * 6 + p])
+        qf[at, c] = dot(fine[0:144], xw[c * 6 + p])
+
+
+def stiff_dots(p, stiff, xs, ks):
+    for t in (2 * p, 2 * p + 1):
+        y = dot(stiff[...], xs[t])
+        c, q = t // 4, t % 4
+        ks[c, 2 * q] = y[:, :128]
+        ks[c, 2 * q + 1] = y[:, 128:]
+
+
+def put_conv(xc, c, r, conv):
+    hi, lo = split(conv)
+    xc[c, 16 * r : 16 * r + 16] = hi
+    xc[c, 144 + 16 * r : 160 + 16 * r] = hi
+    xc[c, 288 + 16 * r : 304 + 16 * r] = lo
+
+
+def back_dots(p, back, xc, yf, count):
+    for c in range(count):
+        y = dot(back[...], xc[c])
+        yf[c, 2 * p] = y[:, :128]
+        yf[c, 2 * p + 1] = y[:, 128:]
+
+
+def fine_rows(pf, qf, p, c, r):
+    rows = slice(16 * r, 16 * r + 16)
+    return (
+        qf[p, c, rows],
+        pf[p, c, 144 + 16 * r : 160 + 16 * r],
+        pf[p, c, 288 + 16 * r : 304 + 16 * r],
+    )
+
+
+def velocity_rows(pf, lanes, p, r):
+    rows = slice(16 * r, 16 * r + 16)
+    return [pf[p, n, rows] * lanes[n + 1 : n + 2] for n in range(3)]
+
+
+def stiff_plane(lanes, wjk, sz, ks, c, i, rb):
+    rows = pl.ds(pl.multiple_of(rb * 16, 16), 16)
+    more = pl.ds(pl.multiple_of(64 + rb * 16, 16), 16)
+    kz, kt, kr = lanes[4:5, :128], lanes[5:6, :128], lanes[6:7, :128]
+    plane = kt * ks[c, i, rows] + kr * ks[c, i, more]
+    return wjk[rows] * kz * sz[c, i, rows] + float(W[i]) * plane
+
+
+def residual(u, lanes, fine, back, stiff, wjk, res, pf, qf, xu, xw, xs, xc0, xc1, yf, sz, ks):
+    along_pipe(u, xu, xw, xs, sz)
+    fine_dots(0, 0, fine, xu, xw, pf, qf)
+    for p in range(6):
+        if p < 5:
+            fine_dots(p + 1, (p + 1) % 2, fine, xu, xw, pf, qf)
+        stiff_dots(p, stiff, xs, ks)
+        xc = (xc0, xc1)[p % 2]
         for r in range(9):
-            rows = slice(16 * r, 16 * r + 16)
-            vz = pf[0, rows] * lz
-            vt = pf[1, rows] * lt
-            vr = pf[2, rows] * lr
+            v = velocity_rows(pf, lanes, p % 2, r)
             for c in range(3):
-                conv = (
-                    vz * qf[c, rows]
-                    + vt * pf[c, 144 + 16 * r : 160 + 16 * r]
-                    + vr * pf[c, 288 + 16 * r : 304 + 16 * r]
-                )
-                hi, lo = split(conv)
-                xc[c, rows] = hi
-                xc[c, 144 + 16 * r : 160 + 16 * r] = hi
-                xc[c, 288 + 16 * r : 304 + 16 * r] = lo
-        for c in range(3):
-            y = dot(back[...], xc[c])
-            yf[c, 2 * p] = y[:, :128]
-            yf[c, 2 * p + 1] = y[:, 128:]
-        return carry
-
-    lax.fori_loop(0, 6, second, 0)
-
-    def third(t, carry):
-        y = dot(stiff[...], xs[t])
-        c, p = t // 4, t % 4
-        ks[c, 2 * p] = y[:, :128]
-        ks[c, 2 * p + 1] = y[:, 128:]
-        return carry
-
-    lax.fori_loop(0, 12, third, 0)
-    kz, kt, kr = lanes[4:5, :128], lanes[5:6, :128], lanes[6:7, :128]
+                g = fine_rows(pf, qf, p % 2, c, r)
+                put_conv(xc, c, r, v[0] * g[0] + v[1] * g[1] + v[2] * g[2])
+        back_dots(p, back, xc, yf, 3)
     keep = keep_rows(16)
 
-    def fourth(t, carry):
+    def body(t, carry):
         c, rb = t // 4, t % 4
         rows = pl.ds(pl.multiple_of(rb * 16, 16), 16)
-        more = pl.ds(pl.multiple_of(64 + rb * 16, 16), 16)
         adv = even_odd(JV, [yf[c, a, rows] for a in range(12)], 1)
-        wz = wjk[rows] * kz
         for i in range(8):
-            plane = float(W[i]) * (kt * ks[c, i, rows] + kr * ks[c, i, more])
-            res[c, i, rows] = -(adv[i] + wz * sz[c, i, rows] + plane) * keep
-        return carry
-
-    lax.fori_loop(0, 12, fourth, 0)
+            res[c, i, rows] = -(adv[i] + stiff_plane(lanes, wjk, sz, ks, c, i, rb)) * keep
+        return carry
+
+    lax.fori_loop(0, 12, body, 0)
+
+
+def change_kernel(
+    u, d, lanes, fine, back, stiff, wjk, lin, quad, pf, qf, xu, xw, pd, qd, xd, xe, xs,
+    xc0, xc1, yf, sz, ks
+):
+    along_pipe(u, xu, xw)
+    along_pipe(d, xd, xe, xs, sz)
+    fine_dots(0, 0, fine, xu, xw, pf, qf)
+    fine_dots(0, 0, fine, xd, xe, pd, qd)
+    for p in range(6):
+        if p < 5:
+            fine_dots(p + 1, (p + 1) % 2, fine, xu, xw, pf, qf)
+            fine_dots(p + 1, (p + 1) % 2, fine, xd, xe, pd, qd)
+        stiff_dots(p, stiff, xs, ks)
+        xc = (xc0, xc1)[p % 2]
+        for r in range(9):
+            v = velocity_rows(pf, lanes, p % 2, r)
+            w = velocity_rows(pd, lanes, p % 2, r)
+            for c in range(3):
+                g = fine_rows(pf, qf, p % 2, c, r)
+                h = fine_rows(pd, qd, p % 2, c, r)
+                put_conv(
+                    xc,
+                    c,
+                    r,
+                    (v[0] * h[0] + v[1] * h[1] + v[2] * h[2])
+                    + (w[0] * g[0] + w[1] * g[1] + w[2] * g[2]),
+                )
+                put_conv(xc, 3 + c, r, w[0] * h[0] + w[1] * h[1] + w[2] * h[2])
+        back_dots(p, back, xc, yf, 6)
+    keep = keep_rows(16)
+
+    def body(t, carry):
+        c, rb = t // 4, t % 4
+        rows = pl.ds(pl.multiple_of(rb * 16, 16), 16)
+        one = even_odd(JV, [yf[c, a, rows] for a in range(12)], 1)
+        two = even_odd(JV, [yf[3 + c, a, rows] for a in range(12)], 1)
+        for i in range(8):
+            lin[c, i, rows] = -(one[i] + stiff_plane(lanes, wjk, sz, ks, c, i, rb)) * keep
+            quad[c, i, rows] = -two[i] * keep
+        return carry
+
+    lax.fori_loop(0, 12, body, 0)
 
 
 def pack_two(res, low, high):
@@ -450,7 +525,7 @@
     return total[:, 0:1] / total[:, 1:2]
 
 
-def advance(u_old, d, sums, u):
+def advance_kernel(u_old, d, sums, lanes, fine, back, stiff, wjk, u, res, low, high, *scratch):
     alpha = step_length(sums)
 
     def body(t, carry):
@@ -459,12 +534,6 @@
         return carry
 
     lax.fori_loop(0, 24, body, 0)
-
-
-def advance_kernel(
-    u_old, d, sums, lanes, fine, back, stiff, wjk, u, res, low, high, *scratch
-):
-    advance(u_old, d, sums, u)
     residual(u, lanes, fine, back, stiff, wjk, res, *scratch)
     pack_two(res, low, high)
 
@@ -491,46 +560,49 @@
     lax.fori_loop(0, 3, body, 0)
 
 
+def widen_planes(e, xf, half):
+    lane, k = iota((8, 128), 1), iota((8, 128), 0)
+    extra = e[64:72]
+    planes = [e[8 * j : 8 * j + 8] for j in range(8)]
+    under = jnp.where(lane < 16, extra, lanes_by(planes[6], 16))
+    over = jnp.where(lane >= 112, extra, lanes_by(planes[1], -16))
+    cols = slice(half * 128, half * 128 + 128)
+    for j, v in enumerate([under] + planes + [over]):
+        below, above = radial_parts(v)
+        own = radial_sum(v, below, above)
+        side = jnp.where(k == 0, rows_by(below, 2), jnp.where(k == 1, above, 0.0))
+        hi, lo = split(jnp.concatenate([own, side], axis=0))
+        xf[16 * j : 16 * j + 16, cols] = hi
+        xf[160 + 16 * j : 176 + 16 * j, cols] = hi
+        xf[320 + 16 * j : 336 + 16 * j, cols] = lo
+
+
+def transform_kernel(field, forward, out, *xf):
+    def body(c, carry):
+        for p in range(4):
+            buf = xf[p % 2]
+            for half in range(2):
+                widen_planes(field[c, 2 * p + half], buf, half)
+            y = dot(forward[...], buf[...])
+            out[c, 2 * p] = y[:, :128]
+            out[c, 2 * p + 1] = y[:, 128:]
+        return carry
+
+    lax.fori_loop(0, 3, body, 0)
+
+
 def solve_kernel(
-    field, zlo, zhi, vectors, forward, inverse, scale, corr, low, high, xf, yf, xb
+    own, zlo, zhi, vectors, forward, inverse, scale, corr, low, high, xf0, xf1, yf, xb
 ):
-    lane = iota((8, 128), 1)
-    k = iota((8, 128), 0)
-    r = lane & (RADIAL - 1)
-
-    def widen(c, p):
-        for half in range(2):
-            n = 2 * p + half
-            if n == 0:
-                e = zlo[c, 0]
-            elif n == 1:
-                e = field[c, 0] + zlo[c, 1]
-            elif n == 8:
-                e = field[c, 7] + zhi[c, 0]
-            elif n == 9:
-                e = zhi[c, 1]
-            else:
-                e = field[c, n - 1]
-            extra = e[64:72]
-            planes = [e[8 * j : 8 * j + 8] for j in range(8)]
-            under = jnp.where(lane < 16, extra, lanes_by(planes[6], 16))
-            over = jnp.where(lane >= 112, extra, lanes_by(planes[1], -16))
-            for j, v in enumerate([under] + planes + [over]):
-                below, above = radial_parts(v)
-                own = radial_sum(v, below, above)
-                side = jnp.where(k == 0, rows_by(below, 2), jnp.where(k == 1, above, 0.0))
-                hi, lo = split(jnp.concatenate([own, side], axis=0))
-                cols = slice(half * 128, half * 128 + 128)
-                xf[16 * j : 16 * j + 16, cols] = hi
-                xf[160 + 16 * j : 176 + 16 * j, cols] = hi
-                xf[320 + 16 * j : 336 + 16 * j, cols] = lo
-
     def body(c, carry):
-        for p in range(5):
-            widen(c, p)
-            y = dot(forward[...], xf[...])
-            yf[c, 2 * p] = y[:, :128]
-            yf[c, 2 * p + 1] = y[:, 128:]
+        for buf, halo, at in ((xf0, zlo, 0), (xf1, zhi, 8)):
+            widen_planes(halo[c, 0], buf, 0)
+            widen_planes(halo[c, 1], buf, 1)
+        y0, y1 = dot(forward[...], xf0[...]), dot(forward[...], xf1[...])
+        yf[c, 0] = y0[:, :128]
+        yf[c, 1] = y0[:, 128:] + own[c, 0]
+        yf[c, 2] = y1[:, :128] + own[c, 7]
+        yf[c, 3] = y1[:, 128:]
         return carry
 
     lax.fori_loop(0, 3, body, 0)
@@ -538,7 +610,11 @@
     def mid(t, carry):
         c, rb = t // 7, t % 7
         rows = pl.ds(pl.multiple_of(rb * 16, 16), 16)
-        y = [yf[c, i, rows] for i in range(10)]
+        y = (
+            [yf[c, 0, rows], yf[c, 1, rows]]
+            + [own[c, i, rows] for i in range(1, 7)]
+            + [yf[c, 2, rows], yf[c, 3, rows]]
+        )
         spec = []
         for a in range(10):
             acc = vectors[0, a] * y[0]
@@ -558,19 +634,22 @@
 
     lax.fori_loop(0, 21, mid, 0)
 
+    k = iota((8, 128), 0)
+    r = iota((8, 128), 1) & (RADIAL - 1)
     inner = ((k == 0) & (r > 0)) | ((k == 7) & (r < RADIAL - 1))
     share = jnp.where(inner, 0.5, 1.0).astype(F32)
+    for t in range(12):
+        c, p = t // 4, t % 4
+        y = dot(inverse[...], xb[t])
+        for half in range(2):
+            i = 2 * p + half
+            for j in range(8):
+                f = (0.5 if i in (0, 7) else 1.0) * (0.5 if j in (0, 7) else 1.0)
+                corr[c, i, 8 * j : 8 * j + 8] = (
+                    y[8 * j : 8 * j + 8, half * 128 : half * 128 + 128] * (share * f)
+                )
 
     def last(c, carry):
-        for p in range(4):
-            y = dot(inverse[...], xb[c * 4 + p])
-            for half in range(2):
-                i = 2 * p + half
-                for j in range(8):
-                    f = (0.5 if i in (0, 7) else 1.0) * (0.5 if j in (0, 7) else 1.0)
-                    corr[c, i, 8 * j : 8 * j + 8] = (
-                        y[8 * j : 8 * j + 8, half * 128 : half * 128 + 128] * (share * f)
-                    )
         low[c] = pack_low(lambda i: corr[c, i, 0:8])
         high[c] = pack_high(lambda i: corr[c, i, 56:64])
         return carry
@@ -627,55 +706,93 @@
     sums[...] = jnp.where(at == 0, num, jnp.where(at == 1, den, 0.0))
 
 
-def last_kernel(
-    u_old, d, sums, lanes, fine, back, stiff, wjk, slot, place, vel, dense, u, res, *scratch
-):
-    advance(u_old, d, sums, u)
-    residual(u, lanes, fine, back, stiff, wjk, res, *scratch)
+def route_kernel(slot, corner, inside, owner):
     hot = (slot[...] == iota((128, 128), 0)).astype(F32)
     nt = (((1,), (1,)), ((), ()))
+    ids = corner[...].astype(F32)
+    by_elem = lax.dot_general(hot, ids, nt, precision=EXACT, preferred_element_type=F32)
+    by_corner = lax.dot_general(ids, hot, nt, precision=EXACT, preferred_element_type=F32)
+    owner[...] = (by_corner + 0.5).astype(jnp.int32) // 136
+    ids = (by_elem + 0.5).astype(jnp.int32)
+    inside[...] = ids - ids // 136 * 136
+
+
+def route_corners_kernel(res, lin, quad, inside, owner, part, dense, left, right):
     row, col = iota((8, 64), 0), iota((8, 64), 1)
 
     def weight(node, upper):
-        out = jnp.zeros((8, 64), F32)
+        acc = jnp.zeros((8, 64), F32)
         for n in range(8):
-            out = jnp.where(
-                node == n, jnp.where(upper, float(LIN[1, n]), float(LIN[0, n])), out
+            acc = jnp.where(
+                node == n, jnp.where(upper, float(LIN[1, n]), float(LIN[0, n])), acc
             )
-        return out
+        return acc
 
     corner_jk = weight(col >> 3, (row & 2) != 0) * weight(col & 7, (row & 1) != 0)
-    owner = place[...] // 136
-    place_in = place[...] - owner * 136
-    dev = iota((128, 128), 0)
-    dense[...] = jnp.zeros_like(dense)
+    pos, dev = iota((128, 256), 1), iota((128, 128), 0)
+    for q in range(8):
+        right[128 * q : 128 * q + 128] = (inside[:, q : q + 1] == pos).astype(F32).astype(BF16)
+    for n, ref in enumerate((res, lin, quad)):
+        for c in range(3):
+            planes = [ref[c, i] for i in range(8)]
+            z1 = sum(float(LIN[1, i]) * planes[i] for i in range(1, 8))
+            z0 = sum(float(LIN[0, i]) * planes[i] for i in range(7))
+            both = jnp.dot(
+                corner_jk,
+                jnp.concatenate([z0, z1], axis=1),
+                precision=EXACT,
+                preferred_element_type=F32,
+            )
+            hi = both.astype(BF16).astype(F32)
+            mid = (both - hi).astype(BF16).astype(F32)
+            for q in range(8):
+                mine = owner[q : q + 1] == dev
+                cols = slice((q // 4) * 128, (q // 4) * 128 + 128)
+                for m, piece in enumerate((hi, mid, both - hi - mid)):
+                    at = (3 * c + m) * 128
+                    left[at : at + 128, 128 * q : 128 * q + 128] = jnp.where(
+                        mine, piece[q % 4 : q % 4 + 1, cols], 0.0
+                    ).astype(BF16)
+        y = dot(left[...], right[...])
+        for c in range(3):
+            block = 3 * n + c
+            total = (
+                y[384 * c : 384 * c + 128]
+                + y[384 * c + 128 : 384 * c + 256]
+                + y[384 * c + 256 : 384 * c + 384]
+            )
+            total = lanes_by(total, 8 * block)
+            first = slice(128 * block, 128 * block + 128)
+            dense[:, first] = total[:, :128] if block == 0 else dense[:, first] + total[:, :128]
+            dense[:, 128 * block + 128 : 128 * block + 256] = total[:, 128:]
+    dense[:, 1152:1280] += lanes_by(part[...], 72)
+
+
+def store_kernel(u, d, slot, u_out, d_out):
+    hot = (slot[...] == iota((128, 128), 0)).astype(F32)
 
     def body(c, carry):
-        flat = u[c].reshape(512, 128)
-        vel[c] = jnp.dot(flat, hot, precision=EXACT, preferred_element_type=F32).reshape(
-            8, 64, 128
-        )
-        planes = [res[c, i] for i in range(8)]
-        z1 = sum(float(LIN[1, i]) * planes[i] for i in range(1, 8))
-        z0 = sum(float(LIN[0, i]) * planes[i] for i in range(7))
-        s0 = jnp.dot(corner_jk, z0, precision=EXACT, preferred_element_type=F32)
-        s1 = jnp.dot(corner_jk, z1, precision=EXACT, preferred_element_type=F32)
-        left, right = [], []
-        pos = iota((408, 128), 0)
-        for q in range(8):
-            val = (s1 if q >= 4 else s0)[q % 4 : q % 4 + 1]
-            left.append(jnp.where(owner[q : q + 1] == dev, val, 0.0))
-            right.append((place_in[q : q + 1] + c * 136 == pos).astype(F32))
-        dense[...] += lax.dot_general(
-            jnp.concatenate(left, axis=1),
-            jnp.concatenate(right, axis=1),
-            nt,
-            precision=EXACT,
-            preferred_element_type=F32,
-        )
+        for x, y in ((u, u_out), (d, d_out)):
+            flat = x[c].reshape(512, 128)
+            y[c] = jnp.dot(flat, hot, precision=EXACT, preferred_element_type=F32).reshape(
+                8, 64, 128
+            )
         return carry
 
     lax.fori_loop(0, 3, body, 0)
+
+
+def end_kernel(u, d, total, vel, coarse):
+    alpha = total[0:1, 1224:1225] / total[0:1, 1225:1226]
+    one, two = lanes_by(total[...], -408), lanes_by(total[...], -816)
+    coarse[...] = (total[...] + alpha * (one + alpha * two))[0:1, 0:512]
+
+    def body(t, carry):
+        c, i = t // 8, t % 8
+        vel[c, i] = u[c, i] + alpha * d[c, i]
+        return carry
+
+    lax.fori_loop(0, 24, body, 0)
 
 
 FIELD = (3, 8, 64, 128)
@@ -688,15 +805,21 @@
     return lax.ppermute(to_next, axis, up), lax.ppermute(to_prev, axis, down)
 
 
-def residual_scratch():
+def fine_scratch():
     return [
+        pltpu.VMEM((2, 3, 432, 256), F32),
+        pltpu.VMEM((2, 3, 144, 256), F32),
         pltpu.VMEM((18, 256, 256), BF16),
         pltpu.VMEM((18, 256, 256), BF16),
+    ]
+
+
+def local_scratch(count):
+    return [
         pltpu.VMEM((12, 256, 256), BF16),
-        pltpu.VMEM((3, 432, 256), F32),
-        pltpu.VMEM((3, 144, 256), F32),
-        pltpu.VMEM((3, 432, 256), BF16),
-        pltpu.VMEM((3, 12, 64, 128), F32),
+        pltpu.VMEM((count, 432, 256), BF16),
+        pltpu.VMEM((count, 432, 256), BF16),
+        pltpu.VMEM((count, 12, 64, 128), F32),
         pltpu.VMEM(FIELD, F32),
         pltpu.VMEM((3, 8, 128, 128), F32),
     ]
@@ -706,12 +829,17 @@
     fine, back, stiff, grad = (jnp.asarray(m) for m in (FINE, BACK, STIFF_JK, GRAD_JK))
     wjk = jnp.asarray(np.broadcast_to(WJK[:, None], (64, 128)).astype(np.float32))
     smem = pltpu.SMEM
-    mv, low, high, lanes, place = call(
+    small = ((3, 8, 128), F32)
+    mv, low, high, lanes = call(
         start_kernel,
-        [(FIELD, F32), ((3, 8, 128), F32), ((3, 8, 128), F32), ((16, 256), F32),
-         ((8, 128), jnp.int32)],
-        (vel.reshape(FIELD), slot, corner, arc[None], rad[None], axial),
-        spaces={5: smem},
+        [(FIELD, F32), small, small, ((16, 256), F32)],
+        (vel.reshape(FIELD), slot, arc[None], rad[None], axial),
+        spaces={4: smem},
+    )
+    inside, owner = call(
+        route_kernel,
+        [((128, 8), jnp.int32), ((8, 128), jnp.int32)],
+        (slot, corner),
     )
     forward, inverse, scale = call(
         solve_tables_kernel,
@@ -729,16 +857,20 @@
         zlo, zhi = both_ways("wide", up, down)
         return out, zlo, zhi
 
+    fine, back, stiff, wjk, grad, mv = lax.optimization_barrier((fine, back, stiff, wjk, grad, mv))
     local = (lanes, fine, back, stiff, wjk)
     packs = [(FIELD, F32), (FIELD, F32), ((3, 16, 128), F32), ((3, 16, 128), F32)]
     u, res, low, high = call(
-        project_kernel, packs, (*sum_rounds(mv, low, high), *local), residual_scratch()
-    )
-    sums = None
+        project_kernel,
+        packs,
+        (*sum_rounds(mv, low, high), *local),
+        fine_scratch() + local_scratch(3),
+    )
     for step in range(2):
         if step > 0:
+            sums = lax.all_to_all(part, BOTH, 0, 0, tiled=True)
             u, res, low, high = call(
-                advance_kernel, packs, (u, d, sums, *local), residual_scratch()
+                advance_kernel, packs, (u, d, sums, *local), fine_scratch() + local_scratch(3)
             )
         tlo, thi = both_ways("narrow", high, low)
         wide_field, down, up = call(
@@ -747,13 +879,21 @@
             (res, tlo, thi),
         )
         zlo, zhi = both_ways("wide", up, down)
+        (own,) = call(
+            transform_kernel,
+            [((3, 8, 112, 128), F32)],
+            (wide_field, forward),
+            [pltpu.VMEM((480, 256), BF16), pltpu.VMEM((480, 256), BF16)],
+        )
+        zlo, zhi, own = lax.optimization_barrier((zlo, zhi, own))
         corr, low, high = call(
             solve_kernel,
-            [(FIELD, F32), ((3, 8, 128), F32), ((3, 8, 128), F32)],
-            (wide_field, zlo, zhi, vectors, forward, inverse, scale),
+            [(FIELD, F32), small, small],
+            (own, zlo, zhi, vectors, forward, inverse, scale),
             [
                 pltpu.VMEM((480, 256), BF16),
-                pltpu.VMEM((3, 10, 112, 128), F32),
+                pltpu.VMEM((480, 256), BF16),
+                pltpu.VMEM((3, 4, 112, 128), F32),
                 pltpu.VMEM((12, 336, 256), BF16),
             ],
             spaces={3: smem},
@@ -764,15 +904,25 @@
             (*sum_rounds(corr, low, high), res, lanes, grad, wjk),
             [pltpu.VMEM((12, 256, 256), BF16), pltpu.VMEM((2, 16, 128), F32)],
         )
-        sums = lax.all_to_all(part, BOTH, 0, 0, tiled=True)
-    out, dense = call(
-        last_kernel,
-        [(FIELD, F32), ((128, 408), F32)],
-        (u, d, sums, *local, slot, place),
-        [pltpu.VMEM(FIELD, F32), pltpu.VMEM(FIELD, F32)] + residual_scratch(),
-    )
-    coarse = jnp.sum(lax.all_to_all(dense, BOTH, 0, 0, tiled=True), axis=0)
-    return out.reshape(3, 512, 128), coarse.reshape(3, 136)
+    lin, quad = call(
+        change_kernel,
+        [(FIELD, F32), (FIELD, F32)],
+        (u, d, *local),
+        fine_scratch() + fine_scratch() + local_scratch(6),
+    )
+    (dense,) = call(
+        route_corners_kernel,
+        [((128, 1280), F32)],
+        (res, lin, quad, inside, owner, part),
+        [pltpu.VMEM((1152, 1024), BF16), pltpu.VMEM((1024, 256), BF16)],
+    )
+    parts = lax.all_to_all(dense, BOTH, 0, 0, tiled=True)
+    u, d = call(store_kernel, [(FIELD, F32), (FIELD, F32)], (u, d, slot))
+    total = jnp.sum(parts, axis=0, keepdims=True)
+    out, coarse = call(
+        end_kernel, [(FIELD, F32), ((1, 512), F32)], (u, d, total), hbm_out={0}
+    )
+    return out.reshape(3, 512, 128), coarse[0, :408].reshape(3, 136)
 
 
 def solution(mesh):

time: 216 us -> 167 us (0.77)
  blocking collectives: 55.5 us -> 19.7 us
  Pallas kernels: 85.7 us -> 55.1 us
  starting transfers between devices: 34.7 us -> 45.8 us
  waiting for transfers between devices: 29.7 us -> 38 us
  local copies, waits for them, and re-layouts: 8.47 us -> 5.35 us
    pallas_call x14 -> x20, Pallas kernels: 85.7 us -> 55.1 us  [call(): pl.pallas_call(kernel, out_shape=[jax.ShapeDtypeStruct(s, d) if i in hbm_...]
    all_to_all x2 -> x1, blocking collectives: 40 us -> 19.7 us  [shards(): sums = lax.all_to_all(part, BOTH, 0, 0, tiled=True)]
    all_to_all x1 -> x0, blocking collectives: 15.5 us -> none  [shards(): coarse = jnp.sum(lax.all_to_all(dense, BOTH, 0, 0, tiled=True), axis=0)]
    all_to_all x0 -> x1, waiting for transfers between devices: none -> 13.1 us  [shards(): parts = lax.all_to_all(dense, BOTH, 0, 0, tiled=True)]
    all_to_all x0 -> x1, starting transfers between devices: none -> 9.79 us  [shards(): parts = lax.all_to_all(dense, BOTH, 0, 0, tiled=True)]
    ppermute x20, waiting for transfers between devices: 29.7 us -> 24.9 us  [both_ways(): return (lax.ppermute(to_next, axis, up), lax.ppermute(to_prev, axis, down))]
    unnamed x40 -> x26, local copies, waits for them, and re-layouts: 6.57 us -> 3.14 us
  transfers between devices with their start and end apart: 20 -> 21, of which waited for: 15 -> 16; matrix products, arithmetic and copies ran while one was open for 0% -> 0% of each run, Pallas kernels for 1% -> 4%
where the time goes in v2:
time: 167 us
  Pallas kernels  55.1 us (33%)
  starting transfers between devices  45.8 us (27%)
  waiting for transfers between devices  38 us (23%)
  blocking collectives  19.7 us (12%)
  local copies, waits for them, and re-layouts  5.35 us (3%)
    pallas_call x20, Pallas kernels, call(): pl.pallas_call(kernel, out_shape=[jax.ShapeDtypeStruct(s, d) if i in hbm_...  55.1 us
    ppermute x20, starting transfers between devices, both_ways(): return (lax.ppermute(to_next, axis, up), lax.ppermute(to_prev, axis, down))  36 us
    ppermute x20, waiting for transfers between devices, both_ways(): return (lax.ppermute(to_next, axis, up), lax.ppermute(to_prev, axis, down))  24.9 us
    all_to_all x1, blocking collectives, shards(): sums = lax.all_to_all(part, BOTH, 0, 0, tiled=True)  19.7 us
    all_to_all x1, waiting for transfers between devices, shards(): parts = lax.all_to_all(dense, BOTH, 0, 0, tiled=True)  13.1 us
    all_to_all x1, starting transfers between devices, shards(): parts = lax.all_to_all(dense, BOTH, 0, 0, tiled=True)  9.79 us
  transfers between devices with their start and end apart: 21, of which 16 were waited for; matrix products, arithmetic and copies ran while one was open for 0% of the time, Pallas kernels for 4%

profile of v2, /device:TPU:1, one launch (start us, length us, event | category | flops | bytes accessed | tf_op | source)
XLA Modules:
  0.0 167.0 jit_solution(6914265602824100980)
XLA Ops:
  1.3 1.1 copy-done.2
  2.5 0.7 copy-done.7
  3.1 0.7 copy-done.10
  4.4 1.6 start_kernel.1
  6.0 2.6 %collective-permute-start = (f32[3,8,128]{2,1,0:T(8,128)S(1)}, f32[3,8,128]{2,1,0:T(8,128)S(1)}, u32[]{:S(2)}, u32[]{:S(2)}) collective-permute-start(f32[3,8,128]{2,1,0:T(8,128)S(1)} %get-tuple-element.64), channel_id=1, source_target_pairs={{0,1},{1,2},{2,3},{3,4},{4,5},{5,6},{6,7},{7,0},{8,9},{9,10},{10,1... | collective-permute-start | bytes 36872 | tf_op jit(solution)/shard_map/ppermute | solution.py:805
  8.6 0.8 collective-permute-done.tlo
  9.4 2.3 %collective-permute-done.1.thi = f32[3,8,128]{2,1,0:T(8,128)S(1)} collective-permute-done((f32[3,8,128]{2,1,0:T(8,128)S(1)}, f32[3,8,128]{2,1,0:T(8,128)S(1)}, u32[]{:S(2)}, u32[]{:S(2)}) %collective-permute-start.1) | collective-permute-done | bytes 12320 | tf_op jit(solution)/shard_map/ppermute | solution.py:805
  12.1 1.4 collective-permute-start.2
  13.4 5.0 %collective-permute-start.3 = (f32[200,128]{1,0:T(8,128)S(1)}, f32[200,128]{1,0:T(8,128)S(1)}, u32[]{:S(2)}, u32[]{:S(2)}) collective-permute-start(f32[200,128]{1,0:T(8,128)S(1)} %get-tuple-element.69), channel_id=1, source_target_pairs={{8,0},{16,8},{24,16},{32,24},{40,32},{48,40},{56,48},{64,56},{72,6... | collective-permute-start | bytes 307208 | tf_op jit(solution)/shard_map/ppermute | solution.py:805
  18.4 3.0 %collective-permute-done.2.zlo = f32[200,128]{1,0:T(8,128)S(1)} collective-permute-done((f32[200,128]{1,0:T(8,128)S(1)}, f32[200,128]{1,0:T(8,128)S(1)}, u32[]{:S(2)}, u32[]{:S(2)}) %collective-permute-start.2) | collective-permute-done | bytes 102432 | tf_op jit(solution)/shard_map/ppermute | solution.py:805
  21.5 6.2 %project_kernel.1 = (f32[3,8,64,128]{3,2,1,0:T(8,128)S(1)}, f32[3,8,64,128]{3,2,1,0:T(8,128)S(1)}, f32[3,16,128]{2,1,0:T(8,128)S(1)}, f32[3,16,128]{2,1,0:T(8,128)S(1)}) custom-call(f32[3,8,64,128]{3,2,1,0:T(8,128)S(1)} %get-tuple-element.67.field, f32[200,128]{1,0:T(8,128)S(1)} %collective-permute-done.2.zlo, f32[200,128]{1,0:T(8,128)S(1)} %collective-permute-done.3.zhi, ...), custom_call_target="tpu_custom_call" | custom-call | tf_op jit(solution)/shard_map/project_kernel/pallas_call | solution.py:103
  27.7 0.7 collective-permute-start.5
  28.4 0.7 collective-permute-done.4.tlo
  29.1 1.9 %collective-permute-done.5.thi = f32[3,16,128]{2,1,0:T(8,128)S(1)} collective-permute-done((f32[3,16,128]{2,1,0:T(8,128)S(1)}, f32[3,16,128]{2,1,0:T(8,128)S(1)}, u32[]{:S(2)}, u32[]{:S(2)}) %collective-permute-start.5) | collective-permute-done | bytes 24608 | tf_op jit(solution)/shard_map/ppermute | solution.py:805
  31.4 5.8 %collective-permute-start.7 = (f32[3,2,72,128]{3,2,1,0:T(8,128)S(1)}, f32[3,2,72,128]{3,2,1,0:T(8,128)S(1)}, u32[]{:S(2)}, u32[]{:S(2)}) collective-permute-start(f32[3,2,72,128]{3,2,1,0:T(8,128)S(1)} %get-tuple-element.79), channel_id=1, source_target_pairs={{8,0},{16,8},{24,16},{32,24},{40,32},{48,40},{56,48},{64,56},{72,6... | collective-permute-start | bytes 663560 | tf_op jit(solution)/shard_map/ppermute | solution.py:805
  37.2 1.3 solve_tables_kernel.1
  38.5 1.9 %transform_kernel.2.own = f32[3,8,112,128]{3,2,1,0:T(8,128)S(1)} custom-call(f32[3,8,72,128]{3,2,1,0:T(8,128)S(1)} %get-tuple-element.80.field, bf16[112,480]{1,0:T(8,128)(2,1)S(1)} %get-tuple-element.81.forward), custom_call_target="tpu_custom_call" | custom-call | tf_op jit(solution)/shard_map/transform_kernel/pallas_call | solution.py:103
  40.4 1.3 collective-permute-done.6.zlo
  41.7 5.7 %solve_kernel.2 = (f32[3,8,64,128]{3,2,1,0:T(8,128)S(1)}, f32[3,8,128]{2,1,0:T(8,128)S(1)}, f32[3,8,128]{2,1,0:T(8,128)S(1)}) custom-call(f32[3,8,112,128]{3,2,1,0:T(8,128)S(1)} %transform_kernel.2.own, f32[3,2,72,128]{3,2,1,0:T(8,128)S(1)} %collective-permute-done.6.zlo, f32[3,2,72,128]{3,2,1,0:T(8,128)S(1)} %collective-permute-done.7.zhi, ...), custom_call_target="tpu_custom_call" | custom-call | tf_op jit(solution)/shard_map/solve_kernel/pallas_call | solution.py:103
  47.9 1.3 collective-permute-start.9
  49.9 1.2 collective-permute-done.9.thi
  51.5 5.5 %collective-permute-start.11 = (f32[200,128]{1,0:T(8,128)S(1)}, f32[200,128]{1,0:T(8,128)S(1)}, u32[]{:S(2)}, u32[]{:S(2)}) collective-permute-start(f32[200,128]{1,0:T(8,128)S(1)} %get-tuple-element.92), channel_id=1, source_target_pairs={{8,0},{16,8},{24,16},{32,24},{40,32},{48,40},{56,48},{64,56},{72,6... | collective-permute-start | bytes 307208 | tf_op jit(solution)/shard_map/ppermute | solution.py:805
  57.0 2.0 %collective-permute-done.10.zlo = f32[200,128]{1,0:T(8,128)S(1)} collective-permute-done((f32[200,128]{1,0:T(8,128)S(1)}, f32[200,128]{1,0:T(8,128)S(1)}, u32[]{:S(2)}, u32[]{:S(2)}) %collective-permute-start.10) | collective-permute-done | bytes 102432 | tf_op jit(solution)/shard_map/ppermute | solution.py:805
  59.0 2.3 %direction_kernel.2 = (f32[3,8,64,128]{3,2,1,0:T(8,128)S(1)}, f32[128,128]{1,0:T(8,128)S(1)}) custom-call(f32[3,8,64,128]{3,2,1,0:T(8,128)S(1)} %get-tuple-element.90.field, f32[200,128]{1,0:T(8,128)S(1)} %collective-permute-done.10.zlo, f32[200,128]{1,0:T(8,128)S(1)} %collective-permute-done.11.zhi, f32[3,8,64,128]{3,2,1,0:T(8,128)S(1)} %get-tuple-element.75.res, ...), custom_call_target="tpu_custom_call" | custom-call | tf_op jit(solution)/shard_map/direction_kernel/pallas_call | solution.py:103
  61.2 19.7 %all_to_all.20 = f32[128,1,128]{2,1,0:T(1,128)S(1)} all-to-all(f32[128,1,128]{2,1,0:T(1,128)S(1)} %bitcast.13), channel_id=1, replica_groups=mesh['wide'=16,'narrow'=8] {'wide','narrow'}, dimensions={0} | all-to-all | bytes 131072 | tf_op jit(solution)/shard_map/all_to_all | solution.py:871
  80.9 6.5 %advance_kernel.1 = (f32[3,8,64,128]{3,2,1,0:T(8,128)S(1)}, f32[3,8,64,128]{3,2,1,0:T(8,128)S(1)}, f32[3,16,128]{2,1,0:T(8,128)S(1)}, f32[3,16,128]{2,1,0:T(8,128)S(1)}) custom-call(f32[3,8,64,128]{3,2,1,0:T(8,128)S(1)} %get-tuple-element.74.u_old, f32[3,8,64,128]{3,2,1,0:T(8,128)S(1)} %get-tuple-element.94.d, f32[128,128]{1,0:T(8,128)S(1)} %bitcast.12, ...), custom_call_target="tpu_custom_call" | custom-call | tf_op jit(solution)/shard_map/advance_kernel/pallas_call | solution.py:103
  87.4 1.0 collective-permute-start.12
  88.4 0.9 collective-permute-done.12.tlo
  89.3 2.6 %collective-permute-done.13.thi = f32[3,16,128]{2,1,0:T(8,128)S(1)} collective-permute-done((f32[3,16,128]{2,1,0:T(8,128)S(1)}, f32[3,16,128]{2,1,0:T(8,128)S(1)}, u32[]{:S(2)}, u32[]{:S(2)}) %collective-permute-start.13) | collective-permute-done | bytes 24608 | tf_op jit(solution)/shard_map/ppermute | solution.py:805
  92.7 4.6 %collective-permute-start.15 = (f32[3,2,72,128]{3,2,1,0:T(8,128)S(1)}, f32[3,2,72,128]{3,2,1,0:T(8,128)S(1)}, u32[]{:S(2)}, u32[]{:S(2)}) collective-permute-start(f32[3,2,72,128]{3,2,1,0:T(8,128)S(1)} %get-tuple-element.101), channel_id=1, source_target_pairs={{8,0},{16,8},{24,16},{32,24},{40,32},{48,40},{56,48},{64,56},{72,6... | collective-permute-start | bytes 663560 | tf_op jit(solution)/shard_map/ppermute | solution.py:805
  97.3 1.9 %transform_kernel.3.own = f32[3,8,112,128]{3,2,1,0:T(8,128)S(1)} custom-call(f32[3,8,72,128]{3,2,1,0:T(8,128)S(1)} %get-tuple-element.102.field, bf16[112,480]{1,0:T(8,128)(2,1)S(1)} %get-tuple-element.81.forward), custom_call_target="tpu_custom_call" | custom-call | tf_op jit(solution)/shard_map/transform_kernel/pallas_call | solution.py:103
  99.2 2.9 %collective-permute-done.14.zlo = f32[3,2,72,128]{3,2,1,0:T(8,128)S(1)} collective-permute-done((f32[3,2,72,128]{3,2,1,0:T(8,128)S(1)}, f32[3,2,72,128]{3,2,1,0:T(8,128)S(1)}, u32[]{:S(2)}, u32[]{:S(2)}) %collective-permute-start.14) | collective-permute-done | bytes 221216 | tf_op jit(solution)/shard_map/ppermute | solution.py:805
  102.1 5.7 %solve_kernel.3 = (f32[3,8,64,128]{3,2,1,0:T(8,128)S(1)}, f32[3,8,128]{2,1,0:T(8,128)S(1)}, f32[3,8,128]{2,1,0:T(8,128)S(1)}) custom-call(f32[3,8,112,128]{3,2,1,0:T(8,128)S(1)} %transform_kernel.3.own, f32[3,2,72,128]{3,2,1,0:T(8,128)S(1)} %collective-permute-done.14.zlo, f32[3,2,72,128]{3,2,1,0:T(8,128)S(1)} %collective-permute-done.15.zhi, ...), custom_call_target="tpu_custom_call" | custom-call | tf_op jit(solution)/shard_map/solve_kernel/pallas_call | solution.py:103
  107.7 1.5 collective-permute-start.16
  109.4 0.7 collective-permute-done.16.tlo
  110.1 2.3 %collective-permute-done.17.thi = f32[3,8,128]{2,1,0:T(8,128)S(1)} collective-permute-done((f32[3,8,128]{2,1,0:T(8,128)S(1)}, f32[3,8,128]{2,1,0:T(8,128)S(1)}, u32[]{:S(2)}, u32[]{:S(2)}) %collective-permute-start.17) | collective-permute-done | bytes 12320 | tf_op jit(solution)/shard_map/ppermute | solution.py:805
  112.8 5.2 %collective-permute-start.19 = (f32[200,128]{1,0:T(8,128)S(1)}, f32[200,128]{1,0:T(8,128)S(1)}, u32[]{:S(2)}, u32[]{:S(2)}) collective-permute-start(f32[200,128]{1,0:T(8,128)S(1)} %get-tuple-element.111), channel_id=1, source_target_pairs={{8,0},{16,8},{24,16},{32,24},{40,32},{48,40},{56,48},{64,56},{72,6... | collective-permute-start | bytes 307208 | tf_op jit(solution)/shard_map/ppermute | solution.py:805
  118.3 1.7 collective-permute-done.18.zlo
  120.0 2.2 %direction_kernel.3 = (f32[3,8,64,128]{3,2,1,0:T(8,128)S(1)}, f32[128,128]{1,0:T(8,128)S(1)}) custom-call(f32[3,8,64,128]{3,2,1,0:T(8,128)S(1)} %get-tuple-element.109.field, f32[200,128]{1,0:T(8,128)S(1)} %collective-permute-done.18.zlo, f32[200,128]{1,0:T(8,128)S(1)} %collective-permute-done.19.zhi, f32[3,8,64,128]{3,2,1,0:T(8,128)S(1)} %get-tuple-element.97.res, ...), custom_call_target="tpu_custom_call" | custom-call | tf_op jit(solution)/shard_map/direction_kernel/pallas_call | solution.py:103
  122.2 10.3 %change_kernel.1 = (f32[3,8,64,128]{3,2,1,0:T(8,128)S(1)}, f32[3,8,64,128]{3,2,1,0:T(8,128)S(1)}) custom-call(f32[3,8,64,128]{3,2,1,0:T(8,128)S(1)} %get-tuple-element.96.u, f32[3,8,64,128]{3,2,1,0:T(8,128)S(1)} %get-tuple-element.112.d, f32[16,256]{1,0:T(8,128)S(1)} %get-tuple-element.66.lanes, bf16[432,256]{1,0:T(8,128)(2,1)S(1)} %copy-done, ...), custom_call_target="tpu_custom_call" | custom-call | tf_op jit(solution)/shard_map/change_kernel/pallas_call | solution.py:103
  132.5 3.3 %route_corners_kernel.1 = f32[128,1280]{1,0:T(8,128)S(1)} custom-call(f32[3,8,64,128]{3,2,1,0:T(8,128)S(1)} %get-tuple-element.97.res, f32[3,8,64,128]{3,2,1,0:T(8,128)S(1)} %get-tuple-element.115.lin, f32[3,8,64,128]{3,2,1,0:T(8,128)S(1)} %get-tuple-element.116.quad, s32[128,8]{1,0:T(8,128)S(1)} %get-tuple-element.117.inside, ...), custom_call_target="tpu_custom_call" | custom-call | tf_op jit(solution)/shard_map/route_corners_kernel/pallas_call | solution.py:103
  135.8 1.5 copy.16
  137.4 9.8 %all-to-all-start.1 = ((f32[128,1,1280]{2,1,0:T(1,128)}), f32[128,1,1280]{2,1,0:T(1,128)}, u32[]{:S(2)}, u32[]{:S(2)}) async-start(f32[128,1,1280]{2,1,0:T(1,128)} %copy.16), calls=%async_computation.1 | async-start | bytes 1310720 | tf_op jit(solution)/shard_map/all_to_all | solution.py:919
  147.2 1.7 %store_kernel.1 = (f32[3,8,64,128]{3,2,1,0:T(8,128)S(1)}, f32[3,8,64,128]{3,2,1,0:T(8,128)S(1)}) custom-call(f32[3,8,64,128]{3,2,1,0:T(8,128)S(1)} %get-tuple-element.96.u, f32[3,8,64,128]{3,2,1,0:T(8,128)S(1)} %get-tuple-element.112.d, s32[1,128]{1,0:T(1,128)S(1)} %copy-done.8), custom_call_target="tpu_custom_call" | custom-call | tf_op jit(solution)/shard_map/store_kernel/pallas_call | solution.py:103
  148.9 13.1 %all-to-all-done.1 = f32[128,1,1280]{2,1,0:T(1,128)} async-done(((f32[128,1,1280]{2,1,0:T(1,128)}), f32[128,1,1280]{2,1,0:T(1,128)}, u32[]{:S(2)}, u32[]{:S(2)}) %all-to-all-start.1) | async-done | bytes 655392 | tf_op jit(solution)/shard_map/all_to_all | solution.py:919
  162.0 1.5 reduce_sum.9
  163.5 2.8 %end_kernel.1 = (f32[3,8,64,128]{3,2,1,0:T(8,128)}, f32[1,512]{1,0:T(1,128)S(1)}) custom-call(f32[3,8,64,128]{3,2,1,0:T(8,128)S(1)} %get-tuple-element.113.u, f32[3,8,64,128]{3,2,1,0:T(8,128)S(1)} %get-tuple-element.114.d, f32[1,1280]{1,0:T(1,128)S(1)} %broadcast_in_dim.15.total), custom_call_target="tpu_custom_call" | custom-call | tf_op jit(solution)/shard_map/end_kernel/pallas_call | solution.py:103
  166.3 0.7 reshape_squeeze.3
  (46 shorter events, 4.8 us)
Async XLA Ops:
  0.6 20.8 %copy-start = (bf16[432,256]{1,0:T(8,128)(2,1)S(1)}, bf16[432,256]{1,0:T(8,128)(2,1)}, u32[]{:S(2)}) copy-start(bf16[432,256]{1,0:T(8,128)(2,1)} %constant.12.clone.fine) | copy-start | bytes 663556
  0.6 20.8 %copy-start.1 = (f32[64,128]{1,0:T(8,128)S(1)}, f32[64,128]{1,0:T(8,128)}, u32[]{:S(2)}) copy-start(f32[64,128]{1,0:T(8,128)} %constant.16.clone.wjk) | copy-start | bytes 98308
  1.3 1.1 copy-start.2
  2.5 0.7 copy-start.7
  3.1 0.7 copy-start.10
  3.8 0.7 copy-start.11
  4.4 17.0 %copy-start.3 = (bf16[64,432]{1,0:T(8,128)(2,1)S(1)}, bf16[64,432]{1,0:T(8,128)(2,1)}, u32[]{:S(2)}) copy-start(bf16[64,432]{1,0:T(8,128)(2,1)} %constant.13.clone.back) | copy-start | bytes 165892
  4.4 17.0 %copy-start.4 = (bf16[128,256]{1,0:T(8,128)(2,1)S(1)}, bf16[128,256]{1,0:T(8,128)(2,1)}, u32[]{:S(2)}) copy-start(bf16[128,256]{1,0:T(8,128)(2,1)} %constant.14.clone.stiff) | copy-start | bytes 196612
  6.0 3.4 %collective-permute-start = (f32[3,8,128]{2,1,0:T(8,128)S(1)}, f32[3,8,128]{2,1,0:T(8,128)S(1)}, u32[]{:S(2)}, u32[]{:S(2)}) collective-permute-start(f32[3,8,128]{2,1,0:T(8,128)S(1)} %get-tuple-element.64), channel_id=1, source_target_pairs={{0,1},{1,2},{2,3},{3,4},{4,5},{5,6},{6,7},{7,0},{8,9},{9,10},{10,1... | collective-permute-start | bytes 36872 | tf_op jit(solution)/shard_map/ppermute | solution.py:805
  8.6 3.1 %collective-permute-start.1 = (f32[3,8,128]{2,1,0:T(8,128)S(1)}, f32[3,8,128]{2,1,0:T(8,128)S(1)}, u32[]{:S(2)}, u32[]{:S(2)}) collective-permute-start(f32[3,8,128]{2,1,0:T(8,128)S(1)} %get-tuple-element.65), channel_id=1, source_target_pairs={{1,0},{2,1},{3,2},{4,3},{5,4},{6,5},{7,6},{0,7},{9,8},{10,9},{11,1... | collective-permute-start | bytes 36872 | tf_op jit(solution)/shard_map/ppermute | solution.py:805
  11.7 25.5 %copy-start.6 = (f32[10,10]{1,0:T(8,128)S(1)}, f32[10,10]{1,0:T(8,128)}, u32[]{:S(2)}) copy-start(f32[10,10]{1,0:T(8,128)} %vectors.5) | copy-start | bytes 1204
  11.7 25.5 %copy-start.12 = (f32[10]{0:T(128)S(1)}, f32[10]{0:T(128)}, u32[]{:S(2)}) copy-start(f32[10]{0:T(128)} %param.20) | copy-start | bytes 124
  12.1 9.4 %collective-permute-start.2 = (f32[200,128]{1,0:T(8,128)S(1)}, f32[200,128]{1,0:T(8,128)S(1)}, u32[]{:S(2)}, u32[]{:S(2)}) collective-permute-start(f32[200,128]{1,0:T(8,128)S(1)} %get-tuple-element.68), channel_id=1, source_target_pairs={{0,8},{8,16},{16,24},{24,32},{32,40},{40,48},{48,56},{56,64},{64,7... | collective-permute-start | bytes 307208 | tf_op jit(solution)/shard_map/ppermute | solution.py:805
  13.4 8.0 %collective-permute-start.3 = (f32[200,128]{1,0:T(8,128)S(1)}, f32[200,128]{1,0:T(8,128)S(1)}, u32[]{:S(2)}, u32[]{:S(2)}) collective-permute-start(f32[200,128]{1,0:T(8,128)S(1)} %get-tuple-element.69), channel_id=1, source_target_pairs={{8,0},{16,8},{24,16},{32,24},{40,32},{48,40},{56,48},{64,56},{72,6... | collective-permute-start | bytes 307208 | tf_op jit(solution)/shard_map/ppermute | solution.py:805
  27.6 1.4 collective-permute-start.4
  27.7 3.3 %collective-permute-start.5 = (f32[3,16,128]{2,1,0:T(8,128)S(1)}, f32[3,16,128]{2,1,0:T(8,128)S(1)}, u32[]{:S(2)}, u32[]{:S(2)}) collective-permute-start(f32[3,16,128]{2,1,0:T(8,128)S(1)} %get-tuple-element.77), channel_id=1, source_target_pairs={{1,0},{2,1},{3,2},{4,3},{5,4},{6,5},{7,6},{0,7},{9,8},{10,9},{11,1... | collective-permute-start | bytes 73736 | tf_op jit(solution)/shard_map/ppermute | solution.py:805
  31.3 10.4 %collective-permute-start.6 = (f32[3,2,72,128]{3,2,1,0:T(8,128)S(1)}, f32[3,2,72,128]{3,2,1,0:T(8,128)S(1)}, u32[]{:S(2)}, u32[]{:S(2)}) collective-permute-start(f32[3,2,72,128]{3,2,1,0:T(8,128)S(1)} %get-tuple-element.78), channel_id=1, source_target_pairs={{0,8},{8,16},{16,24},{24,32},{32,40},{40,48},{48,56},{56,64},{64,7... | collective-permute-start | bytes 663560 | tf_op jit(solution)/shard_map/ppermute | solution.py:805
  31.4 10.3 %collective-permute-start.7 = (f32[3,2,72,128]{3,2,1,0:T(8,128)S(1)}, f32[3,2,72,128]{3,2,1,0:T(8,128)S(1)}, u32[]{:S(2)}, u32[]{:S(2)}) collective-permute-start(f32[3,2,72,128]{3,2,1,0:T(8,128)S(1)} %get-tuple-element.79), channel_id=1, source_target_pairs={{8,0},{16,8},{24,16},{32,24},{40,32},{48,40},{56,48},{64,56},{72,6... | collective-permute-start | bytes 663560 | tf_op jit(solution)/shard_map/ppermute | solution.py:805
  41.7 17.3 %copy-start.5 = (bf16[128,256]{1,0:T(8,128)(2,1)S(1)}, bf16[128,256]{1,0:T(8,128)(2,1)}, u32[]{:S(2)}) copy-start(bf16[128,256]{1,0:T(8,128)(2,1)} %constant.15.clone.grad) | copy-start | bytes 196612
  47.4 2.5 %collective-permute-start.8 = (f32[3,8,128]{2,1,0:T(8,128)S(1)}, f32[3,8,128]{2,1,0:T(8,128)S(1)}, u32[]{:S(2)}, u32[]{:S(2)}) collective-permute-start(f32[3,8,128]{2,1,0:T(8,128)S(1)} %get-tuple-element.88), channel_id=1, source_target_pairs={{0,1},{1,2},{2,3},{3,4},{4,5},{5,6},{6,7},{7,0},{8,9},{9,10},{10,1... | collective-permute-start | bytes 36872 | tf_op jit(solution)/shard_map/ppermute | solution.py:805
  47.9 3.1 %collective-permute-start.9 = (f32[3,8,128]{2,1,0:T(8,128)S(1)}, f32[3,8,128]{2,1,0:T(8,128)S(1)}, u32[]{:S(2)}, u32[]{:S(2)}) collective-permute-start(f32[3,8,128]{2,1,0:T(8,128)S(1)} %get-tuple-element.89), channel_id=1, source_target_pairs={{1,0},{2,1},{3,2},{4,3},{5,4},{6,5},{7,6},{0,7},{9,8},{10,9},{11,1... | collective-permute-start | bytes 36872 | tf_op jit(solution)/shard_map/ppermute | solution.py:805
  51.4 7.6 %collective-permute-start.10 = (f32[200,128]{1,0:T(8,128)S(1)}, f32[200,128]{1,0:T(8,128)S(1)}, u32[]{:S(2)}, u32[]{:S(2)}) collective-permute-start(f32[200,128]{1,0:T(8,128)S(1)} %get-tuple-element.91), channel_id=1, source_target_pairs={{0,8},{8,16},{16,24},{24,32},{32,40},{40,48},{48,56},{56,64},{64,7... | collective-permute-start | bytes 307208 | tf_op jit(solution)/shard_map/ppermute | solution.py:805
  51.5 7.5 %collective-permute-start.11 = (f32[200,128]{1,0:T(8,128)S(1)}, f32[200,128]{1,0:T(8,128)S(1)}, u32[]{:S(2)}, u32[]{:S(2)}) collective-permute-start(f32[200,128]{1,0:T(8,128)S(1)} %get-tuple-element.92), channel_id=1, source_target_pairs={{8,0},{16,8},{24,16},{32,24},{40,32},{48,40},{56,48},{64,56},{72,6... | collective-permute-start | bytes 307208 | tf_op jit(solution)/shard_map/ppermute | solution.py:805
  87.4 1.9 %collective-permute-start.12 = (f32[3,16,128]{2,1,0:T(8,128)S(1)}, f32[3,16,128]{2,1,0:T(8,128)S(1)}, u32[]{:S(2)}, u32[]{:S(2)}) collective-permute-start(f32[3,16,128]{2,1,0:T(8,128)S(1)} %get-tuple-element.98), channel_id=1, source_target_pairs={{0,1},{1,2},{2,3},{3,4},{4,5},{5,6},{6,7},{7,0},{8,9},{9,10},{10,1... | collective-permute-start | bytes 73736 | tf_op jit(solution)/shard_map/ppermute | solution.py:805
  88.4 3.5 %collective-permute-start.13 = (f32[3,16,128]{2,1,0:T(8,128)S(1)}, f32[3,16,128]{2,1,0:T(8,128)S(1)}, u32[]{:S(2)}, u32[]{:S(2)}) collective-permute-start(f32[3,16,128]{2,1,0:T(8,128)S(1)} %get-tuple-element.99), channel_id=1, source_target_pairs={{1,0},{2,1},{3,2},{4,3},{5,4},{6,5},{7,6},{0,7},{9,8},{10,9},{11,1... | collective-permute-start | bytes 73736 | tf_op jit(solution)/shard_map/ppermute | solution.py:805
  92.3 9.8 %collective-permute-start.14 = (f32[3,2,72,128]{3,2,1,0:T(8,128)S(1)}, f32[3,2,72,128]{3,2,1,0:T(8,128)S(1)}, u32[]{:S(2)}, u32[]{:S(2)}) collective-permute-start(f32[3,2,72,128]{3,2,1,0:T(8,128)S(1)} %get-tuple-element.100), channel_id=1, source_target_pairs={{0,8},{8,16},{16,24},{24,32},{32,40},{40,48},{48,56},{56,64},{64,7... | collective-permute-start | bytes 663560 | tf_op jit(solution)/shard_map/ppermute | solution.py:805
  92.7 9.3 %collective-permute-start.15 = (f32[3,2,72,128]{3,2,1,0:T(8,128)S(1)}, f32[3,2,72,128]{3,2,1,0:T(8,128)S(1)}, u32[]{:S(2)}, u32[]{:S(2)}) collective-permute-start(f32[3,2,72,128]{3,2,1,0:T(8,128)S(1)} %get-tuple-element.101), channel_id=1, source_target_pairs={{8,0},{16,8},{24,16},{32,24},{40,32},{48,40},{56,48},{64,56},{72,6... | collective-permute-start | bytes 663560 | tf_op jit(solution)/shard_map/ppermute | solution.py:805
  99.2 18.8 %copy-start.8 = (s32[1,128]{1,0:T(1,128)S(1)}, s32[1,128]{1,0:T(1,128)}, u32[]{:S(2)}) copy-start(s32[1,128]{1,0:T(1,128)} %slot.5) | copy-start | bytes 1540
  99.2 18.8 %copy-start.9 = (s32[8,128]{1,0:T(8,128)S(1)}, s32[8,128]{1,0:T(8,128)}, u32[]{:S(2)}) copy-start(s32[8,128]{1,0:T(8,128)} %corner.1) | copy-start | bytes 12292
  107.7 2.4 %collective-permute-start.16 = (f32[3,8,128]{2,1,0:T(8,128)S(1)}, f32[3,8,128]{2,1,0:T(8,128)S(1)}, u32[]{:S(2)}, u32[]{:S(2)}) collective-permute-start(f32[3,8,128]{2,1,0:T(8,128)S(1)} %get-tuple-element.107), channel_id=1, source_target_pairs={{0,1},{1,2},{2,3},{3,4},{4,5},{5,6},{6,7},{7,0},{8,9},{9,10},{10,1... | collective-permute-start | bytes 36872 | tf_op jit(solution)/shard_map/ppermute | solution.py:805
  109.3 3.1 %collective-permute-start.17 = (f32[3,8,128]{2,1,0:T(8,128)S(1)}, f32[3,8,128]{2,1,0:T(8,128)S(1)}, u32[]{:S(2)}, u32[]{:S(2)}) collective-permute-start(f32[3,8,128]{2,1,0:T(8,128)S(1)} %get-tuple-element.108), channel_id=1, source_target_pairs={{1,0},{2,1},{3,2},{4,3},{5,4},{6,5},{7,6},{0,7},{9,8},{10,9},{11,1... | collective-permute-start | bytes 36872 | tf_op jit(solution)/shard_map/ppermute | solution.py:805
  112.7 7.2 %collective-permute-start.18 = (f32[200,128]{1,0:T(8,128)S(1)}, f32[200,128]{1,0:T(8,128)S(1)}, u32[]{:S(2)}, u32[]{:S(2)}) collective-permute-start(f32[200,128]{1,0:T(8,128)S(1)} %get-tuple-element.110), channel_id=1, source_target_pairs={{0,8},{8,16},{16,24},{24,32},{32,40},{40,48},{48,56},{56,64},{64,7... | collective-permute-start | bytes 307208 | tf_op jit(solution)/shard_map/ppermute | solution.py:805
  112.8 7.1 %collective-permute-start.19 = (f32[200,128]{1,0:T(8,128)S(1)}, f32[200,128]{1,0:T(8,128)S(1)}, u32[]{:S(2)}, u32[]{:S(2)}) collective-permute-start(f32[200,128]{1,0:T(8,128)S(1)} %get-tuple-element.111), channel_id=1, source_target_pairs={{8,0},{16,8},{24,16},{32,24},{40,32},{48,40},{56,48},{64,56},{72,6... | collective-permute-start | bytes 307208 | tf_op jit(solution)/shard_map/ppermute | solution.py:805
  137.4 24.6 %all-to-all-start.1 = ((f32[128,1,1280]{2,1,0:T(1,128)}), f32[128,1,1280]{2,1,0:T(1,128)}, u32[]{:S(2)}, u32[]{:S(2)}) async-start(f32[128,1,1280]{2,1,0:T(1,128)} %copy.16), calls=%async_computation.1 | async-start | bytes 1310720 | tf_op jit(solution)/shard_map/all_to_all | solution.py:919

commit v3 on v2

--- a/solution.py
+++ b/solution.py
@@ -70,6 +70,9 @@
 WJK = np.kron(W, W)
 
 
+WJK_ROWS = np.broadcast_to(WJK[:, None], (64, 128)).astype(np.float32)
+
+
 def two_parts(matrix):
     hi = matrix.astype(np.float32).astype(ml_dtypes.bfloat16)
     lo = (matrix - hi.astype(np.float64)).astype(ml_dtypes.bfloat16)
@@ -91,25 +94,39 @@
 STIFF_JK = four_terms(
     np.concatenate([np.kron(STIFF, np.diag(W)), np.kron(np.diag(W), STIFF)])
 )
+COARSE_Z = LIN @ JV
+COARSE_JK = three_terms(
+    np.concatenate(
+        [
+            np.kron(COARSE_Z, COARSE_Z),
+            np.kron(COARSE_Z, np.stack([JV[0], JV[7]])),
+            np.zeros((8, 144)),
+        ]
+    )
+)
 GRAD_JK = four_terms(np.concatenate([np.kron(D, np.eye(8)), np.kron(np.eye(8), D)]))
 
 
-def call(kernel, outs, args, scratch=(), spaces=None, hbm_out=()):
+def call(kernel, outs, args, scratch=(), spaces=None, hbm_out=(), free=False):
     spaces = spaces or {}
     args = [
-        pltpu.with_memory_space_constraint(a, spaces.get(i, pltpu.VMEM))
+        a if free and i not in spaces
+        else pltpu.with_memory_space_constraint(a, spaces.get(i, pltpu.VMEM))
         for i, a in enumerate(args)
     ]
     return pl.pallas_call(
         kernel,
         out_shape=[
-            jax.ShapeDtypeStruct(s, d) if i in hbm_out else pltpu.VMEM(s, d)
+            (pltpu.HBM if i in hbm_out else pltpu.VMEM)(s, d)
             for i, (s, d) in enumerate(outs)
         ],
         in_specs=[
             pl.BlockSpec(memory_space=spaces.get(i, pltpu.VMEM)) for i in range(len(args))
         ],
-        out_specs=[pl.BlockSpec(memory_space=pltpu.VMEM) for _ in outs],
+        out_specs=[
+            pl.BlockSpec(memory_space=pltpu.HBM if i in hbm_out else pltpu.VMEM)
+            for i in range(len(outs))
+        ],
         scratch_shapes=list(scratch),
         compiler_params=pltpu.CompilerParams(vmem_limit_bytes=32 << 20),
         name=kernel.func.__name__ if isinstance(kernel, partial) else kernel.__name__,
@@ -200,16 +217,26 @@
     return jnp.where(lane >= 112, lanes_by(packed, 112 - 16 * i), lanes_by(plane, -16))
 
 
-def start_kernel(vel, slot, arc, rad, axial, mv, low, high, lanes):
-    ht = jnp.broadcast_to(arc[...], (8, 16))
-    hr = jnp.broadcast_to(rad[...], (8, 16))
-    spread = ((iota((16, 256), 1) & 15) == iota((16, 256), 0)).astype(F32)
-    ht = jnp.dot(ht, spread, precision=EXACT, preferred_element_type=F32)[0:1]
-    hr = jnp.dot(hr, spread, precision=EXACT, preferred_element_type=F32)[0:1]
+CONSTANTS = (FINE, BACK, STIFF_JK, GRAD_JK, COARSE_JK, WJK_ROWS)
+
+
+def start_kernel(vel_hbm, slot_hbm, arc, rad, axial, *refs):
+    n = len(CONSTANTS)
+    hbm, mv, low, high, lanes = refs[:n], *refs[n : n + 4]
+    held, (vel, slot, sems) = refs[n + 4 : 2 * n + 4], refs[2 * n + 4 :]
+    pairs = [(slot_hbm, slot)] + [(vel_hbm.at[c], vel.at[c]) for c in range(3)]
+    pairs += list(zip(hbm, held))
+    copies = [pltpu.make_async_copy(a, b, sems.at[i]) for i, (a, b) in enumerate(pairs)]
+    for copy in copies:
+        copy.start()
+    r = iota((1, 256), 1) & (RADIAL - 1)
+    ht, hr = jnp.zeros((1, 256), F32), jnp.zeros((1, 256), F32)
+    for i in range(RADIAL):
+        ht = jnp.where(r == i, arc[i], ht)
+        hr = jnp.where(r == i, rad[i], hr)
     hz = jnp.zeros((1, 256), F32) + axial[0]
     g = ht * hr / 8.0
     vol = hz * g
-    r = iota((1, 256), 1) & (RADIAL - 1)
     g_low = g + jnp.where(r > 0, lanes_by(g, 1), 0.0)
     g_high = g + jnp.where(r < RADIAL - 1, lanes_by(g, -1), 0.0)
     rows = [
@@ -229,18 +256,18 @@
         lanes[n : n + 1] = row
     for n in range(len(rows), 16):
         lanes[n : n + 1] = jnp.zeros((1, 256), F32)
+    copies[0].wait()
     hot = (slot[...] == iota((128, 128), 0)).astype(F32)
     nt = (((1,), (1,)), ((), ()))
-
-    def body(c, carry):
+    for c in range(3):
+        copies[1 + c].wait()
         x = vel[c].reshape(512, 128)
         y = lax.dot_general(x, hot, nt, precision=EXACT, preferred_element_type=F32)
         mv[c] = (y * vol[:, :128]).reshape(8, 64, 128)
         low[c] = pack_low(lambda i: mv[c, i, 0:8])
         high[c] = pack_high(lambda i: mv[c, i, 56:64])
-        return carry
-
-    lax.fori_loop(0, 3, body, 0)
+    for copy in copies[4:]:
+        copy.wait()
 
 
 def solve_tables_kernel(vectors, values, lanes, forward, inverse, scale):
@@ -440,48 +467,104 @@
     lax.fori_loop(0, 12, body, 0)
 
 
+def fields_kernel(u, fine, pf, qf, xu, xw):
+    along_pipe(u, xu, xw)
+    for p in range(6):
+        fine_dots(p, p, fine, xu, xw, pf, qf)
+
+
+def corner_weights():
+    row, col = iota((8, 64), 0), iota((8, 64), 1)
+
+    def weight(node, upper):
+        acc = jnp.zeros((8, 64), F32)
+        for n in range(8):
+            acc = jnp.where(
+                node == n, jnp.where(upper, float(LIN[1, n]), float(LIN[0, n])), acc
+            )
+        return acc
+
+    return weight(col >> 3, (row & 2) != 0) * weight(col & 7, (row & 1) != 0)
+
+
+def corners_kernel(res, out):
+    weights = corner_weights()
+    for c in range(3):
+        planes = [res[c, i] for i in range(8)]
+        z1 = sum(float(LIN[1, i]) * planes[i] for i in range(1, 8))
+        z0 = sum(float(LIN[0, i]) * planes[i] for i in range(7))
+        both = jnp.concatenate([z0, z1], axis=1)
+        out[c] = jnp.dot(weights, both, precision=EXACT, preferred_element_type=F32)
+
+
 def change_kernel(
-    u, d, lanes, fine, back, stiff, wjk, lin, quad, pf, qf, xu, xw, pd, qd, xd, xe, xs,
-    xc0, xc1, yf, sz, ks
+    d, pf, qf, lanes, fine, stiff, wjk, coarse, out, pd, qd, xd, xe, xs, acc, xc, sz
 ):
-    along_pipe(u, xu, xw)
-    along_pipe(d, xd, xe, xs, sz)
-    fine_dots(0, 0, fine, xu, xw, pf, qf)
+    mean_w = LIN * W[None, :]
+    mean_s = LIN @ STIFF
+
+    def body(t, carry):
+        c, rb = t // 4, t % 4
+        rows = pl.ds(pl.multiple_of(rb * 16, 16), 16)
+        x = [d[c, i, rows] for i in range(8)]
+        for a, val in enumerate(even_odd(J, x, 1)):
+            put(xd, c * 6 + a // 2, rb, a % 2, val)
+        for a, val in enumerate(even_odd(B, x, -1)):
+            put(xe, c * 6 + a // 2, rb, a % 2, val)
+        for a in range(2):
+            put(xs, c, rb, a, sum(float(mean_w[a, i]) * x[i] for i in range(8)))
+            sz[c, a, rows] = sum(float(mean_s[a, i]) * x[i] for i in range(8))
+        return carry
+
+    lax.fori_loop(0, 12, body, 0)
+    acc[...] = jnp.zeros_like(acc)
+
+    def add_conv(n, p, r, conv):
+        rows = slice(16 * r, 16 * r + 16)
+        left, right = conv[:, :128], conv[:, 128:]
+        for a in range(2):
+            acc[n, rows, 128 * a : 128 * a + 128] += (
+                float(COARSE_Z[a, 2 * p]) * left + float(COARSE_Z[a, 2 * p + 1]) * right
+            )
+
     fine_dots(0, 0, fine, xd, xe, pd, qd)
     for p in range(6):
         if p < 5:
-            fine_dots(p + 1, (p + 1) % 2, fine, xu, xw, pf, qf)
             fine_dots(p + 1, (p + 1) % 2, fine, xd, xe, pd, qd)
-        stiff_dots(p, stiff, xs, ks)
-        xc = (xc0, xc1)[p % 2]
         for r in range(9):
-            v = velocity_rows(pf, lanes, p % 2, r)
+            v = velocity_rows(pf, lanes, p, r)
             w = velocity_rows(pd, lanes, p % 2, r)
             for c in range(3):
-                g = fine_rows(pf, qf, p % 2, c, r)
+                g = fine_rows(pf, qf, p, c, r)
                 h = fine_rows(pd, qd, p % 2, c, r)
-                put_conv(
-                    xc,
-                    c,
-                    r,
-                    (v[0] * h[0] + v[1] * h[1] + v[2] * h[2])
-                    + (w[0] * g[0] + w[1] * g[1] + w[2] * g[2]),
+                one = (v[0] * h[0] + v[1] * h[1] + v[2] * h[2]) + (
+                    w[0] * g[0] + w[1] * g[1] + w[2] * g[2]
                 )
-                put_conv(xc, 3 + c, r, w[0] * h[0] + w[1] * h[1] + w[2] * h[2])
-        back_dots(p, back, xc, yf, 6)
-    keep = keep_rows(16)
-
-    def body(t, carry):
-        c, rb = t // 4, t % 4
-        rows = pl.ds(pl.multiple_of(rb * 16, 16), 16)
-        one = even_odd(JV, [yf[c, a, rows] for a in range(12)], 1)
-        two = even_odd(JV, [yf[3 + c, a, rows] for a in range(12)], 1)
-        for i in range(8):
-            lin[c, i, rows] = -(one[i] + stiff_plane(lanes, wjk, sz, ks, c, i, rb)) * keep
-            quad[c, i, rows] = -two[i] * keep
-        return carry
-
-    lax.fori_loop(0, 12, body, 0)
+                add_conv(c, p, r, one)
+                add_conv(3 + c, p, r, w[0] * h[0] + w[1] * h[1] + w[2] * h[2])
+    r = iota((4, 256), 1) & (RADIAL - 1)
+    upper = iota((4, 256), 0) & 1
+    wall = ((upper == 0) & (r == 0)) | ((upper == 1) & (r == RADIAL - 1))
+    wall = jnp.where(wall, 1.0, 0.0).astype(F32)
+    keep = jnp.concatenate([keep_rows(64)] * 2, axis=1)
+    wide = jnp.concatenate([wjk[...]] * 2, axis=1)
+    kz, kt, kr = lanes[4:5], lanes[5:6], lanes[6:7]
+    weights = corner_weights()
+    for n in range(6):
+        for q in range(9):
+            put_conv(xc, n, q, acc[n, 16 * q : 16 * q + 16])
+        y = dot(coarse[...], xc[n])
+        total = y[0:4] - wall * y[4:8]
+        if n < 3:
+            ks = dot(stiff[...], xs[n])
+            plane = jnp.concatenate([sz[n, 0], sz[n, 1]], axis=1) * wide * kz
+            plane = (plane + kt * ks[0:64] + kr * ks[64:128]) * keep
+            total = (
+                total
+                + jnp.dot(weights, plane, precision=EXACT, preferred_element_type=F32)[0:4]
+            )
+        out[n, 0:4] = -total
+        out[n, 4:8] = jnp.zeros((4, 256), F32)
 
 
 def pack_two(res, low, high):
@@ -577,62 +660,75 @@
         xf[320 + 16 * j : 336 + 16 * j, cols] = lo
 
 
-def transform_kernel(field, forward, out, *xf):
+def transform_kernel(field, forward, vectors, out, xf0, xf1, yf):
     def body(c, carry):
         for p in range(4):
-            buf = xf[p % 2]
+            buf = (xf0, xf1)[p % 2]
             for half in range(2):
                 widen_planes(field[c, 2 * p + half], buf, half)
             y = dot(forward[...], buf[...])
-            out[c, 2 * p] = y[:, :128]
-            out[c, 2 * p + 1] = y[:, 128:]
+            yf[c, 2 * p] = y[:, :128]
+            yf[c, 2 * p + 1] = y[:, 128:]
         return carry
 
     lax.fori_loop(0, 3, body, 0)
+
+    def mid(rb, carry):
+        rows = pl.ds(pl.multiple_of(rb * 16, 16), 16)
+        y = [[yf[c, i, rows] for i in range(8)] for c in range(3)]
+        for a in range(10):
+            acc = [vectors[1, a] * y[c][0] for c in range(3)]
+            for i in range(1, 8):
+                s = vectors[i + 1, a]
+                acc = [acc[c] + s * y[c][i] for c in range(3)]
+            for c in range(3):
+                out[c, a, rows] = acc[c]
+        return carry
+
+    lax.fori_loop(0, 7, mid, 0)
 
 
 def solve_kernel(
     own, zlo, zhi, vectors, forward, inverse, scale, corr, low, high, xf0, xf1, yf, xb
 ):
     def body(c, carry):
-        for buf, halo, at in ((xf0, zlo, 0), (xf1, zhi, 8)):
+        for buf, halo in ((xf0, zlo), (xf1, zhi)):
             widen_planes(halo[c, 0], buf, 0)
             widen_planes(halo[c, 1], buf, 1)
         y0, y1 = dot(forward[...], xf0[...]), dot(forward[...], xf1[...])
         yf[c, 0] = y0[:, :128]
-        yf[c, 1] = y0[:, 128:] + own[c, 0]
-        yf[c, 2] = y1[:, :128] + own[c, 7]
+        yf[c, 1] = y0[:, 128:]
+        yf[c, 2] = y1[:, :128]
         yf[c, 3] = y1[:, 128:]
         return carry
 
     lax.fori_loop(0, 3, body, 0)
 
-    def mid(t, carry):
-        c, rb = t // 7, t % 7
+    def mid(rb, carry):
         rows = pl.ds(pl.multiple_of(rb * 16, 16), 16)
-        y = (
-            [yf[c, 0, rows], yf[c, 1, rows]]
-            + [own[c, i, rows] for i in range(1, 7)]
-            + [yf[c, 2, rows], yf[c, 3, rows]]
-        )
+        y = [[yf[c, i, rows] for i in range(4)] for c in range(3)]
         spec = []
         for a in range(10):
-            acc = vectors[0, a] * y[0]
-            for i in range(1, 10):
-                acc = acc + vectors[i, a] * y[i]
-            spec.append(acc * scale[a, rows])
+            acc = [own[c, a, rows] for c in range(3)]
+            for n, i in enumerate((0, 1, 8, 9)):
+                s = vectors[i, a]
+                acc = [acc[c] + s * y[c][n] for c in range(3)]
+            f = scale[a, rows]
+            spec.append([acc[c] * f for c in range(3)])
         for i in range(8):
-            acc = vectors[i + 1, 0] * spec[0]
+            acc = [vectors[i + 1, 0] * spec[0][c] for c in range(3)]
             for a in range(1, 10):
-                acc = acc + vectors[i + 1, a] * spec[a]
-            hi, lo = split(acc)
+                s = vectors[i + 1, a]
+                acc = [acc[c] + s * spec[a][c] for c in range(3)]
             cols = slice((i % 2) * 128, (i % 2) * 128 + 128)
-            for term, part in enumerate((hi, hi, lo)):
-                xb[c * 4 + i // 2, pl.ds(pl.multiple_of(term * 112 + rb * 16, 16), 16),
-                   cols] = part
-        return carry
-
-    lax.fori_loop(0, 21, mid, 0)
+            for c in range(3):
+                hi, lo = split(acc[c])
+                for term, part in enumerate((hi, hi, lo)):
+                    xb[c * 4 + i // 2, pl.ds(pl.multiple_of(term * 112 + rb * 16, 16), 16),
+                       cols] = part
+        return carry
+
+    lax.fori_loop(0, 7, mid, 0)
 
     k = iota((8, 128), 0)
     r = iota((8, 128), 1) & (RADIAL - 1)
@@ -706,7 +802,7 @@
     sums[...] = jnp.where(at == 0, num, jnp.where(at == 1, den, 0.0))
 
 
-def route_kernel(slot, corner, inside, owner):
+def route_kernel(slot, corner, right, owner):
     hot = (slot[...] == iota((128, 128), 0)).astype(F32)
     nt = (((1,), (1,)), ((), ()))
     ids = corner[...].astype(F32)
@@ -714,85 +810,85 @@
     by_corner = lax.dot_general(ids, hot, nt, precision=EXACT, preferred_element_type=F32)
     owner[...] = (by_corner + 0.5).astype(jnp.int32) // 136
     ids = (by_elem + 0.5).astype(jnp.int32)
-    inside[...] = ids - ids // 136 * 136
-
-
-def route_corners_kernel(res, lin, quad, inside, owner, part, dense, left, right):
-    row, col = iota((8, 64), 0), iota((8, 64), 1)
-
-    def weight(node, upper):
-        acc = jnp.zeros((8, 64), F32)
-        for n in range(8):
-            acc = jnp.where(
-                node == n, jnp.where(upper, float(LIN[1, n]), float(LIN[0, n])), acc
-            )
-        return acc
-
-    corner_jk = weight(col >> 3, (row & 2) != 0) * weight(col & 7, (row & 1) != 0)
-    pos, dev = iota((128, 256), 1), iota((128, 128), 0)
+    inside = ids - ids // 136 * 136
+    pos = iota((128, 256), 1)
     for q in range(8):
         right[128 * q : 128 * q + 128] = (inside[:, q : q + 1] == pos).astype(F32).astype(BF16)
-    for n, ref in enumerate((res, lin, quad)):
+
+
+def place_kernel(base, change, right, owner, part, dense, left):
+    dev = iota((128, 128), 0)
+    spill = None
+    for n in range(3):
         for c in range(3):
-            planes = [ref[c, i] for i in range(8)]
-            z1 = sum(float(LIN[1, i]) * planes[i] for i in range(1, 8))
-            z0 = sum(float(LIN[0, i]) * planes[i] for i in range(7))
-            both = jnp.dot(
-                corner_jk,
-                jnp.concatenate([z0, z1], axis=1),
-                precision=EXACT,
-                preferred_element_type=F32,
-            )
+            both = base[c] if n == 0 else change[3 * (n - 1) + c]
             hi = both.astype(BF16).astype(F32)
-            mid = (both - hi).astype(BF16).astype(F32)
             for q in range(8):
                 mine = owner[q : q + 1] == dev
                 cols = slice((q // 4) * 128, (q // 4) * 128 + 128)
-                for m, piece in enumerate((hi, mid, both - hi - mid)):
-                    at = (3 * c + m) * 128
-                    left[at : at + 128, 128 * q : 128 * q + 128] = jnp.where(
+                for m, piece in enumerate((hi, both - hi)):
+                    at = (2 * c + m) * 128
+                    left[n, at : at + 128, 128 * q : 128 * q + 128] = jnp.where(
                         mine, piece[q % 4 : q % 4 + 1, cols], 0.0
                     ).astype(BF16)
-        y = dot(left[...], right[...])
+        y = dot(left[n], right[...])
         for c in range(3):
             block = 3 * n + c
-            total = (
-                y[384 * c : 384 * c + 128]
-                + y[384 * c + 128 : 384 * c + 256]
-                + y[384 * c + 256 : 384 * c + 384]
+            total = lanes_by(y[256 * c : 256 * c + 128] + y[256 * c + 128 : 256 * c + 256],
+                             8 * block)
+            first = total[:, :128]
+            dense[:, 0, 128 * block : 128 * block + 128] = (
+                first if spill is None else first + spill
             )
-            total = lanes_by(total, 8 * block)
-            first = slice(128 * block, 128 * block + 128)
-            dense[:, first] = total[:, :128] if block == 0 else dense[:, first] + total[:, :128]
-            dense[:, 128 * block + 128 : 128 * block + 256] = total[:, 128:]
-    dense[:, 1152:1280] += lanes_by(part[...], 72)
-
-
-def store_kernel(u, d, slot, u_out, d_out):
+            spill = total[:, 128:]
+    dense[:, 0, 1152:1280] = spill + lanes_by(part[...], 72)
+
+
+def store_kernel(u, d, slot, u_hbm, d_hbm, u_out, d_out, sems):
     hot = (slot[...] == iota((128, 128), 0)).astype(F32)
-
-    def body(c, carry):
-        for x, y in ((u, u_out), (d, d_out)):
+    copies = []
+    for c in range(3):
+        for n, (x, y, out) in enumerate(((u, u_out, u_hbm), (d, d_out, d_hbm))):
             flat = x[c].reshape(512, 128)
             y[c] = jnp.dot(flat, hot, precision=EXACT, preferred_element_type=F32).reshape(
                 8, 64, 128
             )
-        return carry
-
-    lax.fori_loop(0, 3, body, 0)
-
-
-def end_kernel(u, d, total, vel, coarse):
-    alpha = total[0:1, 1224:1225] / total[0:1, 1225:1226]
-    one, two = lanes_by(total[...], -408), lanes_by(total[...], -816)
-    coarse[...] = (total[...] + alpha * (one + alpha * two))[0:1, 0:512]
-
-    def body(t, carry):
-        c, i = t // 8, t % 8
-        vel[c, i] = u[c, i] + alpha * d[c, i]
-        return carry
-
-    lax.fori_loop(0, 24, body, 0)
+            copies.append(pltpu.make_async_copy(y.at[c], out.at[c], sems.at[2 * c + n]))
+            copies[-1].start()
+    for copy in copies:
+        copy.wait()
+
+
+def end_kernel(u_hbm, d_hbm, parts_hbm, vel_hbm, coarse, u, d, parts, vel, sems):
+    first = pltpu.make_async_copy(parts_hbm, parts, sems.at[0])
+    loads = [
+        [
+            pltpu.make_async_copy(a.at[c], b.at[c], sems.at[1 + 2 * c + n])
+            for n, (a, b) in enumerate(((u_hbm, u), (d_hbm, d)))
+        ]
+        for c in range(3)
+    ]
+    stores = [
+        pltpu.make_async_copy(vel.at[c], vel_hbm.at[c], sems.at[7 + c]) for c in range(3)
+    ]
+    first.start()
+    for pair in loads:
+        for copy in pair:
+            copy.start()
+    first.wait()
+    total = jnp.sum(parts[...], axis=0)
+    alpha = total[:, 1224:1225] / total[:, 1225:1226]
+    for c in range(3):
+        for copy in loads[c]:
+            copy.wait()
+        vel[c] = u[c] + alpha * d[c]
+        stores[c].start()
+    one, two = lanes_by(total, -408), lanes_by(total, -816)
+    both = total + alpha * (one + alpha * two)
+    for c in range(3):
+        coarse[c : c + 1] = lanes_by(both, -136 * c)[:, :136]
+    for copy in stores:
+        copy.wait()
 
 
 FIELD = (3, 8, 64, 128)
@@ -826,20 +922,22 @@
 
 
 def shards(vel, slot, corner, axial, arc, rad, vectors, values):
-    fine, back, stiff, grad = (jnp.asarray(m) for m in (FINE, BACK, STIFF_JK, GRAD_JK))
-    wjk = jnp.asarray(np.broadcast_to(WJK[:, None], (64, 128)).astype(np.float32))
     smem = pltpu.SMEM
     small = ((3, 8, 128), F32)
-    mv, low, high, lanes = call(
+    count = len(CONSTANTS)
+    mv, low, high, lanes, fine, back, stiff, grad, coarse_jk, wjk = call(
         start_kernel,
-        [(FIELD, F32), small, small, ((16, 256), F32)],
-        (vel.reshape(FIELD), slot, arc[None], rad[None], axial),
-        spaces={4: smem},
-    )
-    inside, owner = call(
-        route_kernel,
-        [((128, 8), jnp.int32), ((8, 128), jnp.int32)],
-        (slot, corner),
+        [(FIELD, F32), small, small, ((16, 256), F32)] + [(m.shape, m.dtype) for m in CONSTANTS],
+        (vel.reshape(FIELD), slot, arc, rad, axial, *(jnp.asarray(m) for m in CONSTANTS)),
+        [
+            pltpu.VMEM(FIELD, F32),
+            pltpu.VMEM((1, 128), jnp.int32),
+            pltpu.SemaphoreType.DMA((4 + count,)),
+        ],
+        spaces={
+            0: pltpu.HBM, 1: pltpu.HBM, 2: smem, 3: smem, 4: smem,
+            **{5 + i: pltpu.HBM for i in range(count)},
+        },
     )
     forward, inverse, scale = call(
         solve_tables_kernel,
@@ -847,7 +945,7 @@
         (vectors, values[None], lanes),
     )
 
-    def sum_rounds(field, low, high):
+    def sum_rounds(field, low, high, beside=()):
         tlo, thi = both_ways("narrow", high, low)
         out, down, up = call(
             around_sum_kernel,
@@ -855,15 +953,15 @@
             (field, tlo, thi, lanes),
         )
         zlo, zhi = both_ways("wide", up, down)
-        return out, zlo, zhi
-
-    fine, back, stiff, wjk, grad, mv = lax.optimization_barrier((fine, back, stiff, wjk, grad, mv))
+        zlo, zhi, beside = lax.optimization_barrier((zlo, zhi, beside))
+        return (out, zlo, zhi), beside
+
     local = (lanes, fine, back, stiff, wjk)
     packs = [(FIELD, F32), (FIELD, F32), ((3, 16, 128), F32), ((3, 16, 128), F32)]
     u, res, low, high = call(
         project_kernel,
         packs,
-        (*sum_rounds(mv, low, high), *local),
+        (*sum_rounds(mv, low, high)[0], *local),
         fine_scratch() + local_scratch(3),
     )
     for step in range(2):
@@ -881,9 +979,14 @@
         zlo, zhi = both_ways("wide", up, down)
         (own,) = call(
             transform_kernel,
-            [((3, 8, 112, 128), F32)],
-            (wide_field, forward),
-            [pltpu.VMEM((480, 256), BF16), pltpu.VMEM((480, 256), BF16)],
+            [((3, 10, 112, 128), F32)],
+            (wide_field, forward, vectors),
+            [
+                pltpu.VMEM((480, 256), BF16),
+                pltpu.VMEM((480, 256), BF16),
+                pltpu.VMEM((3, 8, 112, 128), F32),
+            ],
+            spaces={2: smem},
         )
         zlo, zhi, own = lax.optimization_barrier((zlo, zhi, own))
         corr, low, high = call(
@@ -898,31 +1001,69 @@
             ],
             spaces={3: smem},
         )
+        beside = ()
+        if step == 1:
+            fields = [((6, 3, 432, 256), F32), ((6, 3, 144, 256), F32)]
+            beside = (
+                call(fields_kernel, fields, (u, fine), fine_scratch()[2:]),
+                call(corners_kernel, [((3, 8, 256), F32)], (res,)),
+                call(
+                    route_kernel,
+                    [((1024, 256), BF16), ((8, 128), jnp.int32)],
+                    (slot, corner),
+                    free=True,
+                ),
+            )
+        halo, beside = sum_rounds(corr, low, high, beside)
         d, part = call(
             direction_kernel,
             [(FIELD, F32), ((128, 128), F32)],
-            (*sum_rounds(corr, low, high), res, lanes, grad, wjk),
+            (*halo, res, lanes, grad, wjk),
             [pltpu.VMEM((12, 256, 256), BF16), pltpu.VMEM((2, 16, 128), F32)],
         )
-    lin, quad = call(
+    (pf, qf), (base,), (right, owner) = beside
+    (change,) = call(
         change_kernel,
+        [((6, 8, 256), F32)],
+        (d, pf, qf, lanes, fine, stiff, wjk, coarse_jk),
+        fine_scratch()
+        + [
+            pltpu.VMEM((3, 256, 256), BF16),
+            pltpu.VMEM((6, 144, 256), F32),
+            pltpu.VMEM((6, 432, 256), BF16),
+            pltpu.VMEM((3, 2, 64, 128), F32),
+        ],
+    )
+    (dense,) = call(
+        place_kernel,
+        [((128, 1, 1280), F32)],
+        (base, change, right, owner, part),
+        [pltpu.VMEM((3, 768, 1024), BF16)],
+    )
+    parts = lax.all_to_all(dense, BOTH, 0, 0, tiled=True)
+    u, d = call(
+        store_kernel,
         [(FIELD, F32), (FIELD, F32)],
-        (u, d, *local),
-        fine_scratch() + fine_scratch() + local_scratch(6),
-    )
-    (dense,) = call(
-        route_corners_kernel,
-        [((128, 1280), F32)],
-        (res, lin, quad, inside, owner, part),
-        [pltpu.VMEM((1152, 1024), BF16), pltpu.VMEM((1024, 256), BF16)],
-    )
-    parts = lax.all_to_all(dense, BOTH, 0, 0, tiled=True)
-    u, d = call(store_kernel, [(FIELD, F32), (FIELD, F32)], (u, d, slot))
-    total = jnp.sum(parts, axis=0, keepdims=True)
+        (u, d, slot),
+        [pltpu.VMEM(FIELD, F32), pltpu.VMEM(FIELD, F32), pltpu.SemaphoreType.DMA((6,))],
+        hbm_out={0, 1},
+        free=True,
+    )
     out, coarse = call(
-        end_kernel, [(FIELD, F32), ((1, 512), F32)], (u, d, total), hbm_out={0}
-    )
-    return out.reshape(3, 512, 128), coarse[0, :408].reshape(3, 136)
+        end_kernel,
+        [(FIELD, F32), ((3, 136), F32)],
+        (u, d, parts),
+        [
+            pltpu.VMEM(FIELD, F32),
+            pltpu.VMEM(FIELD, F32),
+            pltpu.VMEM((128, 1, 1280), F32),
+            pltpu.VMEM(FIELD, F32),
+            pltpu.SemaphoreType.DMA((10,)),
+        ],
+        spaces={0: pltpu.HBM, 1: pltpu.HBM, 2: pltpu.HBM},
+        hbm_out={0},
+    )
+    return out.reshape(3, 512, 128), coarse
 
 
 def solution(mesh):

time: 167 us -> 157 us (0.940)
  waiting for transfers between devices: 38 us -> 33.1 us
  starting transfers between devices: 45.8 us -> 43.1 us
  local copies, waits for them, and re-layouts: 5.35 us -> 2.75 us
    ppermute x20, waiting for transfers between devices: 24.9 us -> 20.3 us  [both_ways(): return (lax.ppermute(to_next, axis, up), lax.ppermute(to_prev, axis, down))]
    all_to_all x1, starting transfers between devices: 9.79 us -> 7.64 us  [shards(): parts = lax.all_to_all(dense, BOTH, 0, 0, tiled=True)]
    pallas_call x20 -> x22, Pallas kernels: 55.1 us -> 56.6 us  [call(): pl.pallas_call(kernel, out_shape=[(pltpu.HBM if i in hbm_out else pltpu.V...]
  transfers between devices with their start and end apart: 21 -> 21, of which waited for: 16 -> 14; matrix products, arithmetic and copies ran while one was open for 0% -> 0% of each run, Pallas kernels for 4% -> 9%
where the time goes in v3:
time: 157 us
  Pallas kernels  56.6 us (36%)
  starting transfers between devices  43.1 us (27%)
  waiting for transfers between devices  33.1 us (21%)
  blocking collectives  19.7 us (13%)
  local copies, waits for them, and re-layouts  2.75 us (2%)
    pallas_call x22, Pallas kernels, call(): pl.pallas_call(kernel, out_shape=[(pltpu.HBM if i in hbm_out else pltpu.V...  56.6 us
    ppermute x20, starting transfers between devices, both_ways(): return (lax.ppermute(to_next, axis, up), lax.ppermute(to_prev, axis, down))  35.4 us
    ppermute x20, waiting for transfers between devices, both_ways(): return (lax.ppermute(to_next, axis, up), lax.ppermute(to_prev, axis, down))  20.3 us
    all_to_all x1, blocking collectives, shards(): sums = lax.all_to_all(part, BOTH, 0, 0, tiled=True)  19.7 us
    all_to_all x1, waiting for transfers between devices, shards(): parts = lax.all_to_all(dense, BOTH, 0, 0, tiled=True)  12.8 us
    all_to_all x1, starting transfers between devices, shards(): parts = lax.all_to_all(dense, BOTH, 0, 0, tiled=True)  7.64 us
  transfers between devices with their start and end apart: 21, of which 14 were waited for; matrix products, arithmetic and copies ran while one was open for 0% of the time, Pallas kernels for 9%

profile of v3, /device:TPU:1, one launch (start us, length us, event | category | flops | bytes accessed | tf_op | source)
XLA Modules:
  0.0 156.8 jit_solution(2622237126384038647)
XLA Ops:
  1.3 0.6 copy-done.3
  2.0 0.7 copy-done.4
  2.6 3.3 %start_kernel.1 = (f32[3,8,64,128]{3,2,1,0:T(8,128)S(1)}, f32[3,8,128]{2,1,0:T(8,128)S(1)}, f32[3,8,128]{2,1,0:T(8,128)S(1)}, f32[16,256]{1,0:T(8,128)S(1)}, bf1...) custom-call(f32[3,8,64,128]{3,2,1,0:T(8,128)} %bitcast.10, ...), custom_call_target="tpu_custom_call" | custom-call | tf_op jit(solution)/shard_map/start_kernel/pallas_call | solution.py:117
  5.9 2.6 %collective-permute-start = (f32[3,8,128]{2,1,0:T(8,128)S(1)}, f32[3,8,128]{2,1,0:T(8,128)S(1)}, u32[]{:S(2)}, u32[]{:S(2)}) collective-permute-start(f32[3,8,128]{2,1,0:T(8,128)S(1)} %get-tuple-element.74), channel_id=1, source_target_pairs={{0,1},{1,2},{2,3},{3,4},{4,5},{5,6},{6,7},{7,0},{8,9},{9,10},{10,1... | collective-permute-start | bytes 36872 | tf_op jit(solution)/shard_map/ppermute | solution.py:901
  8.5 0.8 collective-permute-done.tlo
  9.4 2.3 %collective-permute-done.1.thi = f32[3,8,128]{2,1,0:T(8,128)S(1)} collective-permute-done((f32[3,8,128]{2,1,0:T(8,128)S(1)}, f32[3,8,128]{2,1,0:T(8,128)S(1)}, u32[]{:S(2)}, u32[]{:S(2)}) %collective-permute-start.1) | collective-permute-done | bytes 12320 | tf_op jit(solution)/shard_map/ppermute | solution.py:901
  12.0 1.4 collective-permute-start.2
  13.3 5.0 %collective-permute-start.3 = (f32[200,128]{1,0:T(8,128)S(1)}, f32[200,128]{1,0:T(8,128)S(1)}, u32[]{:S(2)}, u32[]{:S(2)}) collective-permute-start(f32[200,128]{1,0:T(8,128)S(1)} %get-tuple-element.79), channel_id=1, source_target_pairs={{8,0},{16,8},{24,16},{32,24},{40,32},{48,40},{56,48},{64,56},{72,6... | collective-permute-start | bytes 307208 | tf_op jit(solution)/shard_map/ppermute | solution.py:901
  18.3 3.0 %collective-permute-done.2.zlo = f32[200,128]{1,0:T(8,128)S(1)} collective-permute-done((f32[200,128]{1,0:T(8,128)S(1)}, f32[200,128]{1,0:T(8,128)S(1)}, u32[]{:S(2)}, u32[]{:S(2)}) %collective-permute-start.2) | collective-permute-done | bytes 102432 | tf_op jit(solution)/shard_map/ppermute | solution.py:901
  21.4 6.1 %project_kernel.1 = (f32[3,8,64,128]{3,2,1,0:T(8,128)S(1)}, f32[3,8,64,128]{3,2,1,0:T(8,128)S(1)}, f32[3,16,128]{2,1,0:T(8,128)S(1)}, f32[3,16,128]{2,1,0:T(8,128)S(1)}) custom-call(f32[3,8,64,128]{3,2,1,0:T(8,128)S(1)} %get-tuple-element.77.field, f32[200,128]{1,0:T(8,128)S(1)} %collective-permute-done.2.zlo, f32[200,128]{1,0:T(8,128)S(1)} %collective-permute-done.3.zhi, ...), custom_call_target="tpu_custom_call" | custom-call | tf_op jit(solution)/shard_map/project_kernel/pallas_call | solution.py:117
  27.5 0.7 collective-permute-start.5
  28.2 0.7 collective-permute-done.4.tlo
  28.9 1.9 %collective-permute-done.5.thi = f32[3,16,128]{2,1,0:T(8,128)S(1)} collective-permute-done((f32[3,16,128]{2,1,0:T(8,128)S(1)}, f32[3,16,128]{2,1,0:T(8,128)S(1)}, u32[]{:S(2)}, u32[]{:S(2)}) %collective-permute-start.5) | collective-permute-done | bytes 24608 | tf_op jit(solution)/shard_map/ppermute | solution.py:901
  31.2 5.8 %collective-permute-start.7 = (f32[3,2,72,128]{3,2,1,0:T(8,128)S(1)}, f32[3,2,72,128]{3,2,1,0:T(8,128)S(1)}, u32[]{:S(2)}, u32[]{:S(2)}) collective-permute-start(f32[3,2,72,128]{3,2,1,0:T(8,128)S(1)} %get-tuple-element.91), channel_id=1, source_target_pairs={{8,0},{16,8},{24,16},{32,24},{40,32},{48,40},{56,48},{64,56},{72,6... | collective-permute-start | bytes 663560 | tf_op jit(solution)/shard_map/ppermute | solution.py:901
  37.0 1.3 solve_tables_kernel.1
  38.3 3.5 %transform_kernel.2.own = f32[3,10,112,128]{3,2,1,0:T(8,128)S(1)} custom-call(f32[3,8,72,128]{3,2,1,0:T(8,128)S(1)} %get-tuple-element.92.field, bf16[112,480]{1,0:T(8,128)(2,1)S(1)} %get-tuple-element.93.forward, f32[10,10]{1,0:T(8,128)S(1)} %copy-done), custom_call_target="tpu_custom_call" | custom-call | tf_op jit(solution)/shard_map/transform_kernel/pallas_call | solution.py:117
  41.9 4.4 %solve_kernel.2 = (f32[3,8,64,128]{3,2,1,0:T(8,128)S(1)}, f32[3,8,128]{2,1,0:T(8,128)S(1)}, f32[3,8,128]{2,1,0:T(8,128)S(1)}) custom-call(f32[3,10,112,128]{3,2,1,0:T(8,128)S(1)} %transform_kernel.2.own, f32[3,2,72,128]{3,2,1,0:T(8,128)S(1)} %collective-permute-done.6.zlo, f32[3,2,72,128]{3,2,1,0:T(8,128)S(1)} %collective-permute-done.7.zhi, ...), custom_call_target="tpu_custom_call" | custom-call | tf_op jit(solution)/shard_map/solve_kernel/pallas_call | solution.py:117
  46.5 1.3 collective-permute-start.9
  47.8 0.6 collective-permute-done.8.tlo
  48.5 1.2 collective-permute-done.9.thi
  50.1 5.5 %collective-permute-start.11 = (f32[200,128]{1,0:T(8,128)S(1)}, f32[200,128]{1,0:T(8,128)S(1)}, u32[]{:S(2)}, u32[]{:S(2)}) collective-permute-start(f32[200,128]{1,0:T(8,128)S(1)} %get-tuple-element.104), channel_id=1, source_target_pairs={{8,0},{16,8},{24,16},{32,24},{40,32},{48,40},{56,48},{64,56},{72,6... | collective-permute-start | bytes 307208 | tf_op jit(solution)/shard_map/ppermute | solution.py:901
  55.6 2.0 %collective-permute-done.10.zlo = f32[200,128]{1,0:T(8,128)S(1)} collective-permute-done((f32[200,128]{1,0:T(8,128)S(1)}, f32[200,128]{1,0:T(8,128)S(1)}, u32[]{:S(2)}, u32[]{:S(2)}) %collective-permute-start.10) | collective-permute-done | bytes 102432 | tf_op jit(solution)/shard_map/ppermute | solution.py:901
  57.6 2.2 %direction_kernel.2 = (f32[3,8,64,128]{3,2,1,0:T(8,128)S(1)}, f32[128,128]{1,0:T(8,128)S(1)}) custom-call(f32[3,8,64,128]{3,2,1,0:T(8,128)S(1)} %get-tuple-element.102.field, f32[200,128]{1,0:T(8,128)S(1)} %collective-permute-done.10.zlo, f32[200,128]{1,0:T(8,128)S(1)} %collective-permute-done.11.zhi, f32[3,8,64,128]{3,2,1,0:T(8,128)S(1)} %get-tuple-element.87.res, ...), custom_call_target="tpu_custom_call" | custom-call | tf_op jit(solution)/shard_map/direction_kernel/pallas_call | solution.py:117
  59.8 19.7 %all_to_all.16 = f32[128,1,128]{2,1,0:T(1,128)S(1)} all-to-all(f32[128,1,128]{2,1,0:T(1,128)S(1)} %bitcast.8), channel_id=1, replica_groups=mesh['wide'=16,'narrow'=8] {'wide','narrow'}, dimensions={0} | all-to-all | bytes 131072 | tf_op jit(solution)/shard_map/all_to_all | solution.py:969
  79.5 6.5 %advance_kernel.1 = (f32[3,8,64,128]{3,2,1,0:T(8,128)S(1)}, f32[3,8,64,128]{3,2,1,0:T(8,128)S(1)}, f32[3,16,128]{2,1,0:T(8,128)S(1)}, f32[3,16,128]{2,1,0:T(8,128)S(1)}) custom-call(f32[3,8,64,128]{3,2,1,0:T(8,128)S(1)} %get-tuple-element.86.u_old, f32[3,8,64,128]{3,2,1,0:T(8,128)S(1)} %get-tuple-element.108.d, f32[128,128]{1,0:T(8,128)S(1)} %bitcast.7, ...), custom_call_target="tpu_custom_call" | custom-call | tf_op jit(solution)/shard_map/advance_kernel/pallas_call | solution.py:117
  86.0 1.0 collective-permute-start.12
  86.9 0.9 collective-permute-done.12.tlo
  87.9 2.6 %collective-permute-done.13.thi = f32[3,16,128]{2,1,0:T(8,128)S(1)} collective-permute-done((f32[3,16,128]{2,1,0:T(8,128)S(1)}, f32[3,16,128]{2,1,0:T(8,128)S(1)}, u32[]{:S(2)}, u32[]{:S(2)}) %collective-permute-start.13) | collective-permute-done | bytes 24608 | tf_op jit(solution)/shard_map/ppermute | solution.py:901
  90.5 0.3 around_widen_kernel.3
  91.1 4.6 %collective-permute-start.15 = (f32[3,2,72,128]{3,2,1,0:T(8,128)S(1)}, f32[3,2,72,128]{3,2,1,0:T(8,128)S(1)}, u32[]{:S(2)}, u32[]{:S(2)}) collective-permute-start(f32[3,2,72,128]{3,2,1,0:T(8,128)S(1)} %get-tuple-element.115), channel_id=1, source_target_pairs={{8,0},{16,8},{24,16},{32,24},{40,32},{48,40},{56,48},{64,56},{72,6... | collective-permute-start | bytes 663560 | tf_op jit(solution)/shard_map/ppermute | solution.py:901
  95.7 3.5 %transform_kernel.3.own = f32[3,10,112,128]{3,2,1,0:T(8,128)S(1)} custom-call(f32[3,8,72,128]{3,2,1,0:T(8,128)S(1)} %get-tuple-element.116.field, bf16[112,480]{1,0:T(8,128)(2,1)S(1)} %get-tuple-element.93.forward, f32[10,10]{1,0:T(8,128)S(1)} %copy-done), custom_call_target="tpu_custom_call" | custom-call | tf_op jit(solution)/shard_map/transform_kernel/pallas_call | solution.py:117
  99.2 1.2 collective-permute-done.14.zlo
  100.4 4.4 %solve_kernel.3 = (f32[3,8,64,128]{3,2,1,0:T(8,128)S(1)}, f32[3,8,128]{2,1,0:T(8,128)S(1)}, f32[3,8,128]{2,1,0:T(8,128)S(1)}) custom-call(f32[3,10,112,128]{3,2,1,0:T(8,128)S(1)} %transform_kernel.3.own, f32[3,2,72,128]{3,2,1,0:T(8,128)S(1)} %collective-permute-done.14.zlo, f32[3,2,72,128]{3,2,1,0:T(8,128)S(1)} %collective-permute-done.15.zhi, ...), custom_call_target="tpu_custom_call" | custom-call | tf_op jit(solution)/shard_map/solve_kernel/pallas_call | solution.py:117
  104.9 1.5 collective-permute-start.16
  106.5 0.7 collective-permute-done.16.tlo
  107.2 2.3 %collective-permute-done.17.thi = f32[3,8,128]{2,1,0:T(8,128)S(1)} collective-permute-done((f32[3,8,128]{2,1,0:T(8,128)S(1)}, f32[3,8,128]{2,1,0:T(8,128)S(1)}, u32[]{:S(2)}, u32[]{:S(2)}) %collective-permute-start.17) | collective-permute-done | bytes 12320 | tf_op jit(solution)/shard_map/ppermute | solution.py:901
  109.9 5.2 %collective-permute-start.19 = (f32[200,128]{1,0:T(8,128)S(1)}, f32[200,128]{1,0:T(8,128)S(1)}, u32[]{:S(2)}, u32[]{:S(2)}) collective-permute-start(f32[200,128]{1,0:T(8,128)S(1)} %get-tuple-element.125), channel_id=1, source_target_pairs={{8,0},{16,8},{24,16},{32,24},{40,32},{48,40},{56,48},{64,56},{72,6... | collective-permute-start | bytes 307208 | tf_op jit(solution)/shard_map/ppermute | solution.py:901
  115.1 0.5 route_kernel.1
  115.9 2.9 %fields_kernel.1 = (f32[6,3,432,256]{3,2,1,0:T(8,128)S(1)}, f32[6,3,144,256]{3,2,1,0:T(8,128)S(1)}) custom-call(f32[3,8,64,128]{3,2,1,0:T(8,128)S(1)} %get-tuple-element.110.u, bf16[432,256]{1,0:T(8,128)(2,1)S(1)} %get-tuple-element.82.fine), custom_call_target="tpu_custom_call" | custom-call | tf_op jit(solution)/shard_map/fields_kernel/pallas_call | solution.py:117
  118.8 2.3 %direction_kernel.3 = (f32[3,8,64,128]{3,2,1,0:T(8,128)S(1)}, f32[128,128]{1,0:T(8,128)S(1)}) custom-call(f32[3,8,64,128]{3,2,1,0:T(8,128)S(1)} %get-tuple-element.123.field, f32[200,128]{1,0:T(8,128)S(1)} %collective-permute-done.18.zlo, f32[200,128]{1,0:T(8,128)S(1)} %collective-permute-done.19.zhi, f32[3,8,64,128]{3,2,1,0:T(8,128)S(1)} %get-tuple-element.111.res, ...), custom_call_target="tpu_custom_call" | custom-call | tf_op jit(solution)/shard_map/direction_kernel/pallas_call | solution.py:117
  121.1 6.1 %change_kernel.1.change = f32[6,8,256]{2,1,0:T(8,128)S(1)} custom-call(f32[3,8,64,128]{3,2,1,0:T(8,128)S(1)} %get-tuple-element.132.d, f32[6,3,432,256]{3,2,1,0:T(8,128)S(1)} %get-tuple-element.136.pf, f32[6,3,144,256]{3,2,1,0:T(8,128)S(1)} %get-tuple-element.137.qf, f32[16,256]{1,0:T(8,128)S(1)} %get-tuple-element.76.lanes, ...), custom_call_target="tpu_custom_call" | custom-call | tf_op jit(solution)/shard_map/change_kernel/pallas_call | solution.py:117
  127.2 2.7 %place_kernel.1 = f32[128,1,1280]{2,1,0:T(1,128)} custom-call(f32[3,8,256]{2,1,0:T(8,128)S(1)} %corners_kernel.1.base, f32[6,8,256]{2,1,0:T(8,128)S(1)} %change_kernel.1.change, bf16[1024,256]{1,0:T(8,128)(2,1)S(1)} %get-tuple-element.139.right, s32[8,128]{1,0:T(8,128)S(1)} %get-tuple-element.140.owner, f32[128,128]{1,0:T(8,128)S(1)} %get-tuple-element.141.part), custom_call_target="tpu_custom_call" | custom-call | tf_op jit(solution)/shard_map/place_kernel/pallas_call | solution.py:117
  129.9 7.6 %all-to-all-start.1 = ((f32[128,1,1280]{2,1,0:T(1,128)}), f32[128,1,1280]{2,1,0:T(1,128)S(1)}, u32[]{:S(2)}, u32[]{:S(2)}) async-start(f32[128,1,1280]{2,1,0:T(1,128)} %place_kernel.1), calls=%async_computation.1 | async-start | bytes 1310720 | tf_op jit(solution)/shard_map/all_to_all | solution.py:1043
  137.5 2.3 %store_kernel.1 = (f32[3,8,64,128]{3,2,1,0:T(8,128)}, f32[3,8,64,128]{3,2,1,0:T(8,128)}) custom-call(f32[3,8,64,128]{3,2,1,0:T(8,128)S(1)} %get-tuple-element.110.u, f32[3,8,64,128]{3,2,1,0:T(8,128)S(1)} %get-tuple-element.132.d, s32[1,128]{1,0:T(1,128)S(1)} %copy-done.1), custom_call_target="tpu_custom_call" | custom-call | tf_op jit(solution)/shard_map/store_kernel/pallas_call | solution.py:117
  139.8 12.8 %all-to-all-done.1.parts_hbm = f32[128,1,1280]{2,1,0:T(1,128)S(1)} async-done(((f32[128,1,1280]{2,1,0:T(1,128)}), f32[128,1,1280]{2,1,0:T(1,128)S(1)}, u32[]{:S(2)}, u32[]{:S(2)}) %all-to-all-start.1) | async-done | bytes 655392 | tf_op jit(solution)/shard_map/all_to_all | solution.py:1043
  152.7 0.8 copy-done.6
  153.5 2.7 %end_kernel.1 = (f32[3,8,64,128]{3,2,1,0:T(8,128)}, f32[3,136]{1,0:T(4,128)S(1)}) custom-call(f32[3,8,64,128]{3,2,1,0:T(8,128)} %get-tuple-element.133.u_hbm, f32[3,8,64,128]{3,2,1,0:T(8,128)} %get-tuple-element.134.d_hbm, f32[128,1,1280]{2,1,0:T(1,128)} %copy-done.6), custom_call_target="tpu_custom_call" | custom-call | tf_op jit(solution)/shard_map/end_kernel/pallas_call | solution.py:117
  156.2 0.6 copy.17
  (32 shorter events, 2.6 us)
Async XLA Ops:
  0.6 36.4 %copy-start = (f32[10,10]{1,0:T(8,128)S(1)}, f32[10,10]{1,0:T(8,128)}, u32[]{:S(2)}) copy-start(f32[10,10]{1,0:T(8,128)} %vectors.9) | copy-start | bytes 1204
  1.3 0.7 copy-start.3
  2.0 0.7 copy-start.4
  2.6 34.4 %copy-start.5 = (f32[10]{0:T(128)S(1)}, f32[10]{0:T(128)}, u32[]{:S(2)}) copy-start(f32[10]{0:T(128)} %param.21) | copy-start | bytes 124
  5.9 3.4 %collective-permute-start = (f32[3,8,128]{2,1,0:T(8,128)S(1)}, f32[3,8,128]{2,1,0:T(8,128)S(1)}, u32[]{:S(2)}, u32[]{:S(2)}) collective-permute-start(f32[3,8,128]{2,1,0:T(8,128)S(1)} %get-tuple-element.74), channel_id=1, source_target_pairs={{0,1},{1,2},{2,3},{3,4},{4,5},{5,6},{6,7},{7,0},{8,9},{9,10},{10,1... | collective-permute-start | bytes 36872 | tf_op jit(solution)/shard_map/ppermute | solution.py:901
  8.5 3.1 %collective-permute-start.1 = (f32[3,8,128]{2,1,0:T(8,128)S(1)}, f32[3,8,128]{2,1,0:T(8,128)S(1)}, u32[]{:S(2)}, u32[]{:S(2)}) collective-permute-start(f32[3,8,128]{2,1,0:T(8,128)S(1)} %get-tuple-element.75), channel_id=1, source_target_pairs={{1,0},{2,1},{3,2},{4,3},{5,4},{6,5},{7,6},{0,7},{9,8},{10,9},{11,1... | collective-permute-start | bytes 36872 | tf_op jit(solution)/shard_map/ppermute | solution.py:901
  12.0 9.4 %collective-permute-start.2 = (f32[200,128]{1,0:T(8,128)S(1)}, f32[200,128]{1,0:T(8,128)S(1)}, u32[]{:S(2)}, u32[]{:S(2)}) collective-permute-start(f32[200,128]{1,0:T(8,128)S(1)} %get-tuple-element.78), channel_id=1, source_target_pairs={{0,8},{8,16},{16,24},{24,32},{32,40},{40,48},{48,56},{56,64},{64,7... | collective-permute-start | bytes 307208 | tf_op jit(solution)/shard_map/ppermute | solution.py:901
  13.3 8.0 %collective-permute-start.3 = (f32[200,128]{1,0:T(8,128)S(1)}, f32[200,128]{1,0:T(8,128)S(1)}, u32[]{:S(2)}, u32[]{:S(2)}) collective-permute-start(f32[200,128]{1,0:T(8,128)S(1)} %get-tuple-element.79), channel_id=1, source_target_pairs={{8,0},{16,8},{24,16},{32,24},{40,32},{48,40},{56,48},{64,56},{72,6... | collective-permute-start | bytes 307208 | tf_op jit(solution)/shard_map/ppermute | solution.py:901
  27.5 1.4 collective-permute-start.4
  27.5 3.3 %collective-permute-start.5 = (f32[3,16,128]{2,1,0:T(8,128)S(1)}, f32[3,16,128]{2,1,0:T(8,128)S(1)}, u32[]{:S(2)}, u32[]{:S(2)}) collective-permute-start(f32[3,16,128]{2,1,0:T(8,128)S(1)} %get-tuple-element.89), channel_id=1, source_target_pairs={{1,0},{2,1},{3,2},{4,3},{5,4},{6,5},{7,6},{0,7},{9,8},{10,9},{11,1... | collective-permute-start | bytes 73736 | tf_op jit(solution)/shard_map/ppermute | solution.py:901
  31.1 10.7 %collective-permute-start.6 = (f32[3,2,72,128]{3,2,1,0:T(8,128)S(1)}, f32[3,2,72,128]{3,2,1,0:T(8,128)S(1)}, u32[]{:S(2)}, u32[]{:S(2)}) collective-permute-start(f32[3,2,72,128]{3,2,1,0:T(8,128)S(1)} %get-tuple-element.90), channel_id=1, source_target_pairs={{0,8},{8,16},{16,24},{24,32},{32,40},{40,48},{48,56},{56,64},{64,7... | collective-permute-start | bytes 663560 | tf_op jit(solution)/shard_map/ppermute | solution.py:901
  31.2 10.6 %collective-permute-start.7 = (f32[3,2,72,128]{3,2,1,0:T(8,128)S(1)}, f32[3,2,72,128]{3,2,1,0:T(8,128)S(1)}, u32[]{:S(2)}, u32[]{:S(2)}) collective-permute-start(f32[3,2,72,128]{3,2,1,0:T(8,128)S(1)} %get-tuple-element.91), channel_id=1, source_target_pairs={{8,0},{16,8},{24,16},{32,24},{40,32},{48,40},{56,48},{64,56},{72,6... | collective-permute-start | bytes 663560 | tf_op jit(solution)/shard_map/ppermute | solution.py:901
  46.3 2.2 %collective-permute-start.8 = (f32[3,8,128]{2,1,0:T(8,128)S(1)}, f32[3,8,128]{2,1,0:T(8,128)S(1)}, u32[]{:S(2)}, u32[]{:S(2)}) collective-permute-start(f32[3,8,128]{2,1,0:T(8,128)S(1)} %get-tuple-element.100), channel_id=1, source_target_pairs={{0,1},{1,2},{2,3},{3,4},{4,5},{5,6},{6,7},{7,0},{8,9},{9,10},{10,1... | collective-permute-start | bytes 36872 | tf_op jit(solution)/shard_map/ppermute | solution.py:901
  46.5 3.1 %collective-permute-start.9 = (f32[3,8,128]{2,1,0:T(8,128)S(1)}, f32[3,8,128]{2,1,0:T(8,128)S(1)}, u32[]{:S(2)}, u32[]{:S(2)}) collective-permute-start(f32[3,8,128]{2,1,0:T(8,128)S(1)} %get-tuple-element.101), channel_id=1, source_target_pairs={{1,0},{2,1},{3,2},{4,3},{5,4},{6,5},{7,6},{0,7},{9,8},{10,9},{11,1... | collective-permute-start | bytes 36872 | tf_op jit(solution)/shard_map/ppermute | solution.py:901
  50.0 7.6 %collective-permute-start.10 = (f32[200,128]{1,0:T(8,128)S(1)}, f32[200,128]{1,0:T(8,128)S(1)}, u32[]{:S(2)}, u32[]{:S(2)}) collective-permute-start(f32[200,128]{1,0:T(8,128)S(1)} %get-tuple-element.103), channel_id=1, source_target_pairs={{0,8},{8,16},{16,24},{24,32},{32,40},{40,48},{48,56},{56,64},{64,7... | collective-permute-start | bytes 307208 | tf_op jit(solution)/shard_map/ppermute | solution.py:901
  50.1 7.5 %collective-permute-start.11 = (f32[200,128]{1,0:T(8,128)S(1)}, f32[200,128]{1,0:T(8,128)S(1)}, u32[]{:S(2)}, u32[]{:S(2)}) collective-permute-start(f32[200,128]{1,0:T(8,128)S(1)} %get-tuple-element.104), channel_id=1, source_target_pairs={{8,0},{16,8},{24,16},{32,24},{40,32},{48,40},{56,48},{64,56},{72,6... | collective-permute-start | bytes 307208 | tf_op jit(solution)/shard_map/ppermute | solution.py:901
  86.0 1.9 %collective-permute-start.12 = (f32[3,16,128]{2,1,0:T(8,128)S(1)}, f32[3,16,128]{2,1,0:T(8,128)S(1)}, u32[]{:S(2)}, u32[]{:S(2)}) collective-permute-start(f32[3,16,128]{2,1,0:T(8,128)S(1)} %get-tuple-element.112), channel_id=1, source_target_pairs={{0,1},{1,2},{2,3},{3,4},{4,5},{5,6},{6,7},{7,0},{8,9},{9,10},{10,1... | collective-permute-start | bytes 73736 | tf_op jit(solution)/shard_map/ppermute | solution.py:901
  86.9 3.5 %collective-permute-start.13 = (f32[3,16,128]{2,1,0:T(8,128)S(1)}, f32[3,16,128]{2,1,0:T(8,128)S(1)}, u32[]{:S(2)}, u32[]{:S(2)}) collective-permute-start(f32[3,16,128]{2,1,0:T(8,128)S(1)} %get-tuple-element.113), channel_id=1, source_target_pairs={{1,0},{2,1},{3,2},{4,3},{5,4},{6,5},{7,6},{0,7},{9,8},{10,9},{11,1... | collective-permute-start | bytes 73736 | tf_op jit(solution)/shard_map/ppermute | solution.py:901
  90.8 9.6 %collective-permute-start.14 = (f32[3,2,72,128]{3,2,1,0:T(8,128)S(1)}, f32[3,2,72,128]{3,2,1,0:T(8,128)S(1)}, u32[]{:S(2)}, u32[]{:S(2)}) collective-permute-start(f32[3,2,72,128]{3,2,1,0:T(8,128)S(1)} %get-tuple-element.114), channel_id=1, source_target_pairs={{0,8},{8,16},{16,24},{24,32},{32,40},{40,48},{48,56},{56,64},{64,7... | collective-permute-start | bytes 663560 | tf_op jit(solution)/shard_map/ppermute | solution.py:901
  91.1 9.3 %collective-permute-start.15 = (f32[3,2,72,128]{3,2,1,0:T(8,128)S(1)}, f32[3,2,72,128]{3,2,1,0:T(8,128)S(1)}, u32[]{:S(2)}, u32[]{:S(2)}) collective-permute-start(f32[3,2,72,128]{3,2,1,0:T(8,128)S(1)} %get-tuple-element.115), channel_id=1, source_target_pairs={{8,0},{16,8},{24,16},{32,24},{40,32},{48,40},{56,48},{64,56},{72,6... | collective-permute-start | bytes 663560 | tf_op jit(solution)/shard_map/ppermute | solution.py:901
  95.7 19.4 %copy-start.1 = (s32[1,128]{1,0:T(1,128)S(1)}, s32[1,128]{1,0:T(1,128)}, u32[]{:S(2)}) copy-start(s32[1,128]{1,0:T(1,128)} %slot.3) | copy-start | bytes 1540
  95.7 19.4 %copy-start.2 = (s32[8,128]{1,0:T(8,128)S(1)}, s32[8,128]{1,0:T(8,128)}, u32[]{:S(2)}) copy-start(s32[8,128]{1,0:T(8,128)} %corner.1) | copy-start | bytes 12292
  104.9 2.4 %collective-permute-start.16 = (f32[3,8,128]{2,1,0:T(8,128)S(1)}, f32[3,8,128]{2,1,0:T(8,128)S(1)}, u32[]{:S(2)}, u32[]{:S(2)}) collective-permute-start(f32[3,8,128]{2,1,0:T(8,128)S(1)} %get-tuple-element.121), channel_id=1, source_target_pairs={{0,1},{1,2},{2,3},{3,4},{4,5},{5,6},{6,7},{7,0},{8,9},{9,10},{10,1... | collective-permute-start | bytes 36872 | tf_op jit(solution)/shard_map/ppermute | solution.py:901
  106.4 3.1 %collective-permute-start.17 = (f32[3,8,128]{2,1,0:T(8,128)S(1)}, f32[3,8,128]{2,1,0:T(8,128)S(1)}, u32[]{:S(2)}, u32[]{:S(2)}) collective-permute-start(f32[3,8,128]{2,1,0:T(8,128)S(1)} %get-tuple-element.122), channel_id=1, source_target_pairs={{1,0},{2,1},{3,2},{4,3},{5,4},{6,5},{7,6},{0,7},{9,8},{10,9},{11,1... | collective-permute-start | bytes 36872 | tf_op jit(solution)/shard_map/ppermute | solution.py:901
  109.9 9.0 %collective-permute-start.18 = (f32[200,128]{1,0:T(8,128)S(1)}, f32[200,128]{1,0:T(8,128)S(1)}, u32[]{:S(2)}, u32[]{:S(2)}) collective-permute-start(f32[200,128]{1,0:T(8,128)S(1)} %get-tuple-element.124), channel_id=1, source_target_pairs={{0,8},{8,16},{16,24},{24,32},{32,40},{40,48},{48,56},{56,64},{64,7... | collective-permute-start | bytes 307208 | tf_op jit(solution)/shard_map/ppermute | solution.py:901
  109.9 8.9 %collective-permute-start.19 = (f32[200,128]{1,0:T(8,128)S(1)}, f32[200,128]{1,0:T(8,128)S(1)}, u32[]{:S(2)}, u32[]{:S(2)}) collective-permute-start(f32[200,128]{1,0:T(8,128)S(1)} %get-tuple-element.125), channel_id=1, source_target_pairs={{8,0},{16,8},{24,16},{32,24},{40,32},{48,40},{56,48},{64,56},{72,6... | collective-permute-start | bytes 307208 | tf_op jit(solution)/shard_map/ppermute | solution.py:901
  129.9 22.8 %all-to-all-start.1 = ((f32[128,1,1280]{2,1,0:T(1,128)}), f32[128,1,1280]{2,1,0:T(1,128)S(1)}, u32[]{:S(2)}, u32[]{:S(2)}) async-start(f32[128,1,1280]{2,1,0:T(1,128)} %place_kernel.1), calls=%async_computation.1 | async-start | bytes 1310720 | tf_op jit(solution)/shard_map/all_to_all | solution.py:1043
  152.7 0.8 copy-start.6

commit v4 on v3

--- a/solution.py
+++ b/solution.py
@@ -218,17 +218,26 @@
 
 
 CONSTANTS = (FINE, BACK, STIFF_JK, GRAD_JK, COARSE_JK, WJK_ROWS)
-
-
-def start_kernel(vel_hbm, slot_hbm, arc, rad, axial, *refs):
-    n = len(CONSTANTS)
-    hbm, mv, low, high, lanes = refs[:n], *refs[n : n + 4]
-    held, (vel, slot, sems) = refs[n + 4 : 2 * n + 4], refs[2 * n + 4 :]
-    pairs = [(slot_hbm, slot)] + [(vel_hbm.at[c], vel.at[c]) for c in range(3)]
-    pairs += list(zip(hbm, held))
-    copies = [pltpu.make_async_copy(a, b, sems.at[i]) for i, (a, b) in enumerate(pairs)]
+NT = (((1,), (1,)), ((), ()))
+
+
+def faces_kernel(
+    vel_hbm, slot_hbm, arc_hbm, rad_hbm, axial, down, up, lanes, vel, slot, arc, rad, sems
+):
+    copies = [
+        pltpu.make_async_copy(arc_hbm, arc, sems.at[7]),
+        pltpu.make_async_copy(rad_hbm, rad, sems.at[8]),
+        pltpu.make_async_copy(slot_hbm, slot, sems.at[6]),
+    ]
+    for c in range(3):
+        for n in range(2):
+            copies.append(
+                pltpu.make_async_copy(vel_hbm.at[c, 7 * n], vel.at[n, c], sems.at[3 * n + c])
+            )
     for copy in copies:
         copy.start()
+    for copy in copies[:2]:
+        copy.wait()
     r = iota((1, 256), 1) & (RADIAL - 1)
     ht, hr = jnp.zeros((1, 256), F32), jnp.zeros((1, 256), F32)
     for i in range(RADIAL):
@@ -256,21 +265,64 @@
         lanes[n : n + 1] = row
     for n in range(len(rows), 16):
         lanes[n : n + 1] = jnp.zeros((1, 256), F32)
+    for copy in copies[2:]:
+        copy.wait()
+    hot = (slot[...] == iota((128, 128), 0)).astype(F32)
+    y = lax.dot_general(
+        vel[...].reshape(384, 128), hot, NT, precision=EXACT, preferred_element_type=F32
+    )
+    y = y * vol[:, :128]
+    for n, out in enumerate((down, up)):
+        out[0:192] = y[192 * n : 192 * n + 192]
+        out[192:200] = jnp.broadcast_to(hz[:, :128], (8, 128))
+
+
+def inner_kernel(vel_hbm, slot_hbm, lanes, *refs):
+    n = len(CONSTANTS)
+    hbm, mv, held, (vel, slot, sems) = refs[:n], refs[n], refs[n + 1 : 2 * n + 1], refs[2 * n + 1 :]
+    pairs = [(slot_hbm, slot)]
+    pairs += [(vel_hbm.at[c, pl.ds(1, 6)], vel.at[c]) for c in range(3)]
+    pairs += list(zip(hbm, held))
+    copies = [pltpu.make_async_copy(a, b, sems.at[i]) for i, (a, b) in enumerate(pairs)]
+    for copy in copies:
+        copy.start()
     copies[0].wait()
     hot = (slot[...] == iota((128, 128), 0)).astype(F32)
-    nt = (((1,), (1,)), ((), ()))
     for c in range(3):
         copies[1 + c].wait()
-        x = vel[c].reshape(512, 128)
-        y = lax.dot_general(x, hot, nt, precision=EXACT, preferred_element_type=F32)
-        mv[c] = (y * vol[:, :128]).reshape(8, 64, 128)
-        low[c] = pack_low(lambda i: mv[c, i, 0:8])
-        high[c] = pack_high(lambda i: mv[c, i, 56:64])
+        y = lax.dot_general(
+            vel[c].reshape(384, 128), hot, NT, precision=EXACT, preferred_element_type=F32
+        )
+        mv[c] = (y * lanes[0:1, :128]).reshape(6, 64, 128)
     for copy in copies[4:]:
         copy.wait()
 
 
-def solve_tables_kernel(vectors, values, lanes, forward, inverse, scale):
+def pipe_sum_kernel(mv, down, up, zlo, zhi, field, low, high):
+    def body(c, carry):
+        rows = pl.ds(pl.multiple_of(c * 64, 64), 64)
+        field[c, 0] = down[rows] + zlo[rows]
+        for i in range(6):
+            field[c, 1 + i] = mv[c, i]
+        field[c, 7] = up[rows] + zhi[rows]
+        low[c] = pack_low(lambda i: field[c, i, 0:8])
+        high[c] = pack_high(lambda i: field[c, i, 56:64])
+        return carry
+
+    lax.fori_loop(0, 3, body, 0)
+
+
+def solve_tables_kernel(
+    vectors_hbm, values_hbm, lanes, forward, inverse, scale, vectors, values, sems
+):
+    copies = [
+        pltpu.make_async_copy(vectors_hbm, vectors, sems.at[0]),
+        pltpu.make_async_copy(values_hbm, values, sems.at[1]),
+    ]
+    for copy in copies:
+        copy.start()
+    for copy in copies:
+        copy.wait()
     s = vectors[...]
     ident = (iota((10, 10), 0) == iota((10, 10), 1)).astype(F32)
     st = lax.dot_general(
@@ -580,12 +632,12 @@
 
 
 def project_kernel(
-    field, zlo, zhi, lanes, fine, back, stiff, wjk, u, res, low, high, *scratch
+    field, tlo, thi, hz_low, hz_high, lanes, fine, back, stiff, wjk, u, res, low, high, *scratch
 ):
     hz = lanes[7:8, :128]
     inner = 1.0 / hz
-    first = 1.0 / (hz + zlo[192:193])
-    last = 1.0 / (hz + zhi[192:193])
+    first = 1.0 / (hz + hz_low[192:193])
+    last = 1.0 / (hz + hz_high[192:193])
     k = iota((8, 128), 0)
     rk = jnp.where(
         k == 0, lanes[9:10, :128], jnp.where(k == 7, lanes[10:11, :128], lanes[8:9, :128])
@@ -594,11 +646,22 @@
     by_plane = {0: rk * first, 7: rk * last}
     middle = rk * inner
 
-    def factor(i, j):
-        f = by_plane.get(i, middle)
-        return 0.5 * f if j in (0, 7) else f
-
-    finish_sum(field, zlo, zhi, u, factor)
+    def body(c, carry):
+        lo, hi = tlo[c], thi[c]
+        for i in range(8):
+            x = field[c, i]
+            for j in range(8):
+                v = x[8 * j : 8 * j + 8]
+                f = by_plane.get(i, middle)
+                if j == 0:
+                    v, f = v + from_low(x[56:64], lo, i), 0.5 * f
+                if j == 7:
+                    v, f = v + from_high(x[0:8], hi, i), 0.5 * f
+                below, above = radial_parts(v)
+                u[c, i, 8 * j : 8 * j + 8] = radial_sum(v, below, above) * f
+        return carry
+
+    lax.fori_loop(0, 3, body, 0)
     residual(u, lanes, fine, back, stiff, wjk, res, *scratch)
     pack_two(res, low, high)
 
@@ -691,18 +754,13 @@
 def solve_kernel(
     own, zlo, zhi, vectors, forward, inverse, scale, corr, low, high, xf0, xf1, yf, xb
 ):
-    def body(c, carry):
-        for buf, halo in ((xf0, zlo), (xf1, zhi)):
-            widen_planes(halo[c, 0], buf, 0)
-            widen_planes(halo[c, 1], buf, 1)
-        y0, y1 = dot(forward[...], xf0[...]), dot(forward[...], xf1[...])
-        yf[c, 0] = y0[:, :128]
-        yf[c, 1] = y0[:, 128:]
-        yf[c, 2] = y1[:, :128]
-        yf[c, 3] = y1[:, 128:]
-        return carry
-
-    lax.fori_loop(0, 3, body, 0)
+    for c in range(3):
+        for n, (buf, halo) in enumerate(((xf0, zlo), (xf1, zhi))):
+            widen_planes(halo[c, 0], buf.at[c], 0)
+            widen_planes(halo[c, 1], buf.at[c], 1)
+            y = dot(forward[...], buf[c])
+            yf[c, 2 * n] = y[:, :128]
+            yf[c, 2 * n + 1] = y[:, 128:]
 
     def mid(rb, carry):
         rows = pl.ds(pl.multiple_of(rb * 16, 16), 16)
@@ -778,24 +836,18 @@
 
     lax.fori_loop(0, 12, first, 0)
 
-    def second(c, carry):
-        total = jnp.zeros((16, 128), F32)
-        for p in range(4):
-            y = dot(grad[...], xs[c * 4 + p])
-            for half in range(2):
-                v = y[:, half * 128 : half * 128 + 128]
-                v = v * v
-                plane = jnp.zeros((16, 128), F32)
-                for q in range(4):
-                    rows = slice(16 * q, 16 * q + 16)
-                    plane = plane + wjk[rows] * (
-                        kt * v[rows] + kr * v[64 + 16 * q : 80 + 16 * q]
-                    )
-                total = total + float(W[2 * p + half]) * plane
-        acc[1] += total
-        return carry
-
-    lax.fori_loop(0, 3, second, 0)
+    total = acc[1]
+    for t in range(12):
+        y = dot(grad[...], xs[t])
+        for half in range(2):
+            v = y[:, half * 128 : half * 128 + 128]
+            v = v * v
+            plane = jnp.zeros((16, 128), F32)
+            for q in range(4):
+                rows = slice(16 * q, 16 * q + 16)
+                plane = plane + wjk[rows] * (kt * v[rows] + kr * v[64 + 16 * q : 80 + 16 * q])
+            total = total + float(W[2 * (t % 4) + half]) * plane
+    acc[1] = total
     num = jnp.sum(jnp.sum(acc[0], axis=0, keepdims=True), axis=1, keepdims=True)
     den = jnp.sum(jnp.sum(acc[1], axis=0, keepdims=True), axis=1, keepdims=True)
     at = iota((128, 128), 1)
@@ -816,32 +868,39 @@
         right[128 * q : 128 * q + 128] = (inside[:, q : q + 1] == pos).astype(F32).astype(BF16)
 
 
-def place_kernel(base, change, right, owner, part, dense, left):
+def placed(values, right, owner, left):
     dev = iota((128, 128), 0)
+    for c, both in enumerate(values):
+        hi = both.astype(BF16).astype(F32)
+        for q in range(8):
+            mine = owner[q : q + 1] == dev
+            cols = slice((q // 4) * 128, (q // 4) * 128 + 128)
+            for m, piece in enumerate((hi, both - hi)):
+                at = (2 * c + m) * 128
+                left[at : at + 128, 128 * q : 128 * q + 128] = jnp.where(
+                    mine, piece[q % 4 : q % 4 + 1, cols], 0.0
+                ).astype(BF16)
+    y = dot(left[...], right[...])
+    return [y[256 * c : 256 * c + 128] + y[256 * c + 128 : 256 * c + 256] for c in range(3)]
+
+
+def place_base_kernel(base, right, owner, out, left):
+    for c, total in enumerate(placed([base[c] for c in range(3)], right, owner, left)):
+        out[c] = lanes_by(total, 8 * c)
+
+
+def place_kernel(base, change, right, owner, part, dense, left0, left1):
+    blocks = [base[c] for c in range(3)]
+    for n, left in enumerate((left0, left1)):
+        values = [change[3 * n + c] for c in range(3)]
+        for c, total in enumerate(placed(values, right, owner, left)):
+            blocks.append(lanes_by(total, 8 * (3 * n + 3 + c)))
     spill = None
-    for n in range(3):
-        for c in range(3):
-            both = base[c] if n == 0 else change[3 * (n - 1) + c]
-            hi = both.astype(BF16).astype(F32)
-            for q in range(8):
-                mine = owner[q : q + 1] == dev
-                cols = slice((q // 4) * 128, (q // 4) * 128 + 128)
-                for m, piece in enumerate((hi, both - hi)):
-                    at = (2 * c + m) * 128
-                    left[n, at : at + 128, 128 * q : 128 * q + 128] = jnp.where(
-                        mine, piece[q % 4 : q % 4 + 1, cols], 0.0
-                    ).astype(BF16)
-        y = dot(left[n], right[...])
-        for c in range(3):
-            block = 3 * n + c
-            total = lanes_by(y[256 * c : 256 * c + 128] + y[256 * c + 128 : 256 * c + 256],
-                             8 * block)
-            first = total[:, :128]
-            dense[:, 0, 128 * block : 128 * block + 128] = (
-                first if spill is None else first + spill
-            )
-            spill = total[:, 128:]
-    dense[:, 0, 1152:1280] = spill + lanes_by(part[...], 72)
+    for n, total in enumerate(blocks):
+        first = total[:, :128]
+        dense[pl.ds(n, 128, stride=10)] = first if spill is None else first + spill
+        spill = total[:, 128:]
+    dense[pl.ds(9, 128, stride=10)] = spill + lanes_by(part[...], 72)
 
 
 def store_kernel(u, d, slot, u_hbm, d_hbm, u_out, d_out, sems):
@@ -859,8 +918,8 @@
         copy.wait()
 
 
-def end_kernel(u_hbm, d_hbm, parts_hbm, vel_hbm, coarse, u, d, parts, vel, sems):
-    first = pltpu.make_async_copy(parts_hbm, parts, sems.at[0])
+def end_kernel(u_hbm, d_hbm, parts, vel_hbm, coarse_hbm, u, d, vel, coarse, sems):
+    last = pltpu.make_async_copy(coarse, coarse_hbm, sems.at[0])
     loads = [
         [
             pltpu.make_async_copy(a.at[c], b.at[c], sems.at[1 + 2 * c + n])
@@ -871,23 +930,25 @@
     stores = [
         pltpu.make_async_copy(vel.at[c], vel_hbm.at[c], sems.at[7 + c]) for c in range(3)
     ]
-    first.start()
     for pair in loads:
         for copy in pair:
             copy.start()
-    first.wait()
-    total = jnp.sum(parts[...], axis=0)
-    alpha = total[:, 1224:1225] / total[:, 1225:1226]
+    sums = [
+        jnp.sum(parts[pl.ds(n, 128, stride=10)], axis=0, keepdims=True) for n in range(10)
+    ]
+    alpha = sums[9][:, 72:73] / sums[9][:, 73:74]
     for c in range(3):
         for copy in loads[c]:
             copy.wait()
         vel[c] = u[c] + alpha * d[c]
         stores[c].start()
+    total = jnp.concatenate(sums, axis=1)
     one, two = lanes_by(total, -408), lanes_by(total, -816)
     both = total + alpha * (one + alpha * two)
     for c in range(3):
         coarse[c : c + 1] = lanes_by(both, -136 * c)[:, :136]
-    for copy in stores:
+    last.start()
+    for copy in (*stores, last):
         copy.wait()
 
 
@@ -922,27 +983,51 @@
 
 
 def shards(vel, slot, corner, axial, arc, rad, vectors, values):
-    smem = pltpu.SMEM
+    smem, hbm = pltpu.SMEM, pltpu.HBM
     small = ((3, 8, 128), F32)
     count = len(CONSTANTS)
-    mv, low, high, lanes, fine, back, stiff, grad, coarse_jk, wjk = call(
-        start_kernel,
-        [(FIELD, F32), small, small, ((16, 256), F32)] + [(m.shape, m.dtype) for m in CONSTANTS],
-        (vel.reshape(FIELD), slot, arc, rad, axial, *(jnp.asarray(m) for m in CONSTANTS)),
+    vel = vel.reshape(FIELD)
+    down, up, lanes = call(
+        faces_kernel,
+        [((200, 128), F32), ((200, 128), F32), ((16, 256), F32)],
+        (vel, slot, arc, rad, axial),
         [
-            pltpu.VMEM(FIELD, F32),
+            pltpu.VMEM((2, 3, 64, 128), F32),
+            pltpu.VMEM((1, 128), jnp.int32),
+            pltpu.SMEM((RADIAL,), F32),
+            pltpu.SMEM((RADIAL,), F32),
+            pltpu.SemaphoreType.DMA((9,)),
+        ],
+        spaces={0: hbm, 1: hbm, 2: hbm, 3: hbm, 4: smem},
+    )
+    zlo, zhi = both_ways("wide", up, down)
+    mv, fine, back, stiff, grad, coarse_jk, wjk = call(
+        inner_kernel,
+        [((3, 6, 64, 128), F32)] + [(m.shape, m.dtype) for m in CONSTANTS],
+        (vel, slot, lanes, *(jnp.asarray(m) for m in CONSTANTS)),
+        [
+            pltpu.VMEM((3, 6, 64, 128), F32),
             pltpu.VMEM((1, 128), jnp.int32),
             pltpu.SemaphoreType.DMA((4 + count,)),
         ],
-        spaces={
-            0: pltpu.HBM, 1: pltpu.HBM, 2: smem, 3: smem, 4: smem,
-            **{5 + i: pltpu.HBM for i in range(count)},
-        },
+        spaces={0: hbm, 1: hbm, **{3 + i: hbm for i in range(count)}},
+    )
+    zlo, zhi, mv, fine, back, stiff, grad, coarse_jk, wjk = lax.optimization_barrier(
+        (zlo, zhi, mv, fine, back, stiff, grad, coarse_jk, wjk)
+    )
+    field, low, high = call(
+        pipe_sum_kernel, [(FIELD, F32), small, small], (mv, down, up, zlo, zhi)
     )
     forward, inverse, scale = call(
         solve_tables_kernel,
         [((112, 480), BF16), ((64, 336), BF16), ((10, 112, 128), F32)],
         (vectors, values[None], lanes),
+        [
+            pltpu.VMEM((10, 10), F32),
+            pltpu.VMEM((1, 10), F32),
+            pltpu.SemaphoreType.DMA((2,)),
+        ],
+        spaces={0: hbm, 1: hbm},
     )
 
     def sum_rounds(field, low, high, beside=()):
@@ -961,7 +1046,7 @@
     u, res, low, high = call(
         project_kernel,
         packs,
-        (*sum_rounds(mv, low, high)[0], *local),
+        (field, *both_ways("narrow", high, low), zlo, zhi, *local),
         fine_scratch() + local_scratch(3),
     )
     for step in range(2):
@@ -994,8 +1079,8 @@
             [(FIELD, F32), small, small],
             (own, zlo, zhi, vectors, forward, inverse, scale),
             [
-                pltpu.VMEM((480, 256), BF16),
-                pltpu.VMEM((480, 256), BF16),
+                pltpu.VMEM((3, 480, 256), BF16),
+                pltpu.VMEM((3, 480, 256), BF16),
                 pltpu.VMEM((3, 4, 112, 128), F32),
                 pltpu.VMEM((12, 336, 256), BF16),
             ],
@@ -1004,16 +1089,20 @@
         beside = ()
         if step == 1:
             fields = [((6, 3, 432, 256), F32), ((6, 3, 144, 256), F32)]
-            beside = (
-                call(fields_kernel, fields, (u, fine), fine_scratch()[2:]),
-                call(corners_kernel, [((3, 8, 256), F32)], (res,)),
-                call(
-                    route_kernel,
-                    [((1024, 256), BF16), ((8, 128), jnp.int32)],
-                    (slot, corner),
-                    free=True,
-                ),
+            right, owner = call(
+                route_kernel,
+                [((1024, 256), BF16), ((8, 128), jnp.int32)],
+                (slot, corner),
+                free=True,
             )
+            (base,) = call(corners_kernel, [((3, 8, 256), F32)], (res,))
+            (base,) = call(
+                place_base_kernel,
+                [((3, 128, 256), F32)],
+                (base, right, owner),
+                [pltpu.VMEM((768, 1024), BF16)],
+            )
+            beside = (call(fields_kernel, fields, (u, fine), fine_scratch()[2:]), base)
         halo, beside = sum_rounds(corr, low, high, beside)
         d, part = call(
             direction_kernel,
@@ -1021,7 +1110,7 @@
             (*halo, res, lanes, grad, wjk),
             [pltpu.VMEM((12, 256, 256), BF16), pltpu.VMEM((2, 16, 128), F32)],
         )
-    (pf, qf), (base,), (right, owner) = beside
+    (pf, qf), base = beside
     (change,) = call(
         change_kernel,
         [((6, 8, 256), F32)],
@@ -1036,11 +1125,12 @@
     )
     (dense,) = call(
         place_kernel,
-        [((128, 1, 1280), F32)],
+        [((1280, 128), F32)],
         (base, change, right, owner, part),
-        [pltpu.VMEM((3, 768, 1024), BF16)],
-    )
-    parts = lax.all_to_all(dense, BOTH, 0, 0, tiled=True)
+        [pltpu.VMEM((768, 1024), BF16), pltpu.VMEM((768, 1024), BF16)],
+    )
+    parts = lax.all_to_all(dense.reshape(128, 1, 1280), BOTH, 0, 0, tiled=True)
+    parts = parts.reshape(1280, 128)
     u, d = call(
         store_kernel,
         [(FIELD, F32), (FIELD, F32)],
@@ -1056,12 +1146,12 @@
         [
             pltpu.VMEM(FIELD, F32),
             pltpu.VMEM(FIELD, F32),
-            pltpu.VMEM((128, 1, 1280), F32),
             pltpu.VMEM(FIELD, F32),
+            pltpu.VMEM((3, 136), F32),
             pltpu.SemaphoreType.DMA((10,)),
         ],
-        spaces={0: pltpu.HBM, 1: pltpu.HBM, 2: pltpu.HBM},
-        hbm_out={0},
+        spaces={0: pltpu.HBM, 1: pltpu.HBM},
+        hbm_out={0, 1},
     )
     return out.reshape(3, 512, 128), coarse
 

time: 157 us -> 151 us (0.962)
  local copies, waits for them, and re-layouts: 2.75 us -> 0.01 us
  waiting for transfers between devices: 33.1 us -> 30.5 us
    unnamed x15 -> x6, local copies, waits for them, and re-layouts: 2.75 us -> 0.01 us
    ppermute x20, waiting for transfers between devices: 20.3 us -> 17.7 us  [both_ways(): return (lax.ppermute(to_next, axis, up), lax.ppermute(to_prev, axis, down))]
    pallas_call x22 -> x24, Pallas kernels: 56.6 us -> 56.6 us  [call(): pl.pallas_call(kernel, out_shape=[(pltpu.HBM if i in hbm_out else pltpu.V...]
  transfers between devices with their start and end apart: 21 -> 21, of which waited for: 14 -> 14; matrix products, arithmetic and copies ran while one was open for 0% -> 0% of each run, Pallas kernels for 9% -> 12%
where the time goes in v4:
time: 151 us
  Pallas kernels  56.6 us (37%)
  starting transfers between devices  42.4 us (28%)
  waiting for transfers between devices  30.5 us (20%)
  blocking collectives  19.4 us (13%)
  between operations  1.7 us (1%)
    pallas_call x24, Pallas kernels, call(): pl.pallas_call(kernel, out_shape=[(pltpu.HBM if i in hbm_out else pltpu.V...  56.6 us
    ppermute x20, starting transfers between devices, both_ways(): return (lax.ppermute(to_next, axis, up), lax.ppermute(to_prev, axis, down))  35.5 us
    all_to_all x1, blocking collectives, shards(): sums = lax.all_to_all(part, BOTH, 0, 0, tiled=True)  19.4 us
    ppermute x20, waiting for transfers between devices, both_ways(): return (lax.ppermute(to_next, axis, up), lax.ppermute(to_prev, axis, down))  17.7 us
    all_to_all x1, waiting for transfers between devices, shards(): parts = lax.all_to_all(dense.reshape(128, 1, 1280), BOTH, 0, 0, tiled=True)  12.8 us
    all_to_all x1, starting transfers between devices, shards(): parts = lax.all_to_all(dense.reshape(128, 1, 1280), BOTH, 0, 0, tiled=True)  6.86 us
  transfers between devices with their start and end apart: 21, of which 14 were waited for; matrix products, arithmetic and copies ran while one was open for 0% of the time, Pallas kernels for 12%

profile of v4, /device:TPU:1, one launch (start us, length us, event | category | flops | bytes accessed | tf_op | source)
XLA Modules:
  0.0 150.6 jit_solution(16171806421881951582)
XLA Ops:
  1.3 1.3 faces_kernel.1
  2.6 2.2 %collective-permute-start = (f32[200,128]{1,0:T(8,128)S(1)}, f32[200,128]{1,0:T(8,128)S(1)}, u32[]{:S(2)}, u32[]{:S(2)}) collective-permute-start(f32[200,128]{1,0:T(8,128)S(1)} %get-tuple-element.78.up), channel_id=1, source_target_pairs={{0,8},{8,16},{16,24},{24,32},{32,40},{40,48},{48,56},{56,64},{64,7... | collective-permute-start | bytes 307208 | tf_op jit(solution)/shard_map/ppermute | solution.py:962
  4.8 5.0 %collective-permute-start.1 = (f32[200,128]{1,0:T(8,128)S(1)}, f32[200,128]{1,0:T(8,128)S(1)}, u32[]{:S(2)}, u32[]{:S(2)}) collective-permute-start(f32[200,128]{1,0:T(8,128)S(1)} %get-tuple-element.79.down), channel_id=1, source_target_pairs={{8,0},{16,8},{24,16},{32,24},{40,32},{48,40},{56,48},{64,56},{72,6... | collective-permute-start | bytes 307208 | tf_op jit(solution)/shard_map/ppermute | solution.py:962
  9.8 2.3 %inner_kernel.1 = (f32[3,6,64,128]{3,2,1,0:T(8,128)S(1)}, bf16[432,256]{1,0:T(8,128)(2,1)S(1)}, bf16[64,432]{1,0:T(8,128)(2,1)S(1)}, bf16[128,256]{1,0:T(8,128)(...) custom-call(f32[3,8,64,128]{3,2,1,0:T(8,128)} %bitcast.13, ...), custom_call_target="tpu_custom_call" | custom-call | tf_op jit(solution)/shard_map/inner_kernel/pallas_call | solution.py:117
  12.6 2.3 %collective-permute-start.2 = (f32[3,8,128]{2,1,0:T(8,128)S(1)}, f32[3,8,128]{2,1,0:T(8,128)S(1)}, u32[]{:S(2)}, u32[]{:S(2)}) collective-permute-start(f32[3,8,128]{2,1,0:T(8,128)S(1)} %get-tuple-element.92), channel_id=1, source_target_pairs={{0,1},{1,2},{2,3},{3,4},{4,5},{5,6},{6,7},{7,0},{8,9},{9,10},{10,1... | collective-permute-start | bytes 36872 | tf_op jit(solution)/shard_map/ppermute | solution.py:962
  15.0 0.8 collective-permute-done.2.tlo
  15.8 2.3 %collective-permute-done.3.thi = f32[3,8,128]{2,1,0:T(8,128)S(1)} collective-permute-done((f32[3,8,128]{2,1,0:T(8,128)S(1)}, f32[3,8,128]{2,1,0:T(8,128)S(1)}, u32[]{:S(2)}, u32[]{:S(2)}) %collective-permute-start.3) | collective-permute-done | bytes 12320 | tf_op jit(solution)/shard_map/ppermute | solution.py:962
  18.1 6.9 %project_kernel.1 = (f32[3,8,64,128]{3,2,1,0:T(8,128)S(1)}, f32[3,8,64,128]{3,2,1,0:T(8,128)S(1)}, f32[3,16,128]{2,1,0:T(8,128)S(1)}, f32[3,16,128]{2,1,0:T(8,128)S(1)}) custom-call(f32[3,8,64,128]{3,2,1,0:T(8,128)S(1)} %get-tuple-element.91.field, f32[3,8,128]{2,1,0:T(8,128)S(1)} %collective-permute-done.2.tlo, ...), custom_call_target="tpu_custom_call" | custom-call | tf_op jit(solution)/shard_map/project_kernel/pallas_call | solution.py:117
  25.0 0.5 collective-permute-start.5
  25.5 0.7 collective-permute-done.4.tlo
  26.2 2.1 %collective-permute-done.5.thi = f32[3,16,128]{2,1,0:T(8,128)S(1)} collective-permute-done((f32[3,16,128]{2,1,0:T(8,128)S(1)}, f32[3,16,128]{2,1,0:T(8,128)S(1)}, u32[]{:S(2)}, u32[]{:S(2)}) %collective-permute-start.5) | collective-permute-done | bytes 24608 | tf_op jit(solution)/shard_map/ppermute | solution.py:962
  28.3 0.3 around_widen_kernel.2
  28.7 5.0 %collective-permute-start.7 = (f32[3,2,72,128]{3,2,1,0:T(8,128)S(1)}, f32[3,2,72,128]{3,2,1,0:T(8,128)S(1)}, u32[]{:S(2)}, u32[]{:S(2)}) collective-permute-start(f32[3,2,72,128]{3,2,1,0:T(8,128)S(1)} %get-tuple-element.103), channel_id=1, source_target_pairs={{8,0},{16,8},{24,16},{32,24},{40,32},{48,40},{56,48},{64,56},{72,6... | collective-permute-start | bytes 663560 | tf_op jit(solution)/shard_map/ppermute | solution.py:962
  33.6 2.0 %solve_tables_kernel.1 = (bf16[112,480]{1,0:T(8,128)(2,1)S(1)}, bf16[64,336]{1,0:T(8,128)(2,1)S(1)}, f32[10,112,128]{2,1,0:T(8,128)S(1)}) custom-call(f32[10,10]{1,0:T(8,128)} %vectors.7, f32[1,10]{1,0:T(1,128)} %bitcast.14, f32[16,256]{1,0:T(8,128)S(1)} %get-tuple-element.80.lanes), custom_call_target="tpu_custom_call" | custom-call | tf_op jit(solution)/shard_map/solve_tables_kernel/pallas_call | solution.py:117
  35.6 3.5 %transform_kernel.2.own = f32[3,10,112,128]{3,2,1,0:T(8,128)S(1)} custom-call(f32[3,8,72,128]{3,2,1,0:T(8,128)S(1)} %get-tuple-element.104.field, bf16[112,480]{1,0:T(8,128)(2,1)S(1)} %get-tuple-element.105.forward, f32[10,10]{1,0:T(8,128)S(1)} %copy-done), custom_call_target="tpu_custom_call" | custom-call | tf_op jit(solution)/shard_map/transform_kernel/pallas_call | solution.py:117
  39.2 4.1 %solve_kernel.2 = (f32[3,8,64,128]{3,2,1,0:T(8,128)S(1)}, f32[3,8,128]{2,1,0:T(8,128)S(1)}, f32[3,8,128]{2,1,0:T(8,128)S(1)}) custom-call(f32[3,10,112,128]{3,2,1,0:T(8,128)S(1)} %transform_kernel.2.own, f32[3,2,72,128]{3,2,1,0:T(8,128)S(1)} %collective-permute-done.6.zlo, f32[3,2,72,128]{3,2,1,0:T(8,128)S(1)} %collective-permute-done.7.zhi, ...), custom_call_target="tpu_custom_call" | custom-call | tf_op jit(solution)/shard_map/solve_kernel/pallas_call | solution.py:117
  43.3 0.4 collective-permute-start.8
  43.7 1.3 collective-permute-start.9
  45.0 0.6 collective-permute-done.8.tlo
  45.7 1.1 collective-permute-done.9.thi
  46.8 0.3 around_sum_kernel.2
  47.2 5.7 %collective-permute-start.11 = (f32[200,128]{1,0:T(8,128)S(1)}, f32[200,128]{1,0:T(8,128)S(1)}, u32[]{:S(2)}, u32[]{:S(2)}) collective-permute-start(f32[200,128]{1,0:T(8,128)S(1)} %get-tuple-element.116), channel_id=1, source_target_pairs={{8,0},{16,8},{24,16},{32,24},{40,32},{48,40},{56,48},{64,56},{72,6... | collective-permute-start | bytes 307208 | tf_op jit(solution)/shard_map/ppermute | solution.py:962
  52.9 2.0 %collective-permute-done.10.zlo = f32[200,128]{1,0:T(8,128)S(1)} collective-permute-done((f32[200,128]{1,0:T(8,128)S(1)}, f32[200,128]{1,0:T(8,128)S(1)}, u32[]{:S(2)}, u32[]{:S(2)}) %collective-permute-start.10) | collective-permute-done | bytes 102432 | tf_op jit(solution)/shard_map/ppermute | solution.py:962
  54.9 1.9 %direction_kernel.2 = (f32[3,8,64,128]{3,2,1,0:T(8,128)S(1)}, f32[128,128]{1,0:T(8,128)S(1)}) custom-call(f32[3,8,64,128]{3,2,1,0:T(8,128)S(1)} %get-tuple-element.114.field, f32[200,128]{1,0:T(8,128)S(1)} %collective-permute-done.10.zlo, f32[200,128]{1,0:T(8,128)S(1)} %collective-permute-done.11.zhi, f32[3,8,64,128]{3,2,1,0:T(8,128)S(1)} %get-tuple-element.99.res, ...), custom_call_target="tpu_custom_call" | custom-call | tf_op jit(solution)/shard_map/direction_kernel/pallas_call | solution.py:117
  56.8 19.4 %all_to_all.16 = f32[128,1,128]{2,1,0:T(1,128)S(1)} all-to-all(f32[128,1,128]{2,1,0:T(1,128)S(1)} %bitcast.11), channel_id=1, replica_groups=mesh['wide'=16,'narrow'=8] {'wide','narrow'}, dimensions={0} | all-to-all | bytes 131072 | tf_op jit(solution)/shard_map/all_to_all | solution.py:1054
  76.2 6.5 %advance_kernel.1 = (f32[3,8,64,128]{3,2,1,0:T(8,128)S(1)}, f32[3,8,64,128]{3,2,1,0:T(8,128)S(1)}, f32[3,16,128]{2,1,0:T(8,128)S(1)}, f32[3,16,128]{2,1,0:T(8,128)S(1)}) custom-call(f32[3,8,64,128]{3,2,1,0:T(8,128)S(1)} %get-tuple-element.98.u_old, f32[3,8,64,128]{3,2,1,0:T(8,128)S(1)} %get-tuple-element.120.d, f32[128,128]{1,0:T(8,128)S(1)} %bitcast.10, ...), custom_call_target="tpu_custom_call" | custom-call | tf_op jit(solution)/shard_map/advance_kernel/pallas_call | solution.py:117
  82.7 0.9 collective-permute-start.12
  83.6 0.9 collective-permute-done.12.tlo
  84.6 2.6 %collective-permute-done.13.thi = f32[3,16,128]{2,1,0:T(8,128)S(1)} collective-permute-done((f32[3,16,128]{2,1,0:T(8,128)S(1)}, f32[3,16,128]{2,1,0:T(8,128)S(1)}, u32[]{:S(2)}, u32[]{:S(2)}) %collective-permute-start.13) | collective-permute-done | bytes 24608 | tf_op jit(solution)/shard_map/ppermute | solution.py:962
  87.2 0.3 around_widen_kernel.3
  87.8 4.6 %collective-permute-start.15 = (f32[3,2,72,128]{3,2,1,0:T(8,128)S(1)}, f32[3,2,72,128]{3,2,1,0:T(8,128)S(1)}, u32[]{:S(2)}, u32[]{:S(2)}) collective-permute-start(f32[3,2,72,128]{3,2,1,0:T(8,128)S(1)} %get-tuple-element.127), channel_id=1, source_target_pairs={{8,0},{16,8},{24,16},{32,24},{40,32},{48,40},{56,48},{64,56},{72,6... | collective-permute-start | bytes 663560 | tf_op jit(solution)/shard_map/ppermute | solution.py:962
  92.4 3.5 %transform_kernel.3.own = f32[3,10,112,128]{3,2,1,0:T(8,128)S(1)} custom-call(f32[3,8,72,128]{3,2,1,0:T(8,128)S(1)} %get-tuple-element.128.field, bf16[112,480]{1,0:T(8,128)(2,1)S(1)} %get-tuple-element.105.forward, f32[10,10]{1,0:T(8,128)S(1)} %copy-done), custom_call_target="tpu_custom_call" | custom-call | tf_op jit(solution)/shard_map/transform_kernel/pallas_call | solution.py:117
  95.9 1.2 collective-permute-done.14.zlo
  97.1 4.1 %solve_kernel.3 = (f32[3,8,64,128]{3,2,1,0:T(8,128)S(1)}, f32[3,8,128]{2,1,0:T(8,128)S(1)}, f32[3,8,128]{2,1,0:T(8,128)S(1)}) custom-call(f32[3,10,112,128]{3,2,1,0:T(8,128)S(1)} %transform_kernel.3.own, f32[3,2,72,128]{3,2,1,0:T(8,128)S(1)} %collective-permute-done.14.zlo, f32[3,2,72,128]{3,2,1,0:T(8,128)S(1)} %collective-permute-done.15.zhi, ...), custom_call_target="tpu_custom_call" | custom-call | tf_op jit(solution)/shard_map/solve_kernel/pallas_call | solution.py:117
  101.2 1.5 %collective-permute-start.16 = (f32[3,8,128]{2,1,0:T(8,128)S(1)}, f32[3,8,128]{2,1,0:T(8,128)S(1)}, u32[]{:S(2)}, u32[]{:S(2)}) collective-permute-start(f32[3,8,128]{2,1,0:T(8,128)S(1)} %get-tuple-element.133), channel_id=1, source_target_pairs={{0,1},{1,2},{2,3},{3,4},{4,5},{5,6},{6,7},{7,0},{8,9},{9,10},{10,1... | collective-permute-start | bytes 36872 | tf_op jit(solution)/shard_map/ppermute | solution.py:962
  102.9 0.7 collective-permute-done.16.tlo
  103.6 2.3 %collective-permute-done.17.thi = f32[3,8,128]{2,1,0:T(8,128)S(1)} collective-permute-done((f32[3,8,128]{2,1,0:T(8,128)S(1)}, f32[3,8,128]{2,1,0:T(8,128)S(1)}, u32[]{:S(2)}, u32[]{:S(2)}) %collective-permute-start.17) | collective-permute-done | bytes 12320 | tf_op jit(solution)/shard_map/ppermute | solution.py:962
  106.3 5.4 %collective-permute-start.19 = (f32[200,128]{1,0:T(8,128)S(1)}, f32[200,128]{1,0:T(8,128)S(1)}, u32[]{:S(2)}, u32[]{:S(2)}) collective-permute-start(f32[200,128]{1,0:T(8,128)S(1)} %get-tuple-element.137), channel_id=1, source_target_pairs={{8,0},{16,8},{24,16},{32,24},{40,32},{48,40},{56,48},{64,56},{72,6... | collective-permute-start | bytes 307208 | tf_op jit(solution)/shard_map/ppermute | solution.py:962
  111.7 0.5 route_kernel.1
  112.5 2.9 %fields_kernel.1 = (f32[6,3,432,256]{3,2,1,0:T(8,128)S(1)}, f32[6,3,144,256]{3,2,1,0:T(8,128)S(1)}) custom-call(f32[3,8,64,128]{3,2,1,0:T(8,128)S(1)} %get-tuple-element.122.u, bf16[432,256]{1,0:T(8,128)(2,1)S(1)} %get-tuple-element.94.fine), custom_call_target="tpu_custom_call" | custom-call | tf_op jit(solution)/shard_map/fields_kernel/pallas_call | solution.py:117
  115.4 0.8 place_base_kernel.1.base
  116.2 1.9 %direction_kernel.3 = (f32[3,8,64,128]{3,2,1,0:T(8,128)S(1)}, f32[128,128]{1,0:T(8,128)S(1)}) custom-call(f32[3,8,64,128]{3,2,1,0:T(8,128)S(1)} %get-tuple-element.135.field, f32[200,128]{1,0:T(8,128)S(1)} %collective-permute-done.18.zlo, f32[200,128]{1,0:T(8,128)S(1)} %collective-permute-done.19.zhi, f32[3,8,64,128]{3,2,1,0:T(8,128)S(1)} %get-tuple-element.123.res, ...), custom_call_target="tpu_custom_call" | custom-call | tf_op jit(solution)/shard_map/direction_kernel/pallas_call | solution.py:117
  118.1 6.1 %change_kernel.1.change = f32[6,8,256]{2,1,0:T(8,128)S(1)} custom-call(f32[3,8,64,128]{3,2,1,0:T(8,128)S(1)} %get-tuple-element.144.d, f32[6,3,432,256]{3,2,1,0:T(8,128)S(1)} %get-tuple-element.148.pf, f32[6,3,144,256]{3,2,1,0:T(8,128)S(1)} %get-tuple-element.149.qf, f32[16,256]{1,0:T(8,128)S(1)} %get-tuple-element.80.lanes, ...), custom_call_target="tpu_custom_call" | custom-call | tf_op jit(solution)/shard_map/change_kernel/pallas_call | solution.py:117
  124.2 2.0 %place_kernel.1 = f32[1280,128]{1,0:T(8,128)} custom-call(f32[3,128,256]{2,1,0:T(8,128)S(1)} %place_base_kernel.1.base, f32[6,8,256]{2,1,0:T(8,128)S(1)} %change_kernel.1.change, bf16[1024,256]{1,0:T(8,128)(2,1)S(1)} %get-tuple-element.140.right, s32[8,128]{1,0:T(8,128)S(1)} %get-tuple-element.141.owner, f32[128,128]{1,0:T(8,128)S(1)} %get-tuple-element.151.part), custom_call_target="tpu_custom_call" | custom-call | tf_op jit(solution)/shard_map/place_kernel/pallas_call | solution.py:117
  126.2 6.9 %all-to-all-start.1 = ((f32[128,1,1280]{2,1,0:T(1,128)}), f32[128,1,1280]{2,1,0:T(1,128)S(1)}, u32[]{:S(2)}, u32[]{:S(2)}) async-start(f32[128,1,1280]{2,1,0:T(1,128)} %bitcast.5), calls=%async_computation.1 | async-start | bytes 1310720 | tf_op jit(solution)/shard_map/all_to_all | solution.py:1132
  133.1 2.3 %store_kernel.1 = (f32[3,8,64,128]{3,2,1,0:T(8,128)}, f32[3,8,64,128]{3,2,1,0:T(8,128)}) custom-call(f32[3,8,64,128]{3,2,1,0:T(8,128)S(1)} %get-tuple-element.122.u, f32[3,8,64,128]{3,2,1,0:T(8,128)S(1)} %get-tuple-element.144.d, s32[1,128]{1,0:T(1,128)S(1)} %copy-done.1), custom_call_target="tpu_custom_call" | custom-call | tf_op jit(solution)/shard_map/store_kernel/pallas_call | solution.py:117
  135.3 12.8 %all-to-all-done.1 = f32[128,1,1280]{2,1,0:T(1,128)S(1)} async-done(((f32[128,1,1280]{2,1,0:T(1,128)}), f32[128,1,1280]{2,1,0:T(1,128)S(1)}, u32[]{:S(2)}, u32[]{:S(2)}) %all-to-all-start.1) | async-done | bytes 655392 | tf_op jit(solution)/shard_map/all_to_all | solution.py:1132
  148.2 2.3 %end_kernel.1 = (f32[3,8,64,128]{3,2,1,0:T(8,128)}, f32[3,136]{1,0:T(4,128)}) custom-call(f32[3,8,64,128]{3,2,1,0:T(8,128)} %get-tuple-element.145.u_hbm, f32[3,8,64,128]{3,2,1,0:T(8,128)} %get-tuple-element.146.d_hbm, f32[1280,128]{1,0:T(8,128)S(1)} %bitcast.9), custom_call_target="tpu_custom_call" | custom-call | tf_op jit(solution)/shard_map/end_kernel/pallas_call | solution.py:117
  (25 shorter events, 1.9 us)
Async XLA Ops:
  1.3 34.4 %copy-start = (f32[10,10]{1,0:T(8,128)S(1)}, f32[10,10]{1,0:T(8,128)}, u32[]{:S(2)}) copy-start(f32[10,10]{1,0:T(8,128)} %vectors.7) | copy-start | bytes 1204
  2.6 9.7 %collective-permute-start = (f32[200,128]{1,0:T(8,128)S(1)}, f32[200,128]{1,0:T(8,128)S(1)}, u32[]{:S(2)}, u32[]{:S(2)}) collective-permute-start(f32[200,128]{1,0:T(8,128)S(1)} %get-tuple-element.78.up), channel_id=1, source_target_pairs={{0,8},{8,16},{16,24},{24,32},{32,40},{40,48},{48,56},{56,64},{64,7... | collective-permute-start | bytes 307208 | tf_op jit(solution)/shard_map/ppermute | solution.py:962
  4.8 7.5 %collective-permute-start.1 = (f32[200,128]{1,0:T(8,128)S(1)}, f32[200,128]{1,0:T(8,128)S(1)}, u32[]{:S(2)}, u32[]{:S(2)}) collective-permute-start(f32[200,128]{1,0:T(8,128)S(1)} %get-tuple-element.79.down), channel_id=1, source_target_pairs={{8,0},{16,8},{24,16},{32,24},{40,32},{48,40},{56,48},{64,56},{72,6... | collective-permute-start | bytes 307208 | tf_op jit(solution)/shard_map/ppermute | solution.py:962
  12.6 3.2 %collective-permute-start.2 = (f32[3,8,128]{2,1,0:T(8,128)S(1)}, f32[3,8,128]{2,1,0:T(8,128)S(1)}, u32[]{:S(2)}, u32[]{:S(2)}) collective-permute-start(f32[3,8,128]{2,1,0:T(8,128)S(1)} %get-tuple-element.92), channel_id=1, source_target_pairs={{0,1},{1,2},{2,3},{3,4},{4,5},{5,6},{6,7},{7,0},{8,9},{9,10},{10,1... | collective-permute-start | bytes 36872 | tf_op jit(solution)/shard_map/ppermute | solution.py:962
  15.0 3.1 %collective-permute-start.3 = (f32[3,8,128]{2,1,0:T(8,128)S(1)}, f32[3,8,128]{2,1,0:T(8,128)S(1)}, u32[]{:S(2)}, u32[]{:S(2)}) collective-permute-start(f32[3,8,128]{2,1,0:T(8,128)S(1)} %get-tuple-element.93), channel_id=1, source_target_pairs={{1,0},{2,1},{3,2},{4,3},{5,4},{6,5},{7,6},{0,7},{9,8},{10,9},{11,1... | collective-permute-start | bytes 36872 | tf_op jit(solution)/shard_map/ppermute | solution.py:962
  25.0 1.2 collective-permute-start.4
  25.0 3.3 %collective-permute-start.5 = (f32[3,16,128]{2,1,0:T(8,128)S(1)}, f32[3,16,128]{2,1,0:T(8,128)S(1)}, u32[]{:S(2)}, u32[]{:S(2)}) collective-permute-start(f32[3,16,128]{2,1,0:T(8,128)S(1)} %get-tuple-element.101), channel_id=1, source_target_pairs={{1,0},{2,1},{3,2},{4,3},{5,4},{6,5},{7,6},{0,7},{9,8},{10,9},{11,1... | collective-permute-start | bytes 73736 | tf_op jit(solution)/shard_map/ppermute | solution.py:962
  28.6 10.6 %collective-permute-start.6 = (f32[3,2,72,128]{3,2,1,0:T(8,128)S(1)}, f32[3,2,72,128]{3,2,1,0:T(8,128)S(1)}, u32[]{:S(2)}, u32[]{:S(2)}) collective-permute-start(f32[3,2,72,128]{3,2,1,0:T(8,128)S(1)} %get-tuple-element.102), channel_id=1, source_target_pairs={{0,8},{8,16},{16,24},{24,32},{32,40},{40,48},{48,56},{56,64},{64,7... | collective-permute-start | bytes 663560 | tf_op jit(solution)/shard_map/ppermute | solution.py:962
  28.7 10.5 %collective-permute-start.7 = (f32[3,2,72,128]{3,2,1,0:T(8,128)S(1)}, f32[3,2,72,128]{3,2,1,0:T(8,128)S(1)}, u32[]{:S(2)}, u32[]{:S(2)}) collective-permute-start(f32[3,2,72,128]{3,2,1,0:T(8,128)S(1)} %get-tuple-element.103), channel_id=1, source_target_pairs={{8,0},{16,8},{24,16},{32,24},{40,32},{48,40},{56,48},{64,56},{72,6... | collective-permute-start | bytes 663560 | tf_op jit(solution)/shard_map/ppermute | solution.py:962
  43.3 2.4 %collective-permute-start.8 = (f32[3,8,128]{2,1,0:T(8,128)S(1)}, f32[3,8,128]{2,1,0:T(8,128)S(1)}, u32[]{:S(2)}, u32[]{:S(2)}) collective-permute-start(f32[3,8,128]{2,1,0:T(8,128)S(1)} %get-tuple-element.112), channel_id=1, source_target_pairs={{0,1},{1,2},{2,3},{3,4},{4,5},{5,6},{6,7},{7,0},{8,9},{9,10},{10,1... | collective-permute-start | bytes 36872 | tf_op jit(solution)/shard_map/ppermute | solution.py:962
  43.7 3.1 %collective-permute-start.9 = (f32[3,8,128]{2,1,0:T(8,128)S(1)}, f32[3,8,128]{2,1,0:T(8,128)S(1)}, u32[]{:S(2)}, u32[]{:S(2)}) collective-permute-start(f32[3,8,128]{2,1,0:T(8,128)S(1)} %get-tuple-element.113), channel_id=1, source_target_pairs={{1,0},{2,1},{3,2},{4,3},{5,4},{6,5},{7,6},{0,7},{9,8},{10,9},{11,1... | collective-permute-start | bytes 36872 | tf_op jit(solution)/shard_map/ppermute | solution.py:962
  47.1 7.7 %collective-permute-start.10 = (f32[200,128]{1,0:T(8,128)S(1)}, f32[200,128]{1,0:T(8,128)S(1)}, u32[]{:S(2)}, u32[]{:S(2)}) collective-permute-start(f32[200,128]{1,0:T(8,128)S(1)} %get-tuple-element.115), channel_id=1, source_target_pairs={{0,8},{8,16},{16,24},{24,32},{32,40},{40,48},{48,56},{56,64},{64,7... | collective-permute-start | bytes 307208 | tf_op jit(solution)/shard_map/ppermute | solution.py:962
  47.2 7.6 %collective-permute-start.11 = (f32[200,128]{1,0:T(8,128)S(1)}, f32[200,128]{1,0:T(8,128)S(1)}, u32[]{:S(2)}, u32[]{:S(2)}) collective-permute-start(f32[200,128]{1,0:T(8,128)S(1)} %get-tuple-element.116), channel_id=1, source_target_pairs={{8,0},{16,8},{24,16},{32,24},{40,32},{48,40},{56,48},{64,56},{72,6... | collective-permute-start | bytes 307208 | tf_op jit(solution)/shard_map/ppermute | solution.py:962
  82.7 1.9 %collective-permute-start.12 = (f32[3,16,128]{2,1,0:T(8,128)S(1)}, f32[3,16,128]{2,1,0:T(8,128)S(1)}, u32[]{:S(2)}, u32[]{:S(2)}) collective-permute-start(f32[3,16,128]{2,1,0:T(8,128)S(1)} %get-tuple-element.124), channel_id=1, source_target_pairs={{0,1},{1,2},{2,3},{3,4},{4,5},{5,6},{6,7},{7,0},{8,9},{9,10},{10,1... | collective-permute-start | bytes 73736 | tf_op jit(solution)/shard_map/ppermute | solution.py:962
  83.6 3.5 %collective-permute-start.13 = (f32[3,16,128]{2,1,0:T(8,128)S(1)}, f32[3,16,128]{2,1,0:T(8,128)S(1)}, u32[]{:S(2)}, u32[]{:S(2)}) collective-permute-start(f32[3,16,128]{2,1,0:T(8,128)S(1)} %get-tuple-element.125), channel_id=1, source_target_pairs={{1,0},{2,1},{3,2},{4,3},{5,4},{6,5},{7,6},{0,7},{9,8},{10,9},{11,1... | collective-permute-start | bytes 73736 | tf_op jit(solution)/shard_map/ppermute | solution.py:962
  87.5 9.6 %collective-permute-start.14 = (f32[3,2,72,128]{3,2,1,0:T(8,128)S(1)}, f32[3,2,72,128]{3,2,1,0:T(8,128)S(1)}, u32[]{:S(2)}, u32[]{:S(2)}) collective-permute-start(f32[3,2,72,128]{3,2,1,0:T(8,128)S(1)} %get-tuple-element.126), channel_id=1, source_target_pairs={{0,8},{8,16},{16,24},{24,32},{32,40},{40,48},{48,56},{56,64},{64,7... | collective-permute-start | bytes 663560 | tf_op jit(solution)/shard_map/ppermute | solution.py:962
  87.8 9.3 %collective-permute-start.15 = (f32[3,2,72,128]{3,2,1,0:T(8,128)S(1)}, f32[3,2,72,128]{3,2,1,0:T(8,128)S(1)}, u32[]{:S(2)}, u32[]{:S(2)}) collective-permute-start(f32[3,2,72,128]{3,2,1,0:T(8,128)S(1)} %get-tuple-element.127), channel_id=1, source_target_pairs={{8,0},{16,8},{24,16},{32,24},{40,32},{48,40},{56,48},{64,56},{72,6... | collective-permute-start | bytes 663560 | tf_op jit(solution)/shard_map/ppermute | solution.py:962
  92.4 19.3 %copy-start.1 = (s32[1,128]{1,0:T(1,128)S(1)}, s32[1,128]{1,0:T(1,128)}, u32[]{:S(2)}) copy-start(s32[1,128]{1,0:T(1,128)} %slot.3) | copy-start | bytes 1540
  92.4 19.3 %copy-start.2 = (s32[8,128]{1,0:T(8,128)S(1)}, s32[8,128]{1,0:T(8,128)}, u32[]{:S(2)}) copy-start(s32[8,128]{1,0:T(8,128)} %corner.1) | copy-start | bytes 12292
  101.2 2.4 %collective-permute-start.16 = (f32[3,8,128]{2,1,0:T(8,128)S(1)}, f32[3,8,128]{2,1,0:T(8,128)S(1)}, u32[]{:S(2)}, u32[]{:S(2)}) collective-permute-start(f32[3,8,128]{2,1,0:T(8,128)S(1)} %get-tuple-element.133), channel_id=1, source_target_pairs={{0,1},{1,2},{2,3},{3,4},{4,5},{5,6},{6,7},{7,0},{8,9},{9,10},{10,1... | collective-permute-start | bytes 36872 | tf_op jit(solution)/shard_map/ppermute | solution.py:962
  102.7 3.1 %collective-permute-start.17 = (f32[3,8,128]{2,1,0:T(8,128)S(1)}, f32[3,8,128]{2,1,0:T(8,128)S(1)}, u32[]{:S(2)}, u32[]{:S(2)}) collective-permute-start(f32[3,8,128]{2,1,0:T(8,128)S(1)} %get-tuple-element.134), channel_id=1, source_target_pairs={{1,0},{2,1},{3,2},{4,3},{5,4},{6,5},{7,6},{0,7},{9,8},{10,9},{11,1... | collective-permute-start | bytes 36872 | tf_op jit(solution)/shard_map/ppermute | solution.py:962
  106.2 10.0 %collective-permute-start.18 = (f32[200,128]{1,0:T(8,128)S(1)}, f32[200,128]{1,0:T(8,128)S(1)}, u32[]{:S(2)}, u32[]{:S(2)}) collective-permute-start(f32[200,128]{1,0:T(8,128)S(1)} %get-tuple-element.136), channel_id=1, source_target_pairs={{0,8},{8,16},{16,24},{24,32},{32,40},{40,48},{48,56},{56,64},{64,7... | collective-permute-start | bytes 307208 | tf_op jit(solution)/shard_map/ppermute | solution.py:962
  106.3 9.9 %collective-permute-start.19 = (f32[200,128]{1,0:T(8,128)S(1)}, f32[200,128]{1,0:T(8,128)S(1)}, u32[]{:S(2)}, u32[]{:S(2)}) collective-permute-start(f32[200,128]{1,0:T(8,128)S(1)} %get-tuple-element.137), channel_id=1, source_target_pairs={{8,0},{16,8},{24,16},{32,24},{40,32},{48,40},{56,48},{64,56},{72,6... | collective-permute-start | bytes 307208 | tf_op jit(solution)/shard_map/ppermute | solution.py:962
  126.2 22.0 %all-to-all-start.1 = ((f32[128,1,1280]{2,1,0:T(1,128)}), f32[128,1,1280]{2,1,0:T(1,128)S(1)}, u32[]{:S(2)}, u32[]{:S(2)}) async-start(f32[128,1,1280]{2,1,0:T(1,128)} %bitcast.5), calls=%async_computation.1 | async-start | bytes 1310720 | tf_op jit(solution)/shard_map/all_to_all | solution.py:1132

commit v5 on v4

--- a/solution.py
+++ b/solution.py
@@ -418,40 +418,31 @@
 def put(ref, at, rb, half, x):
     hi, lo = split(x)
     for term, part in enumerate((hi, hi, lo, lo)):
-        rows = pl.ds(pl.multiple_of(term * 64 + rb * 16, 16), 16)
+        start = term * 64 + rb * 16
+        rows = pl.ds(start if isinstance(start, int) else pl.multiple_of(start, 16), 16)
         ref[at, rows, half * 128 : half * 128 + 128] = part
 
 
-def along_pipe(u, xu, xw, xs=None, sz=None):
-    def body(t, carry):
-        c, rb = t // 4, t % 4
-        rows = pl.ds(pl.multiple_of(rb * 16, 16), 16)
-        x = [u[c, i, rows] for i in range(8)]
-        for a, val in enumerate(even_odd(J, x, 1)):
-            put(xu, c * 6 + a // 2, rb, a % 2, val)
-        for a, val in enumerate(even_odd(B, x, -1)):
-            put(xw, c * 6 + a // 2, rb, a % 2, val)
-        if xs is None:
-            return carry
-        for i in range(8):
-            put(xs, c * 4 + i // 2, rb, i % 2, x[i])
-        for i, val in enumerate(even_odd(STIFF, x, 1)):
-            sz[c, i, rows] = val
-        return carry
-
-    lax.fori_loop(0, 12, body, 0)
-
-
-def fine_dots(p, at, fine, xu, xw, pf, qf):
-    for c in range(3):
-        pf[at, c] = dot(fine[...], xu[c * 6 + p])
-        qf[at, c] = dot(fine[0:144], xw[c * 6 + p])
-
-
-def stiff_dots(p, stiff, xs, ks):
-    for t in (2 * p, 2 * p + 1):
-        y = dot(stiff[...], xs[t])
-        c, q = t // 4, t % 4
+def along_pipe(u, c, rb, xu, xw):
+    rows = pl.ds(rb * 16 if isinstance(rb, int) else pl.multiple_of(rb * 16, 16), 16)
+    x = [u[c, i, rows] for i in range(8)]
+    for a, val in enumerate(even_odd(J, x, 1)):
+        put(xu, c * 6 + a // 2, rb, a % 2, val)
+    for a, val in enumerate(even_odd(B, x, -1)):
+        put(xw, c * 6 + a // 2, rb, a % 2, val)
+    return rows, x
+
+
+def fine_dots(pairs, parts, fine, xu, xw, pf, qf):
+    for p in pairs:
+        for c in parts:
+            pf[p, c] = dot(fine[...], xu[c * 6 + p])
+            qf[p, c] = dot(fine[0:144], xw[c * 6 + p])
+
+
+def stiff_dots(c, stiff, xs, ks):
+    for q in range(4):
+        y = dot(stiff[...], xs[4 * c + q])
         ks[c, 2 * q] = y[:, :128]
         ks[c, 2 * q + 1] = y[:, 128:]
 
@@ -493,17 +484,21 @@
 
 
 def residual(u, lanes, fine, back, stiff, wjk, res, pf, qf, xu, xw, xs, xc0, xc1, yf, sz, ks):
-    along_pipe(u, xu, xw, xs, sz)
-    fine_dots(0, 0, fine, xu, xw, pf, qf)
+    for c in range(3):
+        for rb in range(4):
+            rows, x = along_pipe(u, c, rb, xu, xw)
+            for i in range(8):
+                put(xs, c * 4 + i // 2, rb, i % 2, x[i])
+            for i, val in enumerate(even_odd(STIFF, x, 1)):
+                sz[c, i, rows] = val
+        fine_dots(range(6), (c,), fine, xu, xw, pf, qf)
+        stiff_dots(c, stiff, xs, ks)
     for p in range(6):
-        if p < 5:
-            fine_dots(p + 1, (p + 1) % 2, fine, xu, xw, pf, qf)
-        stiff_dots(p, stiff, xs, ks)
         xc = (xc0, xc1)[p % 2]
         for r in range(9):
-            v = velocity_rows(pf, lanes, p % 2, r)
+            v = velocity_rows(pf, lanes, p, r)
             for c in range(3):
-                g = fine_rows(pf, qf, p % 2, c, r)
+                g = fine_rows(pf, qf, p, c, r)
                 put_conv(xc, c, r, v[0] * g[0] + v[1] * g[1] + v[2] * g[2])
         back_dots(p, back, xc, yf, 3)
     keep = keep_rows(16)
@@ -520,9 +515,12 @@
 
 
 def fields_kernel(u, fine, pf, qf, xu, xw):
-    along_pipe(u, xu, xw)
-    for p in range(6):
-        fine_dots(p, p, fine, xu, xw, pf, qf)
+    def body(t, carry):
+        along_pipe(u, t // 4, t % 4, xu, xw)
+        return carry
+
+    lax.fori_loop(0, 12, body, 0)
+    fine_dots(range(6), range(3), fine, xu, xw, pf, qf)
 
 
 def corner_weights():
@@ -557,12 +555,7 @@
 
     def body(t, carry):
         c, rb = t // 4, t % 4
-        rows = pl.ds(pl.multiple_of(rb * 16, 16), 16)
-        x = [d[c, i, rows] for i in range(8)]
-        for a, val in enumerate(even_odd(J, x, 1)):
-            put(xd, c * 6 + a // 2, rb, a % 2, val)
-        for a, val in enumerate(even_odd(B, x, -1)):
-            put(xe, c * 6 + a // 2, rb, a % 2, val)
+        rows, x = along_pipe(d, c, rb, xd, xe)
         for a in range(2):
             put(xs, c, rb, a, sum(float(mean_w[a, i]) * x[i] for i in range(8)))
             sz[c, a, rows] = sum(float(mean_s[a, i]) * x[i] for i in range(8))
@@ -579,16 +572,16 @@
                 float(COARSE_Z[a, 2 * p]) * left + float(COARSE_Z[a, 2 * p + 1]) * right
             )
 
-    fine_dots(0, 0, fine, xd, xe, pd, qd)
+    fine_dots((0,), range(3), fine, xd, xe, pd, qd)
     for p in range(6):
         if p < 5:
-            fine_dots(p + 1, (p + 1) % 2, fine, xd, xe, pd, qd)
+            fine_dots((p + 1,), range(3), fine, xd, xe, pd, qd)
         for r in range(9):
             v = velocity_rows(pf, lanes, p, r)
-            w = velocity_rows(pd, lanes, p % 2, r)
+            w = velocity_rows(pd, lanes, p, r)
             for c in range(3):
                 g = fine_rows(pf, qf, p, c, r)
-                h = fine_rows(pd, qd, p % 2, c, r)
+                h = fine_rows(pd, qd, p, c, r)
                 one = (v[0] * h[0] + v[1] * h[1] + v[2] * h[2]) + (
                     w[0] * g[0] + w[1] * g[1] + w[2] * g[2]
                 )
@@ -637,31 +630,38 @@
     hz = lanes[7:8, :128]
     inner = 1.0 / hz
     first = 1.0 / (hz + hz_low[192:193])
-    last = 1.0 / (hz + hz_high[192:193])
+    final = 1.0 / (hz + hz_high[192:193])
     k = iota((8, 128), 0)
     rk = jnp.where(
         k == 0, lanes[9:10, :128], jnp.where(k == 7, lanes[10:11, :128], lanes[8:9, :128])
     )
     rk = rk * keep_rows(8)
-    by_plane = {0: rk * first, 7: rk * last}
+    by_plane = {0: rk * first, 7: rk * final}
     middle = rk * inner
 
-    def body(c, carry):
+    def around(c, carry):
         lo, hi = tlo[c], thi[c]
         for i in range(8):
             x = field[c, i]
+            first, last = x[0:8], x[56:64]
+            u[c, i] = x
+            u[c, i, 0:8] = first + from_low(last, lo, i)
+            u[c, i, 56:64] = last + from_high(first, hi, i)
+        return carry
+
+    def across(c, carry):
+        for i in range(8):
+            x = u[c, i]
             for j in range(8):
                 v = x[8 * j : 8 * j + 8]
                 f = by_plane.get(i, middle)
-                if j == 0:
-                    v, f = v + from_low(x[56:64], lo, i), 0.5 * f
-                if j == 7:
-                    v, f = v + from_high(x[0:8], hi, i), 0.5 * f
+                f = 0.5 * f if j in (0, 7) else f
                 below, above = radial_parts(v)
                 u[c, i, 8 * j : 8 * j + 8] = radial_sum(v, below, above) * f
         return carry
 
-    lax.fori_loop(0, 3, body, 0)
+    lax.fori_loop(0, 3, around, 0)
+    lax.fori_loop(0, 3, across, 0)
     residual(u, lanes, fine, back, stiff, wjk, res, *scratch)
     pack_two(res, low, high)
 
@@ -964,8 +964,8 @@
 
 def fine_scratch():
     return [
-        pltpu.VMEM((2, 3, 432, 256), F32),
-        pltpu.VMEM((2, 3, 144, 256), F32),
+        pltpu.VMEM((6, 3, 432, 256), F32),
+        pltpu.VMEM((6, 3, 144, 256), F32),
         pltpu.VMEM((18, 256, 256), BF16),
         pltpu.VMEM((18, 256, 256), BF16),
     ]

time: 151 us -> 150 us (level)
  no operation moved by 1% of the time
where the time goes in v5:
time: 150 us; the launch traced here: 149 us
  Pallas kernels  55.4 us (37%)
  starting transfers between devices  42.4 us (28%)
  waiting for transfers between devices  30.5 us (20%)
  blocking collectives  19.4 us (13%)
  between operations  1.7 us (1%)
    pallas_call x24, Pallas kernels, call(): pl.pallas_call(kernel, out_shape=[(pltpu.HBM if i in hbm_out else pltpu.V...  55.4 us
    ppermute x20, starting transfers between devices, both_ways(): return (lax.ppermute(to_next, axis, up), lax.ppermute(to_prev, axis, down))  35.5 us
    all_to_all x1, blocking collectives, shards(): sums = lax.all_to_all(part, BOTH, 0, 0, tiled=True)  19.4 us
    ppermute x20, waiting for transfers between devices, both_ways(): return (lax.ppermute(to_next, axis, up), lax.ppermute(to_prev, axis, down))  17.7 us
    all_to_all x1, waiting for transfers between devices, shards(): parts = lax.all_to_all(dense.reshape(128, 1, 1280), BOTH, 0, 0, tiled=True)  12.8 us
    all_to_all x1, starting transfers between devices, shards(): parts = lax.all_to_all(dense.reshape(128, 1, 1280), BOTH, 0, 0, tiled=True)  6.86 us
  transfers between devices with their start and end apart: 21, of which 14 were waited for; matrix products, arithmetic and copies ran while one was open for 0% of the time, Pallas kernels for 12%

profile of v5, /device:TPU:1, one launch (start us, length us, event | category | flops | bytes accessed | tf_op | source)
XLA Modules:
  0.0 149.5 jit_solution(6510500495396335984)
XLA Ops:
  1.3 1.3 faces_kernel.1
  2.6 2.2 %collective-permute-start = (f32[200,128]{1,0:T(8,128)S(1)}, f32[200,128]{1,0:T(8,128)S(1)}, u32[]{:S(2)}, u32[]{:S(2)}) collective-permute-start(f32[200,128]{1,0:T(8,128)S(1)} %get-tuple-element.78.up), channel_id=1, source_target_pairs={{0,8},{8,16},{16,24},{24,32},{32,40},{40,48},{48,56},{56,64},{64,7... | collective-permute-start | bytes 307208 | tf_op jit(solution)/shard_map/ppermute | solution.py:962
  4.8 5.0 %collective-permute-start.1 = (f32[200,128]{1,0:T(8,128)S(1)}, f32[200,128]{1,0:T(8,128)S(1)}, u32[]{:S(2)}, u32[]{:S(2)}) collective-permute-start(f32[200,128]{1,0:T(8,128)S(1)} %get-tuple-element.79.down), channel_id=1, source_target_pairs={{8,0},{16,8},{24,16},{32,24},{40,32},{48,40},{56,48},{64,56},{72,6... | collective-permute-start | bytes 307208 | tf_op jit(solution)/shard_map/ppermute | solution.py:962
  9.8 2.3 %inner_kernel.1 = (f32[3,6,64,128]{3,2,1,0:T(8,128)S(1)}, bf16[432,256]{1,0:T(8,128)(2,1)S(1)}, bf16[64,432]{1,0:T(8,128)(2,1)S(1)}, bf16[128,256]{1,0:T(8,128)(...) custom-call(f32[3,8,64,128]{3,2,1,0:T(8,128)} %bitcast.13, ...), custom_call_target="tpu_custom_call" | custom-call | tf_op jit(solution)/shard_map/inner_kernel/pallas_call | solution.py:117
  12.6 2.3 %collective-permute-start.2 = (f32[3,8,128]{2,1,0:T(8,128)S(1)}, f32[3,8,128]{2,1,0:T(8,128)S(1)}, u32[]{:S(2)}, u32[]{:S(2)}) collective-permute-start(f32[3,8,128]{2,1,0:T(8,128)S(1)} %get-tuple-element.92), channel_id=1, source_target_pairs={{0,1},{1,2},{2,3},{3,4},{4,5},{5,6},{6,7},{7,0},{8,9},{9,10},{10,1... | collective-permute-start | bytes 36872 | tf_op jit(solution)/shard_map/ppermute | solution.py:962
  15.0 0.8 collective-permute-done.2.tlo
  15.8 2.3 %collective-permute-done.3.thi = f32[3,8,128]{2,1,0:T(8,128)S(1)} collective-permute-done((f32[3,8,128]{2,1,0:T(8,128)S(1)}, f32[3,8,128]{2,1,0:T(8,128)S(1)}, u32[]{:S(2)}, u32[]{:S(2)}) %collective-permute-start.3) | collective-permute-done | bytes 12320 | tf_op jit(solution)/shard_map/ppermute | solution.py:962
  18.1 6.1 %project_kernel.1 = (f32[3,8,64,128]{3,2,1,0:T(8,128)S(1)}, f32[3,8,64,128]{3,2,1,0:T(8,128)S(1)}, f32[3,16,128]{2,1,0:T(8,128)S(1)}, f32[3,16,128]{2,1,0:T(8,128)S(1)}) custom-call(f32[3,8,64,128]{3,2,1,0:T(8,128)S(1)} %get-tuple-element.91.field, f32[3,8,128]{2,1,0:T(8,128)S(1)} %collective-permute-done.2.tlo, ...), custom_call_target="tpu_custom_call" | custom-call | tf_op jit(solution)/shard_map/project_kernel/pallas_call | solution.py:117
  24.2 0.5 collective-permute-start.5
  24.7 0.7 collective-permute-done.4.tlo
  25.4 2.1 %collective-permute-done.5.thi = f32[3,16,128]{2,1,0:T(8,128)S(1)} collective-permute-done((f32[3,16,128]{2,1,0:T(8,128)S(1)}, f32[3,16,128]{2,1,0:T(8,128)S(1)}, u32[]{:S(2)}, u32[]{:S(2)}) %collective-permute-start.5) | collective-permute-done | bytes 24608 | tf_op jit(solution)/shard_map/ppermute | solution.py:962
  27.5 0.3 around_widen_kernel.2
  27.9 5.0 %collective-permute-start.7 = (f32[3,2,72,128]{3,2,1,0:T(8,128)S(1)}, f32[3,2,72,128]{3,2,1,0:T(8,128)S(1)}, u32[]{:S(2)}, u32[]{:S(2)}) collective-permute-start(f32[3,2,72,128]{3,2,1,0:T(8,128)S(1)} %get-tuple-element.103), channel_id=1, source_target_pairs={{8,0},{16,8},{24,16},{32,24},{40,32},{48,40},{56,48},{64,56},{72,6... | collective-permute-start | bytes 663560 | tf_op jit(solution)/shard_map/ppermute | solution.py:962
  32.9 2.0 %solve_tables_kernel.1 = (bf16[112,480]{1,0:T(8,128)(2,1)S(1)}, bf16[64,336]{1,0:T(8,128)(2,1)S(1)}, f32[10,112,128]{2,1,0:T(8,128)S(1)}) custom-call(f32[10,10]{1,0:T(8,128)} %vectors.7, f32[1,10]{1,0:T(1,128)} %bitcast.14, f32[16,256]{1,0:T(8,128)S(1)} %get-tuple-element.80.lanes), custom_call_target="tpu_custom_call" | custom-call | tf_op jit(solution)/shard_map/solve_tables_kernel/pallas_call | solution.py:117
  34.9 3.5 %transform_kernel.2.own = f32[3,10,112,128]{3,2,1,0:T(8,128)S(1)} custom-call(f32[3,8,72,128]{3,2,1,0:T(8,128)S(1)} %get-tuple-element.104.field, bf16[112,480]{1,0:T(8,128)(2,1)S(1)} %get-tuple-element.105.forward, f32[10,10]{1,0:T(8,128)S(1)} %copy-done), custom_call_target="tpu_custom_call" | custom-call | tf_op jit(solution)/shard_map/transform_kernel/pallas_call | solution.py:117
  38.4 4.1 %solve_kernel.2 = (f32[3,8,64,128]{3,2,1,0:T(8,128)S(1)}, f32[3,8,128]{2,1,0:T(8,128)S(1)}, f32[3,8,128]{2,1,0:T(8,128)S(1)}) custom-call(f32[3,10,112,128]{3,2,1,0:T(8,128)S(1)} %transform_kernel.2.own, f32[3,2,72,128]{3,2,1,0:T(8,128)S(1)} %collective-permute-done.6.zlo, f32[3,2,72,128]{3,2,1,0:T(8,128)S(1)} %collective-permute-done.7.zhi, ...), custom_call_target="tpu_custom_call" | custom-call | tf_op jit(solution)/shard_map/solve_kernel/pallas_call | solution.py:117
  42.5 0.4 collective-permute-start.8
  42.9 1.3 collective-permute-start.9
  44.2 0.6 collective-permute-done.8.tlo
  44.9 1.1 collective-permute-done.9.thi
  46.0 0.3 around_sum_kernel.2
  46.4 5.7 %collective-permute-start.11 = (f32[200,128]{1,0:T(8,128)S(1)}, f32[200,128]{1,0:T(8,128)S(1)}, u32[]{:S(2)}, u32[]{:S(2)}) collective-permute-start(f32[200,128]{1,0:T(8,128)S(1)} %get-tuple-element.116), channel_id=1, source_target_pairs={{8,0},{16,8},{24,16},{32,24},{40,32},{48,40},{56,48},{64,56},{72,6... | collective-permute-start | bytes 307208 | tf_op jit(solution)/shard_map/ppermute | solution.py:962
  52.1 2.0 %collective-permute-done.10.zlo = f32[200,128]{1,0:T(8,128)S(1)} collective-permute-done((f32[200,128]{1,0:T(8,128)S(1)}, f32[200,128]{1,0:T(8,128)S(1)}, u32[]{:S(2)}, u32[]{:S(2)}) %collective-permute-start.10) | collective-permute-done | bytes 102432 | tf_op jit(solution)/shard_map/ppermute | solution.py:962
  54.1 1.9 %direction_kernel.2 = (f32[3,8,64,128]{3,2,1,0:T(8,128)S(1)}, f32[128,128]{1,0:T(8,128)S(1)}) custom-call(f32[3,8,64,128]{3,2,1,0:T(8,128)S(1)} %get-tuple-element.114.field, f32[200,128]{1,0:T(8,128)S(1)} %collective-permute-done.10.zlo, f32[200,128]{1,0:T(8,128)S(1)} %collective-permute-done.11.zhi, f32[3,8,64,128]{3,2,1,0:T(8,128)S(1)} %get-tuple-element.99.res, ...), custom_call_target="tpu_custom_call" | custom-call | tf_op jit(solution)/shard_map/direction_kernel/pallas_call | solution.py:117
  56.0 19.4 %all_to_all.16 = f32[128,1,128]{2,1,0:T(1,128)S(1)} all-to-all(f32[128,1,128]{2,1,0:T(1,128)S(1)} %bitcast.11), channel_id=1, replica_groups=mesh['wide'=16,'narrow'=8] {'wide','narrow'}, dimensions={0} | all-to-all | bytes 131072 | tf_op jit(solution)/shard_map/all_to_all | solution.py:1054
  75.4 6.1 %advance_kernel.1 = (f32[3,8,64,128]{3,2,1,0:T(8,128)S(1)}, f32[3,8,64,128]{3,2,1,0:T(8,128)S(1)}, f32[3,16,128]{2,1,0:T(8,128)S(1)}, f32[3,16,128]{2,1,0:T(8,128)S(1)}) custom-call(f32[3,8,64,128]{3,2,1,0:T(8,128)S(1)} %get-tuple-element.98.u_old, f32[3,8,64,128]{3,2,1,0:T(8,128)S(1)} %get-tuple-element.120.d, f32[128,128]{1,0:T(8,128)S(1)} %bitcast.10, ...), custom_call_target="tpu_custom_call" | custom-call | tf_op jit(solution)/shard_map/advance_kernel/pallas_call | solution.py:117
  81.5 0.9 collective-permute-start.12
  82.5 0.9 collective-permute-done.12.tlo
  83.4 2.6 %collective-permute-done.13.thi = f32[3,16,128]{2,1,0:T(8,128)S(1)} collective-permute-done((f32[3,16,128]{2,1,0:T(8,128)S(1)}, f32[3,16,128]{2,1,0:T(8,128)S(1)}, u32[]{:S(2)}, u32[]{:S(2)}) %collective-permute-start.13) | collective-permute-done | bytes 24608 | tf_op jit(solution)/shard_map/ppermute | solution.py:962
  86.0 0.3 around_widen_kernel.3
  86.7 4.6 %collective-permute-start.15 = (f32[3,2,72,128]{3,2,1,0:T(8,128)S(1)}, f32[3,2,72,128]{3,2,1,0:T(8,128)S(1)}, u32[]{:S(2)}, u32[]{:S(2)}) collective-permute-start(f32[3,2,72,128]{3,2,1,0:T(8,128)S(1)} %get-tuple-element.127), channel_id=1, source_target_pairs={{8,0},{16,8},{24,16},{32,24},{40,32},{48,40},{56,48},{64,56},{72,6... | collective-permute-start | bytes 663560 | tf_op jit(solution)/shard_map/ppermute | solution.py:962
  91.2 3.5 %transform_kernel.3.own = f32[3,10,112,128]{3,2,1,0:T(8,128)S(1)} custom-call(f32[3,8,72,128]{3,2,1,0:T(8,128)S(1)} %get-tuple-element.128.field, bf16[112,480]{1,0:T(8,128)(2,1)S(1)} %get-tuple-element.105.forward, f32[10,10]{1,0:T(8,128)S(1)} %copy-done), custom_call_target="tpu_custom_call" | custom-call | tf_op jit(solution)/shard_map/transform_kernel/pallas_call | solution.py:117
  94.7 1.2 collective-permute-done.14.zlo
  96.0 4.1 %solve_kernel.3 = (f32[3,8,64,128]{3,2,1,0:T(8,128)S(1)}, f32[3,8,128]{2,1,0:T(8,128)S(1)}, f32[3,8,128]{2,1,0:T(8,128)S(1)}) custom-call(f32[3,10,112,128]{3,2,1,0:T(8,128)S(1)} %transform_kernel.3.own, f32[3,2,72,128]{3,2,1,0:T(8,128)S(1)} %collective-permute-done.14.zlo, f32[3,2,72,128]{3,2,1,0:T(8,128)S(1)} %collective-permute-done.15.zhi, ...), custom_call_target="tpu_custom_call" | custom-call | tf_op jit(solution)/shard_map/solve_kernel/pallas_call | solution.py:117
  100.1 1.5 %collective-permute-start.16 = (f32[3,8,128]{2,1,0:T(8,128)S(1)}, f32[3,8,128]{2,1,0:T(8,128)S(1)}, u32[]{:S(2)}, u32[]{:S(2)}) collective-permute-start(f32[3,8,128]{2,1,0:T(8,128)S(1)} %get-tuple-element.133), channel_id=1, source_target_pairs={{0,1},{1,2},{2,3},{3,4},{4,5},{5,6},{6,7},{7,0},{8,9},{9,10},{10,1... | collective-permute-start | bytes 36872 | tf_op jit(solution)/shard_map/ppermute | solution.py:962
  101.7 0.7 collective-permute-done.16.tlo
  102.4 2.3 %collective-permute-done.17.thi = f32[3,8,128]{2,1,0:T(8,128)S(1)} collective-permute-done((f32[3,8,128]{2,1,0:T(8,128)S(1)}, f32[3,8,128]{2,1,0:T(8,128)S(1)}, u32[]{:S(2)}, u32[]{:S(2)}) %collective-permute-start.17) | collective-permute-done | bytes 12320 | tf_op jit(solution)/shard_map/ppermute | solution.py:962
  105.1 5.4 %collective-permute-start.19 = (f32[200,128]{1,0:T(8,128)S(1)}, f32[200,128]{1,0:T(8,128)S(1)}, u32[]{:S(2)}, u32[]{:S(2)}) collective-permute-start(f32[200,128]{1,0:T(8,128)S(1)} %get-tuple-element.137), channel_id=1, source_target_pairs={{8,0},{16,8},{24,16},{32,24},{40,32},{48,40},{56,48},{64,56},{72,6... | collective-permute-start | bytes 307208 | tf_op jit(solution)/shard_map/ppermute | solution.py:962
  110.5 0.5 route_kernel.1
  111.3 2.9 %fields_kernel.1 = (f32[6,3,432,256]{3,2,1,0:T(8,128)S(1)}, f32[6,3,144,256]{3,2,1,0:T(8,128)S(1)}) custom-call(f32[3,8,64,128]{3,2,1,0:T(8,128)S(1)} %get-tuple-element.122.u, bf16[432,256]{1,0:T(8,128)(2,1)S(1)} %get-tuple-element.94.fine), custom_call_target="tpu_custom_call" | custom-call | tf_op jit(solution)/shard_map/fields_kernel/pallas_call | solution.py:117
  114.2 0.8 place_base_kernel.1.base
  115.0 1.9 %direction_kernel.3 = (f32[3,8,64,128]{3,2,1,0:T(8,128)S(1)}, f32[128,128]{1,0:T(8,128)S(1)}) custom-call(f32[3,8,64,128]{3,2,1,0:T(8,128)S(1)} %get-tuple-element.135.field, f32[200,128]{1,0:T(8,128)S(1)} %collective-permute-done.18.zlo, f32[200,128]{1,0:T(8,128)S(1)} %collective-permute-done.19.zhi, f32[3,8,64,128]{3,2,1,0:T(8,128)S(1)} %get-tuple-element.123.res, ...), custom_call_target="tpu_custom_call" | custom-call | tf_op jit(solution)/shard_map/direction_kernel/pallas_call | solution.py:117
  116.9 6.1 %change_kernel.1.change = f32[6,8,256]{2,1,0:T(8,128)S(1)} custom-call(f32[3,8,64,128]{3,2,1,0:T(8,128)S(1)} %get-tuple-element.144.d, f32[6,3,432,256]{3,2,1,0:T(8,128)S(1)} %get-tuple-element.148.pf, f32[6,3,144,256]{3,2,1,0:T(8,128)S(1)} %get-tuple-element.149.qf, f32[16,256]{1,0:T(8,128)S(1)} %get-tuple-element.80.lanes, ...), custom_call_target="tpu_custom_call" | custom-call | tf_op jit(solution)/shard_map/change_kernel/pallas_call | solution.py:117
  123.0 2.0 %place_kernel.1 = f32[1280,128]{1,0:T(8,128)} custom-call(f32[3,128,256]{2,1,0:T(8,128)S(1)} %place_base_kernel.1.base, f32[6,8,256]{2,1,0:T(8,128)S(1)} %change_kernel.1.change, bf16[1024,256]{1,0:T(8,128)(2,1)S(1)} %get-tuple-element.140.right, s32[8,128]{1,0:T(8,128)S(1)} %get-tuple-element.141.owner, f32[128,128]{1,0:T(8,128)S(1)} %get-tuple-element.151.part), custom_call_target="tpu_custom_call" | custom-call | tf_op jit(solution)/shard_map/place_kernel/pallas_call | solution.py:117
  125.0 6.9 %all-to-all-start.1 = ((f32[128,1,1280]{2,1,0:T(1,128)}), f32[128,1,1280]{2,1,0:T(1,128)S(1)}, u32[]{:S(2)}, u32[]{:S(2)}) async-start(f32[128,1,1280]{2,1,0:T(1,128)} %bitcast.5), calls=%async_computation.1 | async-start | bytes 1310720 | tf_op jit(solution)/shard_map/all_to_all | solution.py:1132
  131.9 2.3 %store_kernel.1 = (f32[3,8,64,128]{3,2,1,0:T(8,128)}, f32[3,8,64,128]{3,2,1,0:T(8,128)}) custom-call(f32[3,8,64,128]{3,2,1,0:T(8,128)S(1)} %get-tuple-element.122.u, f32[3,8,64,128]{3,2,1,0:T(8,128)S(1)} %get-tuple-element.144.d, s32[1,128]{1,0:T(1,128)S(1)} %copy-done.1), custom_call_target="tpu_custom_call" | custom-call | tf_op jit(solution)/shard_map/store_kernel/pallas_call | solution.py:117
  134.2 12.8 %all-to-all-done.1 = f32[128,1,1280]{2,1,0:T(1,128)S(1)} async-done(((f32[128,1,1280]{2,1,0:T(1,128)}), f32[128,1,1280]{2,1,0:T(1,128)S(1)}, u32[]{:S(2)}, u32[]{:S(2)}) %all-to-all-start.1) | async-done | bytes 655392 | tf_op jit(solution)/shard_map/all_to_all | solution.py:1132
  147.0 2.3 %end_kernel.1 = (f32[3,8,64,128]{3,2,1,0:T(8,128)}, f32[3,136]{1,0:T(4,128)}) custom-call(f32[3,8,64,128]{3,2,1,0:T(8,128)} %get-tuple-element.145.u_hbm, f32[3,8,64,128]{3,2,1,0:T(8,128)} %get-tuple-element.146.d_hbm, f32[1280,128]{1,0:T(8,128)S(1)} %bitcast.9), custom_call_target="tpu_custom_call" | custom-call | tf_op jit(solution)/shard_map/end_kernel/pallas_call | solution.py:117
  (25 shorter events, 1.8 us)
Async XLA Ops:
  1.3 33.6 %copy-start = (f32[10,10]{1,0:T(8,128)S(1)}, f32[10,10]{1,0:T(8,128)}, u32[]{:S(2)}) copy-start(f32[10,10]{1,0:T(8,128)} %vectors.7) | copy-start | bytes 1204
  2.6 9.7 %collective-permute-start = (f32[200,128]{1,0:T(8,128)S(1)}, f32[200,128]{1,0:T(8,128)S(1)}, u32[]{:S(2)}, u32[]{:S(2)}) collective-permute-start(f32[200,128]{1,0:T(8,128)S(1)} %get-tuple-element.78.up), channel_id=1, source_target_pairs={{0,8},{8,16},{16,24},{24,32},{32,40},{40,48},{48,56},{56,64},{64,7... | collective-permute-start | bytes 307208 | tf_op jit(solution)/shard_map/ppermute | solution.py:962
  4.8 7.5 %collective-permute-start.1 = (f32[200,128]{1,0:T(8,128)S(1)}, f32[200,128]{1,0:T(8,128)S(1)}, u32[]{:S(2)}, u32[]{:S(2)}) collective-permute-start(f32[200,128]{1,0:T(8,128)S(1)} %get-tuple-element.79.down), channel_id=1, source_target_pairs={{8,0},{16,8},{24,16},{32,24},{40,32},{48,40},{56,48},{64,56},{72,6... | collective-permute-start | bytes 307208 | tf_op jit(solution)/shard_map/ppermute | solution.py:962
  12.6 3.2 %collective-permute-start.2 = (f32[3,8,128]{2,1,0:T(8,128)S(1)}, f32[3,8,128]{2,1,0:T(8,128)S(1)}, u32[]{:S(2)}, u32[]{:S(2)}) collective-permute-start(f32[3,8,128]{2,1,0:T(8,128)S(1)} %get-tuple-element.92), channel_id=1, source_target_pairs={{0,1},{1,2},{2,3},{3,4},{4,5},{5,6},{6,7},{7,0},{8,9},{9,10},{10,1... | collective-permute-start | bytes 36872 | tf_op jit(solution)/shard_map/ppermute | solution.py:962
  15.0 3.1 %collective-permute-start.3 = (f32[3,8,128]{2,1,0:T(8,128)S(1)}, f32[3,8,128]{2,1,0:T(8,128)S(1)}, u32[]{:S(2)}, u32[]{:S(2)}) collective-permute-start(f32[3,8,128]{2,1,0:T(8,128)S(1)} %get-tuple-element.93), channel_id=1, source_target_pairs={{1,0},{2,1},{3,2},{4,3},{5,4},{6,5},{7,6},{0,7},{9,8},{10,9},{11,1... | collective-permute-start | bytes 36872 | tf_op jit(solution)/shard_map/ppermute | solution.py:962
  24.2 1.2 collective-permute-start.4
  24.2 3.3 %collective-permute-start.5 = (f32[3,16,128]{2,1,0:T(8,128)S(1)}, f32[3,16,128]{2,1,0:T(8,128)S(1)}, u32[]{:S(2)}, u32[]{:S(2)}) collective-permute-start(f32[3,16,128]{2,1,0:T(8,128)S(1)} %get-tuple-element.101), channel_id=1, source_target_pairs={{1,0},{2,1},{3,2},{4,3},{5,4},{6,5},{7,6},{0,7},{9,8},{10,9},{11,1... | collective-permute-start | bytes 73736 | tf_op jit(solution)/shard_map/ppermute | solution.py:962
  27.8 10.6 %collective-permute-start.6 = (f32[3,2,72,128]{3,2,1,0:T(8,128)S(1)}, f32[3,2,72,128]{3,2,1,0:T(8,128)S(1)}, u32[]{:S(2)}, u32[]{:S(2)}) collective-permute-start(f32[3,2,72,128]{3,2,1,0:T(8,128)S(1)} %get-tuple-element.102), channel_id=1, source_target_pairs={{0,8},{8,16},{16,24},{24,32},{32,40},{40,48},{48,56},{56,64},{64,7... | collective-permute-start | bytes 663560 | tf_op jit(solution)/shard_map/ppermute | solution.py:962
  27.9 10.5 %collective-permute-start.7 = (f32[3,2,72,128]{3,2,1,0:T(8,128)S(1)}, f32[3,2,72,128]{3,2,1,0:T(8,128)S(1)}, u32[]{:S(2)}, u32[]{:S(2)}) collective-permute-start(f32[3,2,72,128]{3,2,1,0:T(8,128)S(1)} %get-tuple-element.103), channel_id=1, source_target_pairs={{8,0},{16,8},{24,16},{32,24},{40,32},{48,40},{56,48},{64,56},{72,6... | collective-permute-start | bytes 663560 | tf_op jit(solution)/shard_map/ppermute | solution.py:962
  42.5 2.4 %collective-permute-start.8 = (f32[3,8,128]{2,1,0:T(8,128)S(1)}, f32[3,8,128]{2,1,0:T(8,128)S(1)}, u32[]{:S(2)}, u32[]{:S(2)}) collective-permute-start(f32[3,8,128]{2,1,0:T(8,128)S(1)} %get-tuple-element.112), channel_id=1, source_target_pairs={{0,1},{1,2},{2,3},{3,4},{4,5},{5,6},{6,7},{7,0},{8,9},{9,10},{10,1... | collective-permute-start | bytes 36872 | tf_op jit(solution)/shard_map/ppermute | solution.py:962
  42.9 3.1 %collective-permute-start.9 = (f32[3,8,128]{2,1,0:T(8,128)S(1)}, f32[3,8,128]{2,1,0:T(8,128)S(1)}, u32[]{:S(2)}, u32[]{:S(2)}) collective-permute-start(f32[3,8,128]{2,1,0:T(8,128)S(1)} %get-tuple-element.113), channel_id=1, source_target_pairs={{1,0},{2,1},{3,2},{4,3},{5,4},{6,5},{7,6},{0,7},{9,8},{10,9},{11,1... | collective-permute-start | bytes 36872 | tf_op jit(solution)/shard_map/ppermute | solution.py:962
  46.4 7.7 %collective-permute-start.10 = (f32[200,128]{1,0:T(8,128)S(1)}, f32[200,128]{1,0:T(8,128)S(1)}, u32[]{:S(2)}, u32[]{:S(2)}) collective-permute-start(f32[200,128]{1,0:T(8,128)S(1)} %get-tuple-element.115), channel_id=1, source_target_pairs={{0,8},{8,16},{16,24},{24,32},{32,40},{40,48},{48,56},{56,64},{64,7... | collective-permute-start | bytes 307208 | tf_op jit(solution)/shard_map/ppermute | solution.py:962
  46.4 7.6 %collective-permute-start.11 = (f32[200,128]{1,0:T(8,128)S(1)}, f32[200,128]{1,0:T(8,128)S(1)}, u32[]{:S(2)}, u32[]{:S(2)}) collective-permute-start(f32[200,128]{1,0:T(8,128)S(1)} %get-tuple-element.116), channel_id=1, source_target_pairs={{8,0},{16,8},{24,16},{32,24},{40,32},{48,40},{56,48},{64,56},{72,6... | collective-permute-start | bytes 307208 | tf_op jit(solution)/shard_map/ppermute | solution.py:962
  81.5 1.9 %collective-permute-start.12 = (f32[3,16,128]{2,1,0:T(8,128)S(1)}, f32[3,16,128]{2,1,0:T(8,128)S(1)}, u32[]{:S(2)}, u32[]{:S(2)}) collective-permute-start(f32[3,16,128]{2,1,0:T(8,128)S(1)} %get-tuple-element.124), channel_id=1, source_target_pairs={{0,1},{1,2},{2,3},{3,4},{4,5},{5,6},{6,7},{7,0},{8,9},{9,10},{10,1... | collective-permute-start | bytes 73736 | tf_op jit(solution)/shard_map/ppermute | solution.py:962
  82.5 3.5 %collective-permute-start.13 = (f32[3,16,128]{2,1,0:T(8,128)S(1)}, f32[3,16,128]{2,1,0:T(8,128)S(1)}, u32[]{:S(2)}, u32[]{:S(2)}) collective-permute-start(f32[3,16,128]{2,1,0:T(8,128)S(1)} %get-tuple-element.125), channel_id=1, source_target_pairs={{1,0},{2,1},{3,2},{4,3},{5,4},{6,5},{7,6},{0,7},{9,8},{10,9},{11,1... | collective-permute-start | bytes 73736 | tf_op jit(solution)/shard_map/ppermute | solution.py:962
  86.4 9.6 %collective-permute-start.14 = (f32[3,2,72,128]{3,2,1,0:T(8,128)S(1)}, f32[3,2,72,128]{3,2,1,0:T(8,128)S(1)}, u32[]{:S(2)}, u32[]{:S(2)}) collective-permute-start(f32[3,2,72,128]{3,2,1,0:T(8,128)S(1)} %get-tuple-element.126), channel_id=1, source_target_pairs={{0,8},{8,16},{16,24},{24,32},{32,40},{40,48},{48,56},{56,64},{64,7... | collective-permute-start | bytes 663560 | tf_op jit(solution)/shard_map/ppermute | solution.py:962
  86.7 9.3 %collective-permute-start.15 = (f32[3,2,72,128]{3,2,1,0:T(8,128)S(1)}, f32[3,2,72,128]{3,2,1,0:T(8,128)S(1)}, u32[]{:S(2)}, u32[]{:S(2)}) collective-permute-start(f32[3,2,72,128]{3,2,1,0:T(8,128)S(1)} %get-tuple-element.127), channel_id=1, source_target_pairs={{8,0},{16,8},{24,16},{32,24},{40,32},{48,40},{56,48},{64,56},{72,6... | collective-permute-start | bytes 663560 | tf_op jit(solution)/shard_map/ppermute | solution.py:962
  91.2 19.3 %copy-start.1 = (s32[1,128]{1,0:T(1,128)S(1)}, s32[1,128]{1,0:T(1,128)}, u32[]{:S(2)}) copy-start(s32[1,128]{1,0:T(1,128)} %slot.3) | copy-start | bytes 1540
  91.2 19.3 %copy-start.2 = (s32[8,128]{1,0:T(8,128)S(1)}, s32[8,128]{1,0:T(8,128)}, u32[]{:S(2)}) copy-start(s32[8,128]{1,0:T(8,128)} %corner.1) | copy-start | bytes 12292
  100.1 2.4 %collective-permute-start.16 = (f32[3,8,128]{2,1,0:T(8,128)S(1)}, f32[3,8,128]{2,1,0:T(8,128)S(1)}, u32[]{:S(2)}, u32[]{:S(2)}) collective-permute-start(f32[3,8,128]{2,1,0:T(8,128)S(1)} %get-tuple-element.133), channel_id=1, source_target_pairs={{0,1},{1,2},{2,3},{3,4},{4,5},{5,6},{6,7},{7,0},{8,9},{9,10},{10,1... | collective-permute-start | bytes 36872 | tf_op jit(solution)/shard_map/ppermute | solution.py:962
  101.6 3.1 %collective-permute-start.17 = (f32[3,8,128]{2,1,0:T(8,128)S(1)}, f32[3,8,128]{2,1,0:T(8,128)S(1)}, u32[]{:S(2)}, u32[]{:S(2)}) collective-permute-start(f32[3,8,128]{2,1,0:T(8,128)S(1)} %get-tuple-element.134), channel_id=1, source_target_pairs={{1,0},{2,1},{3,2},{4,3},{5,4},{6,5},{7,6},{0,7},{9,8},{10,9},{11,1... | collective-permute-start | bytes 36872 | tf_op jit(solution)/shard_map/ppermute | solution.py:962
  105.0 10.0 %collective-permute-start.18 = (f32[200,128]{1,0:T(8,128)S(1)}, f32[200,128]{1,0:T(8,128)S(1)}, u32[]{:S(2)}, u32[]{:S(2)}) collective-permute-start(f32[200,128]{1,0:T(8,128)S(1)} %get-tuple-element.136), channel_id=1, source_target_pairs={{0,8},{8,16},{16,24},{24,32},{32,40},{40,48},{48,56},{56,64},{64,7... | collective-permute-start | bytes 307208 | tf_op jit(solution)/shard_map/ppermute | solution.py:962
  105.1 9.9 %collective-permute-start.19 = (f32[200,128]{1,0:T(8,128)S(1)}, f32[200,128]{1,0:T(8,128)S(1)}, u32[]{:S(2)}, u32[]{:S(2)}) collective-permute-start(f32[200,128]{1,0:T(8,128)S(1)} %get-tuple-element.137), channel_id=1, source_target_pairs={{8,0},{16,8},{24,16},{32,24},{40,32},{48,40},{56,48},{64,56},{72,6... | collective-permute-start | bytes 307208 | tf_op jit(solution)/shard_map/ppermute | solution.py:962
  125.0 22.0 %all-to-all-start.1 = ((f32[128,1,1280]{2,1,0:T(1,128)}), f32[128,1,1280]{2,1,0:T(1,128)S(1)}, u32[]{:S(2)}, u32[]{:S(2)}) async-start(f32[128,1,1280]{2,1,0:T(1,128)} %bitcast.5), calls=%async_computation.1 | async-start | bytes 1310720 | tf_op jit(solution)/shard_map/all_to_all | solution.py:1132

commit v6 on v5

--- a/solution.py
+++ b/solution.py
@@ -920,15 +920,17 @@
 
 def end_kernel(u_hbm, d_hbm, parts, vel_hbm, coarse_hbm, u, d, vel, coarse, sems):
     last = pltpu.make_async_copy(coarse, coarse_hbm, sems.at[0])
+    pieces = [(c, pl.ds(4 * h, 4)) for c in range(3) for h in range(2)]
     loads = [
         [
-            pltpu.make_async_copy(a.at[c], b.at[c], sems.at[1 + 2 * c + n])
+            pltpu.make_async_copy(a.at[at], b.at[at], sems.at[1 + 2 * m + n])
             for n, (a, b) in enumerate(((u_hbm, u), (d_hbm, d)))
         ]
-        for c in range(3)
+        for m, at in enumerate(pieces)
     ]
     stores = [
-        pltpu.make_async_copy(vel.at[c], vel_hbm.at[c], sems.at[7 + c]) for c in range(3)
+        pltpu.make_async_copy(vel.at[at], vel_hbm.at[at], sems.at[13 + m])
+        for m, at in enumerate(pieces)
     ]
     for pair in loads:
         for copy in pair:
@@ -937,11 +939,11 @@
         jnp.sum(parts[pl.ds(n, 128, stride=10)], axis=0, keepdims=True) for n in range(10)
     ]
     alpha = sums[9][:, 72:73] / sums[9][:, 73:74]
-    for c in range(3):
-        for copy in loads[c]:
+    for m, at in enumerate(pieces):
+        for copy in loads[m]:
             copy.wait()
-        vel[c] = u[c] + alpha * d[c]
-        stores[c].start()
+        vel[at] = u[at] + alpha * d[at]
+        stores[m].start()
     total = jnp.concatenate(sums, axis=1)
     one, two = lanes_by(total, -408), lanes_by(total, -816)
     both = total + alpha * (one + alpha * two)
@@ -959,7 +961,8 @@
     n = lax.axis_size(axis)
     up = [(i, (i + 1) % n) for i in range(n)]
     down = [((i + 1) % n, i) for i in range(n)]
-    return lax.ppermute(to_next, axis, up), lax.ppermute(to_prev, axis, down)
+    from_next = lax.ppermute(to_prev, axis, down)
+    return lax.ppermute(to_next, axis, up), from_next
 
 
 def fine_scratch():
@@ -1148,7 +1151,7 @@
             pltpu.VMEM(FIELD, F32),
             pltpu.VMEM(FIELD, F32),
             pltpu.VMEM((3, 136), F32),
-            pltpu.SemaphoreType.DMA((10,)),
+            pltpu.SemaphoreType.DMA((19,)),
         ],
         spaces={0: pltpu.HBM, 1: pltpu.HBM},
         hbm_out={0, 1},

time: 150 us -> 150 us (level)
  no operation moved by 1% of the time
where the time goes in v6:
time: 150 us
  Pallas kernels  55.5 us (37%)
  starting transfers between devices  42.4 us (28%)
  waiting for transfers between devices  30.5 us (20%)
  blocking collectives  19.4 us (13%)
  between operations  1.7 us (1%)
    pallas_call x24, Pallas kernels, call(): pl.pallas_call(kernel, out_shape=[(pltpu.HBM if i in hbm_out else pltpu.V...  55.5 us
    ppermute x10, starting transfers between devices, both_ways(): from_next = lax.ppermute(to_prev, axis, down)  27.5 us
    all_to_all x1, blocking collectives, shards(): sums = lax.all_to_all(part, BOTH, 0, 0, tiled=True)  19.4 us
    all_to_all x1, waiting for transfers between devices, shards(): parts = lax.all_to_all(dense.reshape(128, 1, 1280), BOTH, 0, 0, tiled=True)  12.8 us
    ppermute x10, waiting for transfers between devices, both_ways(): from_next = lax.ppermute(to_prev, axis, down)  10.4 us
    ppermute x10, starting transfers between devices, both_ways(): return (lax.ppermute(to_next, axis, up), from_next)  7.99 us
    ppermute x10, waiting for transfers between devices, both_ways(): return (lax.ppermute(to_next, axis, up), from_next)  7.27 us
    all_to_all x1, starting transfers between devices, shards(): parts = lax.all_to_all(dense.reshape(128, 1, 1280), BOTH, 0, 0, tiled=True)  6.86 us
  transfers between devices with their start and end apart: 21, of which 14 were waited for; matrix products, arithmetic and copies ran while one was open for 0% of the time, Pallas kernels for 12%

profile of v6, /device:TPU:1, one launch (start us, length us, event | category | flops | bytes accessed | tf_op | source)
XLA Modules:
  0.0 149.6 jit_solution(1678429563518639636)
XLA Ops:
  1.3 1.3 faces_kernel.1
  2.6 2.2 %collective-permute-start = (f32[200,128]{1,0:T(8,128)S(1)}, f32[200,128]{1,0:T(8,128)S(1)}, u32[]{:S(2)}, u32[]{:S(2)}) collective-permute-start(f32[200,128]{1,0:T(8,128)S(1)} %get-tuple-element.78.up), channel_id=1, source_target_pairs={{0,8},{8,16},{16,24},{24,32},{32,40},{40,48},{48,56},{56,64},{64,7... | collective-permute-start | bytes 307208 | tf_op jit(solution)/shard_map/ppermute | solution.py:965
  4.8 5.0 %collective-permute-start.1 = (f32[200,128]{1,0:T(8,128)S(1)}, f32[200,128]{1,0:T(8,128)S(1)}, u32[]{:S(2)}, u32[]{:S(2)}) collective-permute-start(f32[200,128]{1,0:T(8,128)S(1)} %get-tuple-element.79.down), channel_id=1, source_target_pairs={{8,0},{16,8},{24,16},{32,24},{40,32},{48,40},{56,48},{64,56},{72,6... | collective-permute-start | bytes 307208 | tf_op jit(solution)/shard_map/ppermute | solution.py:964
  9.8 2.3 %inner_kernel.1 = (f32[3,6,64,128]{3,2,1,0:T(8,128)S(1)}, bf16[432,256]{1,0:T(8,128)(2,1)S(1)}, bf16[64,432]{1,0:T(8,128)(2,1)S(1)}, bf16[128,256]{1,0:T(8,128)(...) custom-call(f32[3,8,64,128]{3,2,1,0:T(8,128)} %bitcast.13, ...), custom_call_target="tpu_custom_call" | custom-call | tf_op jit(solution)/shard_map/inner_kernel/pallas_call | solution.py:117
  12.6 2.3 %collective-permute-start.2 = (f32[3,8,128]{2,1,0:T(8,128)S(1)}, f32[3,8,128]{2,1,0:T(8,128)S(1)}, u32[]{:S(2)}, u32[]{:S(2)}) collective-permute-start(f32[3,8,128]{2,1,0:T(8,128)S(1)} %get-tuple-element.92), channel_id=1, source_target_pairs={{0,1},{1,2},{2,3},{3,4},{4,5},{5,6},{6,7},{7,0},{8,9},{9,10},{10,1... | collective-permute-start | bytes 36872 | tf_op jit(solution)/shard_map/ppermute | solution.py:965
  15.0 0.8 collective-permute-done.2.tlo
  15.8 2.3 %collective-permute-done.3.thi = f32[3,8,128]{2,1,0:T(8,128)S(1)} collective-permute-done((f32[3,8,128]{2,1,0:T(8,128)S(1)}, f32[3,8,128]{2,1,0:T(8,128)S(1)}, u32[]{:S(2)}, u32[]{:S(2)}) %collective-permute-start.3) | collective-permute-done | bytes 12320 | tf_op jit(solution)/shard_map/ppermute | solution.py:964
  18.1 6.1 %project_kernel.1 = (f32[3,8,64,128]{3,2,1,0:T(8,128)S(1)}, f32[3,8,64,128]{3,2,1,0:T(8,128)S(1)}, f32[3,16,128]{2,1,0:T(8,128)S(1)}, f32[3,16,128]{2,1,0:T(8,128)S(1)}) custom-call(f32[3,8,64,128]{3,2,1,0:T(8,128)S(1)} %get-tuple-element.91.field, f32[3,8,128]{2,1,0:T(8,128)S(1)} %collective-permute-done.2.tlo, ...), custom_call_target="tpu_custom_call" | custom-call | tf_op jit(solution)/shard_map/project_kernel/pallas_call | solution.py:117
  24.2 0.5 collective-permute-start.5
  24.7 0.7 collective-permute-done.4.tlo
  25.4 2.1 %collective-permute-done.5.thi = f32[3,16,128]{2,1,0:T(8,128)S(1)} collective-permute-done((f32[3,16,128]{2,1,0:T(8,128)S(1)}, f32[3,16,128]{2,1,0:T(8,128)S(1)}, u32[]{:S(2)}, u32[]{:S(2)}) %collective-permute-start.5) | collective-permute-done | bytes 24608 | tf_op jit(solution)/shard_map/ppermute | solution.py:964
  27.5 0.3 around_widen_kernel.2
  27.9 5.0 %collective-permute-start.7 = (f32[3,2,72,128]{3,2,1,0:T(8,128)S(1)}, f32[3,2,72,128]{3,2,1,0:T(8,128)S(1)}, u32[]{:S(2)}, u32[]{:S(2)}) collective-permute-start(f32[3,2,72,128]{3,2,1,0:T(8,128)S(1)} %get-tuple-element.103), channel_id=1, source_target_pairs={{8,0},{16,8},{24,16},{32,24},{40,32},{48,40},{56,48},{64,56},{72,6... | collective-permute-start | bytes 663560 | tf_op jit(solution)/shard_map/ppermute | solution.py:964
  32.9 2.0 %solve_tables_kernel.1 = (bf16[112,480]{1,0:T(8,128)(2,1)S(1)}, bf16[64,336]{1,0:T(8,128)(2,1)S(1)}, f32[10,112,128]{2,1,0:T(8,128)S(1)}) custom-call(f32[10,10]{1,0:T(8,128)} %vectors.7, f32[1,10]{1,0:T(1,128)} %bitcast.14, f32[16,256]{1,0:T(8,128)S(1)} %get-tuple-element.80.lanes), custom_call_target="tpu_custom_call" | custom-call | tf_op jit(solution)/shard_map/solve_tables_kernel/pallas_call | solution.py:117
  34.9 3.5 %transform_kernel.2.own = f32[3,10,112,128]{3,2,1,0:T(8,128)S(1)} custom-call(f32[3,8,72,128]{3,2,1,0:T(8,128)S(1)} %get-tuple-element.104.field, bf16[112,480]{1,0:T(8,128)(2,1)S(1)} %get-tuple-element.105.forward, f32[10,10]{1,0:T(8,128)S(1)} %copy-done), custom_call_target="tpu_custom_call" | custom-call | tf_op jit(solution)/shard_map/transform_kernel/pallas_call | solution.py:117
  38.4 4.1 %solve_kernel.2 = (f32[3,8,64,128]{3,2,1,0:T(8,128)S(1)}, f32[3,8,128]{2,1,0:T(8,128)S(1)}, f32[3,8,128]{2,1,0:T(8,128)S(1)}) custom-call(f32[3,10,112,128]{3,2,1,0:T(8,128)S(1)} %transform_kernel.2.own, f32[3,2,72,128]{3,2,1,0:T(8,128)S(1)} %collective-permute-done.6.zlo, f32[3,2,72,128]{3,2,1,0:T(8,128)S(1)} %collective-permute-done.7.zhi, ...), custom_call_target="tpu_custom_call" | custom-call | tf_op jit(solution)/shard_map/solve_kernel/pallas_call | solution.py:117
  42.5 0.4 collective-permute-start.8
  42.9 1.3 collective-permute-start.9
  44.2 0.6 collective-permute-done.8.tlo
  44.9 1.1 collective-permute-done.9.thi
  46.0 0.3 around_sum_kernel.2
  46.4 5.7 %collective-permute-start.11 = (f32[200,128]{1,0:T(8,128)S(1)}, f32[200,128]{1,0:T(8,128)S(1)}, u32[]{:S(2)}, u32[]{:S(2)}) collective-permute-start(f32[200,128]{1,0:T(8,128)S(1)} %get-tuple-element.116), channel_id=1, source_target_pairs={{8,0},{16,8},{24,16},{32,24},{40,32},{48,40},{56,48},{64,56},{72,6... | collective-permute-start | bytes 307208 | tf_op jit(solution)/shard_map/ppermute | solution.py:964
  52.1 2.0 %collective-permute-done.10.zlo = f32[200,128]{1,0:T(8,128)S(1)} collective-permute-done((f32[200,128]{1,0:T(8,128)S(1)}, f32[200,128]{1,0:T(8,128)S(1)}, u32[]{:S(2)}, u32[]{:S(2)}) %collective-permute-start.10) | collective-permute-done | bytes 102432 | tf_op jit(solution)/shard_map/ppermute | solution.py:965
  54.1 1.9 %direction_kernel.2 = (f32[3,8,64,128]{3,2,1,0:T(8,128)S(1)}, f32[128,128]{1,0:T(8,128)S(1)}) custom-call(f32[3,8,64,128]{3,2,1,0:T(8,128)S(1)} %get-tuple-element.114.field, f32[200,128]{1,0:T(8,128)S(1)} %collective-permute-done.10.zlo, f32[200,128]{1,0:T(8,128)S(1)} %collective-permute-done.11.zhi, f32[3,8,64,128]{3,2,1,0:T(8,128)S(1)} %get-tuple-element.99.res, ...), custom_call_target="tpu_custom_call" | custom-call | tf_op jit(solution)/shard_map/direction_kernel/pallas_call | solution.py:117
  56.0 19.4 %all_to_all.16 = f32[128,1,128]{2,1,0:T(1,128)S(1)} all-to-all(f32[128,1,128]{2,1,0:T(1,128)S(1)} %bitcast.11), channel_id=1, replica_groups=mesh['wide'=16,'narrow'=8] {'wide','narrow'}, dimensions={0} | all-to-all | bytes 131072 | tf_op jit(solution)/shard_map/all_to_all | solution.py:1057
  75.4 6.1 %advance_kernel.1 = (f32[3,8,64,128]{3,2,1,0:T(8,128)S(1)}, f32[3,8,64,128]{3,2,1,0:T(8,128)S(1)}, f32[3,16,128]{2,1,0:T(8,128)S(1)}, f32[3,16,128]{2,1,0:T(8,128)S(1)}) custom-call(f32[3,8,64,128]{3,2,1,0:T(8,128)S(1)} %get-tuple-element.98.u_old, f32[3,8,64,128]{3,2,1,0:T(8,128)S(1)} %get-tuple-element.120.d, f32[128,128]{1,0:T(8,128)S(1)} %bitcast.10, ...), custom_call_target="tpu_custom_call" | custom-call | tf_op jit(solution)/shard_map/advance_kernel/pallas_call | solution.py:117
  81.5 0.9 collective-permute-start.12
  82.5 0.9 collective-permute-done.12.tlo
  83.4 2.6 %collective-permute-done.13.thi = f32[3,16,128]{2,1,0:T(8,128)S(1)} collective-permute-done((f32[3,16,128]{2,1,0:T(8,128)S(1)}, f32[3,16,128]{2,1,0:T(8,128)S(1)}, u32[]{:S(2)}, u32[]{:S(2)}) %collective-permute-start.13) | collective-permute-done | bytes 24608 | tf_op jit(solution)/shard_map/ppermute | solution.py:964
  86.0 0.3 around_widen_kernel.3
  86.7 4.6 %collective-permute-start.15 = (f32[3,2,72,128]{3,2,1,0:T(8,128)S(1)}, f32[3,2,72,128]{3,2,1,0:T(8,128)S(1)}, u32[]{:S(2)}, u32[]{:S(2)}) collective-permute-start(f32[3,2,72,128]{3,2,1,0:T(8,128)S(1)} %get-tuple-element.127), channel_id=1, source_target_pairs={{8,0},{16,8},{24,16},{32,24},{40,32},{48,40},{56,48},{64,56},{72,6... | collective-permute-start | bytes 663560 | tf_op jit(solution)/shard_map/ppermute | solution.py:964
  91.2 3.5 %transform_kernel.3.own = f32[3,10,112,128]{3,2,1,0:T(8,128)S(1)} custom-call(f32[3,8,72,128]{3,2,1,0:T(8,128)S(1)} %get-tuple-element.128.field, bf16[112,480]{1,0:T(8,128)(2,1)S(1)} %get-tuple-element.105.forward, f32[10,10]{1,0:T(8,128)S(1)} %copy-done), custom_call_target="tpu_custom_call" | custom-call | tf_op jit(solution)/shard_map/transform_kernel/pallas_call | solution.py:117
  94.7 1.2 collective-permute-done.14.zlo
  96.0 4.1 %solve_kernel.3 = (f32[3,8,64,128]{3,2,1,0:T(8,128)S(1)}, f32[3,8,128]{2,1,0:T(8,128)S(1)}, f32[3,8,128]{2,1,0:T(8,128)S(1)}) custom-call(f32[3,10,112,128]{3,2,1,0:T(8,128)S(1)} %transform_kernel.3.own, f32[3,2,72,128]{3,2,1,0:T(8,128)S(1)} %collective-permute-done.14.zlo, f32[3,2,72,128]{3,2,1,0:T(8,128)S(1)} %collective-permute-done.15.zhi, ...), custom_call_target="tpu_custom_call" | custom-call | tf_op jit(solution)/shard_map/solve_kernel/pallas_call | solution.py:117
  100.1 1.5 %collective-permute-start.16 = (f32[3,8,128]{2,1,0:T(8,128)S(1)}, f32[3,8,128]{2,1,0:T(8,128)S(1)}, u32[]{:S(2)}, u32[]{:S(2)}) collective-permute-start(f32[3,8,128]{2,1,0:T(8,128)S(1)} %get-tuple-element.133), channel_id=1, source_target_pairs={{0,1},{1,2},{2,3},{3,4},{4,5},{5,6},{6,7},{7,0},{8,9},{9,10},{10,1... | collective-permute-start | bytes 36872 | tf_op jit(solution)/shard_map/ppermute | solution.py:965
  101.7 0.7 collective-permute-done.16.tlo
  102.4 2.3 %collective-permute-done.17.thi = f32[3,8,128]{2,1,0:T(8,128)S(1)} collective-permute-done((f32[3,8,128]{2,1,0:T(8,128)S(1)}, f32[3,8,128]{2,1,0:T(8,128)S(1)}, u32[]{:S(2)}, u32[]{:S(2)}) %collective-permute-start.17) | collective-permute-done | bytes 12320 | tf_op jit(solution)/shard_map/ppermute | solution.py:964
  105.1 5.4 %collective-permute-start.19 = (f32[200,128]{1,0:T(8,128)S(1)}, f32[200,128]{1,0:T(8,128)S(1)}, u32[]{:S(2)}, u32[]{:S(2)}) collective-permute-start(f32[200,128]{1,0:T(8,128)S(1)} %get-tuple-element.137), channel_id=1, source_target_pairs={{8,0},{16,8},{24,16},{32,24},{40,32},{48,40},{56,48},{64,56},{72,6... | collective-permute-start | bytes 307208 | tf_op jit(solution)/shard_map/ppermute | solution.py:964
  110.5 0.5 route_kernel.1
  111.3 2.9 %fields_kernel.1 = (f32[6,3,432,256]{3,2,1,0:T(8,128)S(1)}, f32[6,3,144,256]{3,2,1,0:T(8,128)S(1)}) custom-call(f32[3,8,64,128]{3,2,1,0:T(8,128)S(1)} %get-tuple-element.122.u, bf16[432,256]{1,0:T(8,128)(2,1)S(1)} %get-tuple-element.94.fine), custom_call_target="tpu_custom_call" | custom-call | tf_op jit(solution)/shard_map/fields_kernel/pallas_call | solution.py:117
  114.2 0.8 place_base_kernel.1.base
  115.0 1.9 %direction_kernel.3 = (f32[3,8,64,128]{3,2,1,0:T(8,128)S(1)}, f32[128,128]{1,0:T(8,128)S(1)}) custom-call(f32[3,8,64,128]{3,2,1,0:T(8,128)S(1)} %get-tuple-element.135.field, f32[200,128]{1,0:T(8,128)S(1)} %collective-permute-done.18.zlo, f32[200,128]{1,0:T(8,128)S(1)} %collective-permute-done.19.zhi, f32[3,8,64,128]{3,2,1,0:T(8,128)S(1)} %get-tuple-element.123.res, ...), custom_call_target="tpu_custom_call" | custom-call | tf_op jit(solution)/shard_map/direction_kernel/pallas_call | solution.py:117
  116.9 6.1 %change_kernel.1.change = f32[6,8,256]{2,1,0:T(8,128)S(1)} custom-call(f32[3,8,64,128]{3,2,1,0:T(8,128)S(1)} %get-tuple-element.144.d, f32[6,3,432,256]{3,2,1,0:T(8,128)S(1)} %get-tuple-element.148.pf, f32[6,3,144,256]{3,2,1,0:T(8,128)S(1)} %get-tuple-element.149.qf, f32[16,256]{1,0:T(8,128)S(1)} %get-tuple-element.80.lanes, ...), custom_call_target="tpu_custom_call" | custom-call | tf_op jit(solution)/shard_map/change_kernel/pallas_call | solution.py:117
  123.0 2.0 %place_kernel.1 = f32[1280,128]{1,0:T(8,128)} custom-call(f32[3,128,256]{2,1,0:T(8,128)S(1)} %place_base_kernel.1.base, f32[6,8,256]{2,1,0:T(8,128)S(1)} %change_kernel.1.change, bf16[1024,256]{1,0:T(8,128)(2,1)S(1)} %get-tuple-element.140.right, s32[8,128]{1,0:T(8,128)S(1)} %get-tuple-element.141.owner, f32[128,128]{1,0:T(8,128)S(1)} %get-tuple-element.151.part), custom_call_target="tpu_custom_call" | custom-call | tf_op jit(solution)/shard_map/place_kernel/pallas_call | solution.py:117
  125.0 6.9 %all-to-all-start.1 = ((f32[128,1,1280]{2,1,0:T(1,128)}), f32[128,1,1280]{2,1,0:T(1,128)S(1)}, u32[]{:S(2)}, u32[]{:S(2)}) async-start(f32[128,1,1280]{2,1,0:T(1,128)} %bitcast.5), calls=%async_computation.1 | async-start | bytes 1310720 | tf_op jit(solution)/shard_map/all_to_all | solution.py:1135
  131.9 2.3 %store_kernel.1 = (f32[3,8,64,128]{3,2,1,0:T(8,128)}, f32[3,8,64,128]{3,2,1,0:T(8,128)}) custom-call(f32[3,8,64,128]{3,2,1,0:T(8,128)S(1)} %get-tuple-element.122.u, f32[3,8,64,128]{3,2,1,0:T(8,128)S(1)} %get-tuple-element.144.d, s32[1,128]{1,0:T(1,128)S(1)} %copy-done.1), custom_call_target="tpu_custom_call" | custom-call | tf_op jit(solution)/shard_map/store_kernel/pallas_call | solution.py:117
  134.2 12.8 %all-to-all-done.1 = f32[128,1,1280]{2,1,0:T(1,128)S(1)} async-done(((f32[128,1,1280]{2,1,0:T(1,128)}), f32[128,1,1280]{2,1,0:T(1,128)S(1)}, u32[]{:S(2)}, u32[]{:S(2)}) %all-to-all-start.1) | async-done | bytes 655392 | tf_op jit(solution)/shard_map/all_to_all | solution.py:1135
  147.0 2.4 %end_kernel.1 = (f32[3,8,64,128]{3,2,1,0:T(8,128)}, f32[3,136]{1,0:T(4,128)}) custom-call(f32[3,8,64,128]{3,2,1,0:T(8,128)} %get-tuple-element.145.u_hbm, f32[3,8,64,128]{3,2,1,0:T(8,128)} %get-tuple-element.146.d_hbm, f32[1280,128]{1,0:T(8,128)S(1)} %bitcast.9), custom_call_target="tpu_custom_call" | custom-call | tf_op jit(solution)/shard_map/end_kernel/pallas_call | solution.py:117
  (25 shorter events, 1.8 us)
Async XLA Ops:
  1.3 33.6 %copy-start = (f32[10,10]{1,0:T(8,128)S(1)}, f32[10,10]{1,0:T(8,128)}, u32[]{:S(2)}) copy-start(f32[10,10]{1,0:T(8,128)} %vectors.7) | copy-start | bytes 1204
  2.6 9.7 %collective-permute-start = (f32[200,128]{1,0:T(8,128)S(1)}, f32[200,128]{1,0:T(8,128)S(1)}, u32[]{:S(2)}, u32[]{:S(2)}) collective-permute-start(f32[200,128]{1,0:T(8,128)S(1)} %get-tuple-element.78.up), channel_id=1, source_target_pairs={{0,8},{8,16},{16,24},{24,32},{32,40},{40,48},{48,56},{56,64},{64,7... | collective-permute-start | bytes 307208 | tf_op jit(solution)/shard_map/ppermute | solution.py:965
  4.8 7.5 %collective-permute-start.1 = (f32[200,128]{1,0:T(8,128)S(1)}, f32[200,128]{1,0:T(8,128)S(1)}, u32[]{:S(2)}, u32[]{:S(2)}) collective-permute-start(f32[200,128]{1,0:T(8,128)S(1)} %get-tuple-element.79.down), channel_id=1, source_target_pairs={{8,0},{16,8},{24,16},{32,24},{40,32},{48,40},{56,48},{64,56},{72,6... | collective-permute-start | bytes 307208 | tf_op jit(solution)/shard_map/ppermute | solution.py:964
  12.6 3.2 %collective-permute-start.2 = (f32[3,8,128]{2,1,0:T(8,128)S(1)}, f32[3,8,128]{2,1,0:T(8,128)S(1)}, u32[]{:S(2)}, u32[]{:S(2)}) collective-permute-start(f32[3,8,128]{2,1,0:T(8,128)S(1)} %get-tuple-element.92), channel_id=1, source_target_pairs={{0,1},{1,2},{2,3},{3,4},{4,5},{5,6},{6,7},{7,0},{8,9},{9,10},{10,1... | collective-permute-start | bytes 36872 | tf_op jit(solution)/shard_map/ppermute | solution.py:965
  15.0 3.1 %collective-permute-start.3 = (f32[3,8,128]{2,1,0:T(8,128)S(1)}, f32[3,8,128]{2,1,0:T(8,128)S(1)}, u32[]{:S(2)}, u32[]{:S(2)}) collective-permute-start(f32[3,8,128]{2,1,0:T(8,128)S(1)} %get-tuple-element.93), channel_id=1, source_target_pairs={{1,0},{2,1},{3,2},{4,3},{5,4},{6,5},{7,6},{0,7},{9,8},{10,9},{11,1... | collective-permute-start | bytes 36872 | tf_op jit(solution)/shard_map/ppermute | solution.py:964
  24.2 1.2 collective-permute-start.4
  24.2 3.3 %collective-permute-start.5 = (f32[3,16,128]{2,1,0:T(8,128)S(1)}, f32[3,16,128]{2,1,0:T(8,128)S(1)}, u32[]{:S(2)}, u32[]{:S(2)}) collective-permute-start(f32[3,16,128]{2,1,0:T(8,128)S(1)} %get-tuple-element.101), channel_id=1, source_target_pairs={{1,0},{2,1},{3,2},{4,3},{5,4},{6,5},{7,6},{0,7},{9,8},{10,9},{11,1... | collective-permute-start | bytes 73736 | tf_op jit(solution)/shard_map/ppermute | solution.py:964
  27.8 10.6 %collective-permute-start.6 = (f32[3,2,72,128]{3,2,1,0:T(8,128)S(1)}, f32[3,2,72,128]{3,2,1,0:T(8,128)S(1)}, u32[]{:S(2)}, u32[]{:S(2)}) collective-permute-start(f32[3,2,72,128]{3,2,1,0:T(8,128)S(1)} %get-tuple-element.102), channel_id=1, source_target_pairs={{0,8},{8,16},{16,24},{24,32},{32,40},{40,48},{48,56},{56,64},{64,7... | collective-permute-start | bytes 663560 | tf_op jit(solution)/shard_map/ppermute | solution.py:965
  27.9 10.5 %collective-permute-start.7 = (f32[3,2,72,128]{3,2,1,0:T(8,128)S(1)}, f32[3,2,72,128]{3,2,1,0:T(8,128)S(1)}, u32[]{:S(2)}, u32[]{:S(2)}) collective-permute-start(f32[3,2,72,128]{3,2,1,0:T(8,128)S(1)} %get-tuple-element.103), channel_id=1, source_target_pairs={{8,0},{16,8},{24,16},{32,24},{40,32},{48,40},{56,48},{64,56},{72,6... | collective-permute-start | bytes 663560 | tf_op jit(solution)/shard_map/ppermute | solution.py:964
  42.5 2.4 %collective-permute-start.8 = (f32[3,8,128]{2,1,0:T(8,128)S(1)}, f32[3,8,128]{2,1,0:T(8,128)S(1)}, u32[]{:S(2)}, u32[]{:S(2)}) collective-permute-start(f32[3,8,128]{2,1,0:T(8,128)S(1)} %get-tuple-element.112), channel_id=1, source_target_pairs={{0,1},{1,2},{2,3},{3,4},{4,5},{5,6},{6,7},{7,0},{8,9},{9,10},{10,1... | collective-permute-start | bytes 36872 | tf_op jit(solution)/shard_map/ppermute | solution.py:965
  42.9 3.1 %collective-permute-start.9 = (f32[3,8,128]{2,1,0:T(8,128)S(1)}, f32[3,8,128]{2,1,0:T(8,128)S(1)}, u32[]{:S(2)}, u32[]{:S(2)}) collective-permute-start(f32[3,8,128]{2,1,0:T(8,128)S(1)} %get-tuple-element.113), channel_id=1, source_target_pairs={{1,0},{2,1},{3,2},{4,3},{5,4},{6,5},{7,6},{0,7},{9,8},{10,9},{11,1... | collective-permute-start | bytes 36872 | tf_op jit(solution)/shard_map/ppermute | solution.py:964
  46.4 7.7 %collective-permute-start.10 = (f32[200,128]{1,0:T(8,128)S(1)}, f32[200,128]{1,0:T(8,128)S(1)}, u32[]{:S(2)}, u32[]{:S(2)}) collective-permute-start(f32[200,128]{1,0:T(8,128)S(1)} %get-tuple-element.115), channel_id=1, source_target_pairs={{0,8},{8,16},{16,24},{24,32},{32,40},{40,48},{48,56},{56,64},{64,7... | collective-permute-start | bytes 307208 | tf_op jit(solution)/shard_map/ppermute | solution.py:965
  46.4 7.6 %collective-permute-start.11 = (f32[200,128]{1,0:T(8,128)S(1)}, f32[200,128]{1,0:T(8,128)S(1)}, u32[]{:S(2)}, u32[]{:S(2)}) collective-permute-start(f32[200,128]{1,0:T(8,128)S(1)} %get-tuple-element.116), channel_id=1, source_target_pairs={{8,0},{16,8},{24,16},{32,24},{40,32},{48,40},{56,48},{64,56},{72,6... | collective-permute-start | bytes 307208 | tf_op jit(solution)/shard_map/ppermute | solution.py:964
  81.5 1.9 %collective-permute-start.12 = (f32[3,16,128]{2,1,0:T(8,128)S(1)}, f32[3,16,128]{2,1,0:T(8,128)S(1)}, u32[]{:S(2)}, u32[]{:S(2)}) collective-permute-start(f32[3,16,128]{2,1,0:T(8,128)S(1)} %get-tuple-element.124), channel_id=1, source_target_pairs={{0,1},{1,2},{2,3},{3,4},{4,5},{5,6},{6,7},{7,0},{8,9},{9,10},{10,1... | collective-permute-start | bytes 73736 | tf_op jit(solution)/shard_map/ppermute | solution.py:965
  82.5 3.5 %collective-permute-start.13 = (f32[3,16,128]{2,1,0:T(8,128)S(1)}, f32[3,16,128]{2,1,0:T(8,128)S(1)}, u32[]{:S(2)}, u32[]{:S(2)}) collective-permute-start(f32[3,16,128]{2,1,0:T(8,128)S(1)} %get-tuple-element.125), channel_id=1, source_target_pairs={{1,0},{2,1},{3,2},{4,3},{5,4},{6,5},{7,6},{0,7},{9,8},{10,9},{11,1... | collective-permute-start | bytes 73736 | tf_op jit(solution)/shard_map/ppermute | solution.py:964
  86.4 9.6 %collective-permute-start.14 = (f32[3,2,72,128]{3,2,1,0:T(8,128)S(1)}, f32[3,2,72,128]{3,2,1,0:T(8,128)S(1)}, u32[]{:S(2)}, u32[]{:S(2)}) collective-permute-start(f32[3,2,72,128]{3,2,1,0:T(8,128)S(1)} %get-tuple-element.126), channel_id=1, source_target_pairs={{0,8},{8,16},{16,24},{24,32},{32,40},{40,48},{48,56},{56,64},{64,7... | collective-permute-start | bytes 663560 | tf_op jit(solution)/shard_map/ppermute | solution.py:965
  86.7 9.3 %collective-permute-start.15 = (f32[3,2,72,128]{3,2,1,0:T(8,128)S(1)}, f32[3,2,72,128]{3,2,1,0:T(8,128)S(1)}, u32[]{:S(2)}, u32[]{:S(2)}) collective-permute-start(f32[3,2,72,128]{3,2,1,0:T(8,128)S(1)} %get-tuple-element.127), channel_id=1, source_target_pairs={{8,0},{16,8},{24,16},{32,24},{40,32},{48,40},{56,48},{64,56},{72,6... | collective-permute-start | bytes 663560 | tf_op jit(solution)/shard_map/ppermute | solution.py:964
  91.2 19.3 %copy-start.1 = (s32[1,128]{1,0:T(1,128)S(1)}, s32[1,128]{1,0:T(1,128)}, u32[]{:S(2)}) copy-start(s32[1,128]{1,0:T(1,128)} %slot.3) | copy-start | bytes 1540
  91.2 19.3 %copy-start.2 = (s32[8,128]{1,0:T(8,128)S(1)}, s32[8,128]{1,0:T(8,128)}, u32[]{:S(2)}) copy-start(s32[8,128]{1,0:T(8,128)} %corner.1) | copy-start | bytes 12292
  100.1 2.4 %collective-permute-start.16 = (f32[3,8,128]{2,1,0:T(8,128)S(1)}, f32[3,8,128]{2,1,0:T(8,128)S(1)}, u32[]{:S(2)}, u32[]{:S(2)}) collective-permute-start(f32[3,8,128]{2,1,0:T(8,128)S(1)} %get-tuple-element.133), channel_id=1, source_target_pairs={{0,1},{1,2},{2,3},{3,4},{4,5},{5,6},{6,7},{7,0},{8,9},{9,10},{10,1... | collective-permute-start | bytes 36872 | tf_op jit(solution)/shard_map/ppermute | solution.py:965
  101.6 3.1 %collective-permute-start.17 = (f32[3,8,128]{2,1,0:T(8,128)S(1)}, f32[3,8,128]{2,1,0:T(8,128)S(1)}, u32[]{:S(2)}, u32[]{:S(2)}) collective-permute-start(f32[3,8,128]{2,1,0:T(8,128)S(1)} %get-tuple-element.134), channel_id=1, source_target_pairs={{1,0},{2,1},{3,2},{4,3},{5,4},{6,5},{7,6},{0,7},{9,8},{10,9},{11,1... | collective-permute-start | bytes 36872 | tf_op jit(solution)/shard_map/ppermute | solution.py:964
  105.0 10.0 %collective-permute-start.18 = (f32[200,128]{1,0:T(8,128)S(1)}, f32[200,128]{1,0:T(8,128)S(1)}, u32[]{:S(2)}, u32[]{:S(2)}) collective-permute-start(f32[200,128]{1,0:T(8,128)S(1)} %get-tuple-element.136), channel_id=1, source_target_pairs={{0,8},{8,16},{16,24},{24,32},{32,40},{40,48},{48,56},{56,64},{64,7... | collective-permute-start | bytes 307208 | tf_op jit(solution)/shard_map/ppermute | solution.py:965
  105.1 9.9 %collective-permute-start.19 = (f32[200,128]{1,0:T(8,128)S(1)}, f32[200,128]{1,0:T(8,128)S(1)}, u32[]{:S(2)}, u32[]{:S(2)}) collective-permute-start(f32[200,128]{1,0:T(8,128)S(1)} %get-tuple-element.137), channel_id=1, source_target_pairs={{8,0},{16,8},{24,16},{32,24},{40,32},{48,40},{56,48},{64,56},{72,6... | collective-permute-start | bytes 307208 | tf_op jit(solution)/shard_map/ppermute | solution.py:964
  125.0 22.0 %all-to-all-start.1 = ((f32[128,1,1280]{2,1,0:T(1,128)}), f32[128,1,1280]{2,1,0:T(1,128)S(1)}, u32[]{:S(2)}, u32[]{:S(2)}) async-start(f32[128,1,1280]{2,1,0:T(1,128)} %bitcast.5), calls=%async_computation.1 | async-start | bytes 1310720 | tf_op jit(solution)/shard_map/all_to_all | solution.py:1135
